TPU v7x, 512 devices: a whole 4x8x8 slice. The times are simulated.
512 devices in a mesh: blk: 16 (over y_lo, x), rhs: 32 (over z, y_hi, core).
Axes of the slice: x: 4, y: 8 (y_hi: 2, y_lo: 4; y = y_hi * 4 + y_lo), z: 8, core: 2. Of those that a mesh axis runs over, the one named last changes fastest.
Arguments:
- factor: bfloat16 [2, 16, 2048, 8192], P(None, 'blk', 'rhs'), as said below
- loads: float32 [2, 16, 2048, 128], P(None, 'blk', 'rhs'), may hold values from -6 to 6
Outputs:
- advanced: float32 [2, 16, 2048, 128], P(None, 'blk', 'rhs')
Inputs may be any that keep to these rules, and one draw needn't show every extreme that they name: factor is block lower triangular: F_gk is zero for k > g, and each diagonal block F_kk is lower triangular with diagonal entries of 0.5 to 1.5.
All inputs are finite; a program needn't handle non-finite values.
Results may differ from a plain program's by a relative error of at most 0.002.
Values may be sent and summed in bfloat16 or wider, within the bound.
No kernel may reach another device: no remote copies, remote signals or barrier semaphores. Data moves between devices by JAX's collectives and lax.ppermute only.
A program may use at most 64 MiB of HBM per device.

v0:
```python
import jax
import jax.numpy as jnp
from jax import lax
from jax.sharding import PartitionSpec as P


def spread(value, axis, root):
    mine = lax.axis_index(axis) == root
    return lax.psum(jnp.where(mine, value, jnp.zeros_like(value)), axis)


def body(factor, loads):
    cycle_size = lax.axis_size("blk")
    position = lax.axis_index("blk")
    stored = factor[:, 0]
    work = loads[:, 0]
    rounds = stored.shape[0]
    share = stored.shape[1]
    width = stored.shape[2]
    block = share * lax.axis_size("rhs")
    steps = width // block
    cases = work.shape[2]
    for step in range(steps):
        owner = step % cycle_size
        round_index = step // cycle_size
        diagonal = stored[round_index]

        def add_solve(total, piece, start, diagonal=diagonal, step=step):
            columns = lax.dynamic_slice_in_dim(diagonal, step * block, piece.shape[0], 1).astype(
                jnp.float32
            )
            return jnp.dot(columns, piece, precision=lax.Precision.HIGHEST)

        solution = add_solve(
            jnp.zeros((share, cases), jnp.float32),
            lax.all_gather(work[round_index], "rhs", axis=0, tiled=True),
            jnp.int32(0),
        )
        sent_part = solution.astype(jnp.bfloat16)
        panel = stored[:, :, step * block : (step + 1) * block].reshape(rounds * share, block)
        whole = lax.all_gather(sent_part, "rhs", axis=0, tiled=True)
        whole = spread(whole, "blk", owner)
        update = jnp.dot(panel, whole, preferred_element_type=jnp.float32)
        lowered = work - update.reshape(work.shape)
        work = jnp.where(position == owner, lowered.at[round_index].set(solution), lowered)
    return work[:, None]


def solution(mesh):
    return jax.shard_map(
        body,
        mesh=mesh,
        in_specs=(P(None, "blk", "rhs", None), P(None, "blk", "rhs", None)),
        out_specs=P(None, "blk", "rhs", None),
        check_vma=False,
    )
```

profile of v0, /device:TPU:1, one launch (start us, length us, event | category | flops | bytes accessed | tf_op | source)
XLA Modules:
  0.0 1236.8 jit_solution(11613964825453928507)
XLA Ops:
  6.5 1.4 slice.115
  7.9 0.0 all-gather.9.cloned.1.call-update
  7.9 0.0 all-reduce.5.cloned.1.call-start
  8.0 1.3 slice_bitcast_fusion
  9.3 0.0 copy-start
  9.3 93.0 %all-gather.9.cloned.1.call-done = f32[1,1,2048,128]{3,2,1,0:T(8,128)} async-done(((f32[1,1,64,128]{3,2,1,0:T(8,128)}), f32[1,1,2048,128]{3,2,1,0:T(8,128)}) %all-gather.9.cloned.1.call-update) | async-done | bytes 1048592 | tf_op jit(solution)/shard_map/all_gather | solution.py:36
  102.3 1.7 fusion.15
  104.1 50.5 %all_gather.25 = bf16[2048,128]{1,0:T(8,128)(2,1)S(1)} all-gather(bf16[64,128]{1,0:T(8,128)(2,1)S(1)} %get-tuple-element.63), channel_id=1, replica_groups=mesh['blk'=16,'rhs'=32] {'rhs'}, dimensions={0}, use_global_device_ids=true | all-gather | bytes 540672 | tf_op jit(solution)/shard_map/all_gather | solution.py:41
  154.5 0.8 broadcast_select_fusion.3
  155.4 0.0 all-reduce.5.cloned.1.call-update
  155.4 0.0 all-gather.11.cloned.1.call-start
  155.5 1.4 fusion.14
  156.8 153.0 %all-reduce.5.cloned.1.call-done = bf16[2048,128]{1,0:T(8,128)(2,1)} async-done(((bf16[2048,128]{1,0:T(8,128)(2,1)}), bf16[2048,128]{1,0:T(8,128)(2,1)}) %all-reduce.5.cloned.1.call-update) | async-done | bytes 524304 | tf_op jit(solution)/shard_map/psum | solution.py:9
  309.8 1.5 fusion.16
  311.3 0.6 constant_dynamic-update-slice_fusion.2
  312.0 0.0 all-gather.11.cloned.1.call-update
  312.0 0.0 all-reduce.7.cloned.1.call-start
  312.0 96.5 %all-gather.11.cloned.1.call-done = f32[1,2048,128]{2,1,0:T(8,128)} async-done(((f32[1,64,128]{2,1,0:T(8,128)}), f32[1,2048,128]{2,1,0:T(8,128)}) %all-gather.11.cloned.1.call-update) | async-done | bytes 1048592 | tf_op jit(solution)/shard_map/all_gather | solution.py:36
  408.6 1.7 bitcast_convert_fusion.2
  410.3 50.5 %all_gather.27 = bf16[2048,128]{1,0:T(8,128)(2,1)S(1)} all-gather(bf16[64,128]{1,0:T(8,128)(2,1)S(1)} %get-tuple-element.65), channel_id=1, replica_groups=mesh['blk'=16,'rhs'=32] {'rhs'}, dimensions={0}, use_global_device_ids=true | all-gather | bytes 540672 | tf_op jit(solution)/shard_map/all_gather | solution.py:41
  460.8 0.8 broadcast_select_fusion.2
  461.6 0.0 all-reduce.7.cloned.1.call-update
  461.7 0.0 all-gather.13.cloned.1.call-start
  461.7 154.4 %all-reduce.7.cloned.1.call-done = bf16[2048,128]{1,0:T(8,128)(2,1)} async-done(((bf16[2048,128]{1,0:T(8,128)(2,1)}), bf16[2048,128]{1,0:T(8,128)(2,1)}) %all-reduce.7.cloned.1.call-update) | async-done | bytes 524304 | tf_op jit(solution)/shard_map/psum | solution.py:9
  616.1 1.3 fusion.17
  617.5 0.6 constant_dynamic-update-slice_fusion.1
  618.1 0.0 all-gather.13.cloned.1.call-update
  618.1 0.0 all-reduce.9.cloned.1.call-start
  618.2 96.0 %all-gather.13.cloned.1.call-done = f32[1,2048,128]{2,1,0:T(8,128)} async-done(((f32[1,64,128]{2,1,0:T(8,128)}), f32[1,2048,128]{2,1,0:T(8,128)}) %all-gather.13.cloned.1.call-update) | async-done | bytes 1048592 | tf_op jit(solution)/shard_map/all_gather | solution.py:36
  714.2 1.7 bitcast_convert_fusion.1
  715.9 50.5 %all_gather.29 = bf16[2048,128]{1,0:T(8,128)(2,1)S(1)} all-gather(bf16[64,128]{1,0:T(8,128)(2,1)S(1)} %get-tuple-element.67), channel_id=1, replica_groups=mesh['blk'=16,'rhs'=32] {'rhs'}, dimensions={0}, use_global_device_ids=true | all-gather | bytes 540672 | tf_op jit(solution)/shard_map/all_gather | solution.py:41
  766.4 0.8 broadcast_select_fusion.1
  767.2 0.0 all-reduce.9.cloned.1.call-update
  767.2 0.0 all-gather.15.cloned.1.call-start
  767.3 154.4 %all-reduce.9.cloned.1.call-done = bf16[2048,128]{1,0:T(8,128)(2,1)} async-done(((bf16[2048,128]{1,0:T(8,128)(2,1)}), bf16[2048,128]{1,0:T(8,128)(2,1)}) %all-reduce.9.cloned.1.call-update) | async-done | bytes 524304 | tf_op jit(solution)/shard_map/psum | solution.py:9
  921.7 1.3 fusion.18
  923.0 0.6 constant_dynamic-update-slice_fusion
  923.7 0.0 all-gather.15.cloned.1.call-update
  923.7 0.0 all-reduce.11.cloned.1.call-start
  923.7 96.7 %all-gather.15.cloned.1.call-done = f32[1,2048,128]{2,1,0:T(8,128)} async-done(((f32[1,64,128]{2,1,0:T(8,128)}), f32[1,2048,128]{2,1,0:T(8,128)}) %all-gather.15.cloned.1.call-update) | async-done | bytes 1048592 | tf_op jit(solution)/shard_map/all_gather | solution.py:36
  1020.4 1.7 bitcast_convert_fusion
  1022.2 50.5 %all_gather.31 = bf16[2048,128]{1,0:T(8,128)(2,1)S(1)} all-gather(bf16[64,128]{1,0:T(8,128)(2,1)S(1)} %get-tuple-element.69), channel_id=1, replica_groups=mesh['blk'=16,'rhs'=32] {'rhs'}, dimensions={0}, use_global_device_ids=true | all-gather | bytes 540672 | tf_op jit(solution)/shard_map/all_gather | solution.py:41
  1072.6 0.8 broadcast_select_fusion
  1073.5 0.0 all-reduce.11.cloned.1.call-update
  1073.5 154.4 %all-reduce.11.cloned.1.call-done = bf16[2048,128]{1,0:T(8,128)(2,1)} async-done(((bf16[2048,128]{1,0:T(8,128)(2,1)}), bf16[2048,128]{1,0:T(8,128)(2,1)}) %all-reduce.11.cloned.1.call-update) | async-done | bytes 524304 | tf_op jit(solution)/shard_map/psum | solution.py:9
  1227.9 1.3 fusion.19
  1229.3 0.0 copy-start.5
  1229.3 0.6 copy-done.5
  (16 shorter events, 0.1 us)
Async XLA Ops:
  6.5 95.8 %all-gather.9.cloned.1.call-start = ((), (), s32[]{:S(2)}) async-start(), calls=%async_computation.4 | async-start | bytes 1081344 | tf_op jit(solution)/shard_map/all_gather | solution.py:36
  7.9 301.9 %all-reduce.5.cloned.1.call-start = ((), (), s32[]{:S(2)}) async-start(), calls=%async_computation | async-start | bytes 1048576 | tf_op jit(solution)/shard_map/psum | solution.py:9
  9.3 146.1 %copy-start = (bf16[2,1,64,8192]{3,2,1,0:T(8,128)(2,1)S(1)}, bf16[2,1,64,8192]{3,2,1,0:T(8,128)(2,1)}, u32[]{:S(2)}) copy-start(bf16[2,1,64,8192]{3,2,1,0:T(8,128)(2,1)} %param.10) | copy-start | bytes 6291460
  155.4 253.2 %all-gather.11.cloned.1.call-start = ((), (), s32[]{:S(2)}) async-start(), calls=%async_computation.5 | async-start | bytes 1081344 | tf_op jit(solution)/shard_map/all_gather | solution.py:36
  155.4 155.9 %copy-start.4 = (f32[2,1,64,128]{3,2,1,0:T(8,128)S(1)}, f32[2,1,64,128]{3,2,1,0:T(8,128)}, u32[]{:S(2)}) copy-start(f32[2,1,64,128]{3,2,1,0:T(8,128)} %param.11) | copy-start | bytes 196612
  311.3 304.8 %copy-start.3 = (bf16[2,64,2048]{2,1,0:T(8,128)(2,1)S(1)}, bf16[2,64,2048]{2,1,0:T(8,128)(2,1)}, u32[]{:S(2)}) copy-start(bf16[2,64,2048]{2,1,0:T(8,128)(2,1)} %get-tuple-element.61) | copy-start | bytes 1572868
  312.0 304.1 %all-reduce.7.cloned.1.call-start = ((), (), s32[]{:S(2)}) async-start(), calls=%async_computation.1 | async-start | bytes 1048576 | tf_op jit(solution)/shard_map/psum | solution.py:9
  461.7 252.5 %all-gather.13.cloned.1.call-start = ((), (), s32[]{:S(2)}) async-start(), calls=%async_computation.6 | async-start | bytes 1081344 | tf_op jit(solution)/shard_map/all_gather | solution.py:36
  617.4 304.2 %copy-start.2 = (bf16[2,64,2048]{2,1,0:T(8,128)(2,1)S(1)}, bf16[2,64,2048]{2,1,0:T(8,128)(2,1)}, u32[]{:S(2)}) copy-start(bf16[2,64,2048]{2,1,0:T(8,128)(2,1)} %get-tuple-element.60) | copy-start | bytes 1572868
  618.1 303.6 %all-reduce.9.cloned.1.call-start = ((), (), s32[]{:S(2)}) async-start(), calls=%async_computation.2 | async-start | bytes 1048576 | tf_op jit(solution)/shard_map/psum | solution.py:9
  767.2 253.2 %all-gather.15.cloned.1.call-start = ((), (), s32[]{:S(2)}) async-start(), calls=%async_computation.7 | async-start | bytes 1081344 | tf_op jit(solution)/shard_map/all_gather | solution.py:36
  923.0 304.9 %copy-start.1 = (bf16[2,64,2048]{2,1,0:T(8,128)(2,1)S(1)}, bf16[2,64,2048]{2,1,0:T(8,128)(2,1)}, u32[]{:S(2)}) copy-start(bf16[2,64,2048]{2,1,0:T(8,128)(2,1)} %get-tuple-element.59) | copy-start | bytes 1572868
  923.7 304.2 %all-reduce.11.cloned.1.call-start = ((), (), s32[]{:S(2)}) async-start(), calls=%async_computation.3 | async-start | bytes 1048576 | tf_op jit(solution)/shard_map/psum | solution.py:9
  1229.3 0.6 copy-start.5
Sparse Core Ops, SparseCore 0:
  10.7 91.5 all-gather.8
  155.5 154.2 all-reduce.4
  313.7 94.8 all-gather.10
  461.8 154.2 all-reduce.6
  619.3 94.8 all-gather.12
  767.4 154.2 all-reduce.8
  925.6 94.8 all-gather.14
  1073.6 154.2 all-reduce.10
where the time goes:
time: 1250 us; the launch traced here: 1240 us
  waiting for transfers between devices  999 us (80%)
  blocking collectives  202 us (16%)
  between operations  13.7 us (1%)
    psum x4, waiting for transfers between devices, spread(): return lax.psum(jnp.where(mine, value, jnp.zeros_like(value)), axis)  616 us
    all_gather x4, waiting for transfers between devices, body(): lax.all_gather(work[round_index], 'rhs', axis=0, tiled=True)  382 us
    all_gather x4, blocking collectives, body(): whole = lax.all_gather(sent_part, 'rhs', axis=0, tiled=True)  202 us
  transfers between devices with their start and end apart: 8, of which 8 were waited for; matrix products, arithmetic and copies ran while one was open for 0% of the time, Pallas kernels for 0%

commit v1 on v0

v1 whole, which is shorter than its diff:
```python
import jax
import jax.numpy as jnp
from jax import lax
from jax.sharding import Mesh, PartitionSpec as P

BLK = ("yl", "x")
RHS = ("z", "yh", "c")


def gather_rows(part):
    chips = lax.axis_size(("z", "yh"))
    sent = jnp.broadcast_to(part[None], (chips,) + part.shape)
    got = lax.all_to_all(sent, ("z", "yh"), 0, 0, tiled=True)
    both = lax.all_gather(got, "c", axis=1, tiled=True)
    return both.reshape(-1, part.shape[1])


def from_owner(part, owner):
    count = lax.axis_size(BLK)
    sent = jnp.broadcast_to(part[None], (count,) + part.shape)
    return lax.all_to_all(sent, BLK, 0, 0, tiled=True)[owner]


def body(factor, loads):
    position = lax.axis_index(BLK)
    stored = factor[:, 0]
    work = loads[:, 0]
    rounds, share, width = stored.shape
    block = share * lax.axis_size(RHS)
    cycle = lax.axis_size(BLK)
    for step in range(width // block):
        owner = step % cycle
        index = step // cycle
        columns = slice(step * block, (step + 1) * block)
        diagonal = stored[index, :, columns].astype(jnp.float32)
        whole_work = gather_rows(work[index])
        solution = jnp.dot(diagonal, whole_work, precision=lax.Precision.HIGHEST)
        sent = from_owner(solution.astype(jnp.bfloat16), owner)
        whole = gather_rows(sent)
        panel = stored[:, :, columns].reshape(rounds * share, block)
        update = jnp.dot(panel, whole, preferred_element_type=jnp.float32)
        lowered = work - update.reshape(work.shape)
        work = jnp.where(position == owner, lowered.at[index].set(solution), lowered)
    return work[:, None]


def solution(mesh):
    fine = Mesh(mesh.devices.reshape(4, 4, 8, 2, 2), BLK + RHS)
    spec = P(None, BLK, RHS, None)
    return jax.shard_map(
        body, mesh=fine, in_specs=(spec, spec), out_specs=spec, check_vma=False
    )
```

time: 1250 us -> 365 us (0.29)
  waiting for transfers between devices: 999 us -> 136 us
  blocking collectives: 202 us -> 153 us
  starting transfers between devices: 0.3 us -> 43.6 us
    psum x4 -> x0, waiting for transfers between devices: 616 us -> none  [spread(): return lax.psum(jnp.where(mine, value, jnp.zeros_like(value)), axis)]
    all_gather x4, waiting for transfers between devices: 382 us -> 76.5 us  [gather_rows(): both = lax.all_gather(got, 'c', axis=1, tiled=True)]
    all_gather x4, blocking collectives: 202 us -> 18.9 us  [gather_rows(): both = lax.all_gather(got, 'c', axis=1, tiled=True)]
    all_to_all x0 -> x7, blocking collectives: none -> 134 us  [the longest x4 86.4 us: gather_rows(): got = lax.all_to_all(sent, ('z', 'yh'), 0, 0, tiled=True)]
    all_to_all x0 -> x5, waiting for transfers between devices: none -> 59.3 us  [the longest x4 49.2 us: gather_rows(): got = lax.all_to_all(sent, ('z', 'yh'), 0, 0, tiled=True)]
    all_to_all x0 -> x5, starting transfers between devices: none -> 43.5 us  [the longest x4 37.6 us: gather_rows(): got = lax.all_to_all(sent, ('z', 'yh'), 0, 0, tiled=True)]
  transfers between devices with their start and end apart: 8 -> 9, of which waited for: 8 -> 9; matrix products, arithmetic and copies ran while one was open for 0% -> 0% of each run, Pallas kernels for 0% -> 0%
where the time goes in v1:
time: 365 us; the launch traced here: 364 us
  blocking collectives  153 us (42%)
  waiting for transfers between devices  136 us (37%)
  starting transfers between devices  43.6 us (12%)
  between operations  13.4 us (4%)
  matrix products  11.3 us (3%)
  local copies, waits for them, and re-layouts  6.81 us (2%)
    all_to_all x4, blocking collectives, gather_rows(): got = lax.all_to_all(sent, ('z', 'yh'), 0, 0, tiled=True)  86.4 us
    all_gather x4, waiting for transfers between devices, gather_rows(): both = lax.all_gather(got, 'c', axis=1, tiled=True)  76.5 us
    all_to_all x4, waiting for transfers between devices, gather_rows(): got = lax.all_to_all(sent, ('z', 'yh'), 0, 0, tiled=True)  49.2 us
    all_to_all x3, blocking collectives, from_owner(): return lax.all_to_all(sent, BLK, 0, 0, tiled=True)[owner]  47.3 us
    all_to_all x4, starting transfers between devices, gather_rows(): got = lax.all_to_all(sent, ('z', 'yh'), 0, 0, tiled=True)  37.6 us
    all_gather x4, blocking collectives, gather_rows(): both = lax.all_gather(got, 'c', axis=1, tiled=True)  18.9 us
    all_to_all x1, waiting for transfers between devices, from_owner(): return lax.all_to_all(sent, BLK, 0, 0, tiled=True)[owner]  10.1 us
    dot_general x4, matrix products, body(): solution = jnp.dot(diagonal, whole_work, precision=lax.Precision.HIGHEST)  8.1 us
  transfers between devices with their start and end apart: 9, of which 9 were waited for; matrix products, arithmetic and copies ran while one was open for 0% of the time, Pallas kernels for 0%

profile of v1, /device:TPU:1, one launch (start us, length us, event | category | flops | bytes accessed | tf_op | source)
XLA Modules:
  0.0 363.6 jit_solution(8481680979805789303)
XLA Ops:
  6.5 0.9 slice_bitcast_fusion.8
  7.5 30.6 %all_to_all.60 = f32[16,64,128]{2,1,0:T(8,128)} all-to-all(f32[16,64,128]{2,1,0:T(8,128)S(1)} %broadcast_in_dim.86), channel_id=1, replica_groups=mesh['yl'=4,'x'=4,'z'=8,'yh'=2,'c'=2] {'z','yh'}, dimensions={0} | all-to-all | bytes 1048576 | tf_op jit(solution)/shard_map/all_to_all | solution.py:13
  38.1 0.0 all-gather.5.cloned.1.call-update
  38.1 19.7 %all-gather.5.cloned.1.call-done = f32[16,128,128]{2,1,0:T(8,128)} async-done(((f32[16,64,128]{2,1,0:T(8,128)}), f32[16,128,128]{2,1,0:T(8,128)}) %all-gather.5.cloned.1.call-update) | async-done | bytes 1048592 | tf_op jit(solution)/shard_map/all_gather | solution.py:14
  57.8 2.3 fusion.13
  60.2 0.7 broadcast_in_dim.87
  60.9 5.8 %all-to-all-start.1 = ((bf16[16,64,128]{2,1,0:T(8,128)(2,1)}), bf16[16,64,128]{2,1,0:T(8,128)(2,1)S(1)}, u32[]{:S(2)}, u32[]{:S(2)}) async-start(bf16[16,64,128]{2,1,0:T(8,128)(2,1)} %broadcast_in_dim.87), calls=%async_computation.1 | async-start | bytes 524288 | tf_op jit(solution)/shard_map/all_to_all | solution.py:21
  66.8 10.1 %all-to-all-done.1 = bf16[16,64,128]{2,1,0:T(8,128)(2,1)S(1)} async-done(((bf16[16,64,128]{2,1,0:T(8,128)(2,1)}), bf16[16,64,128]{2,1,0:T(8,128)(2,1)S(1)}, u32[]{:S(2)}, u32[]{:S(2)}) %all-to-all-start.1) | async-done | bytes 262176 | tf_op jit(solution)/shard_map/all_to_all | solution.py:21
  76.9 0.8 broadcast_in_dim.89
  77.6 9.4 %all-to-all-start.2 = ((bf16[16,64,128]{2,1,0:T(8,128)(2,1)}), bf16[16,64,128]{2,1,0:T(8,128)(2,1)S(1)}, u32[]{:S(2)}, u32[]{:S(2)}) async-start(bf16[16,64,128]{2,1,0:T(8,128)(2,1)} %broadcast_in_dim.89), calls=%async_computation.2 | async-start | bytes 524288 | tf_op jit(solution)/shard_map/all_to_all | solution.py:13
  87.0 0.0 all-gather.7.cloned.1.call-start
  87.1 1.2 fusion.12
  88.3 11.4 %all-to-all-done.2 = bf16[16,64,128]{2,1,0:T(8,128)(2,1)S(1)} async-done(((bf16[16,64,128]{2,1,0:T(8,128)(2,1)}), bf16[16,64,128]{2,1,0:T(8,128)(2,1)S(1)}, u32[]{:S(2)}, u32[]{:S(2)}) %all-to-all-start.2) | async-done | bytes 262176 | tf_op jit(solution)/shard_map/all_to_all | solution.py:13
  99.7 4.8 %all_gather.25 = bf16[16,128,128]{2,1,0:T(8,128)(2,1)S(1)} all-gather(bf16[16,64,128]{2,1,0:T(8,128)(2,1)S(1)} %all-to-all-done.2), channel_id=1, replica_groups=mesh['yl'=4,'x'=4,'z'=8,'yh'=2,'c'=2] {'c'}, dimensions={1}, use_global_device_ids=true | all-gather | bytes 786432 | tf_op jit(solution)/shard_map/all_gather | solution.py:14
  104.5 1.3 fusion.14
  105.9 18.6 %all_to_all.61 = f32[16,64,128]{2,1,0:T(8,128)} all-to-all(f32[16,64,128]{2,1,0:T(8,128)S(1)} %broadcast_in_dim.91), channel_id=1, replica_groups=mesh['yl'=4,'x'=4,'z'=8,'yh'=2,'c'=2] {'z','yh'}, dimensions={0} | all-to-all | bytes 1048576 | tf_op jit(solution)/shard_map/all_to_all | solution.py:13
  124.5 0.0 all-gather.7.cloned.1.call-update
  124.5 19.0 %all-gather.7.cloned.1.call-done = f32[16,128,128]{2,1,0:T(8,128)} async-done(((f32[16,64,128]{2,1,0:T(8,128)}), f32[16,128,128]{2,1,0:T(8,128)}) %all-gather.7.cloned.1.call-update) | async-done | bytes 1048592 | tf_op jit(solution)/shard_map/all_gather | solution.py:14
  143.5 2.3 bitcast_convert_fusion.2
  145.9 15.8 %all_to_all.62 = bf16[16,64,128]{2,1,0:T(8,128)(2,1)S(1)} all-to-all(bf16[16,64,128]{2,1,0:T(8,128)(2,1)S(1)} %broadcast_in_dim.92), channel_id=1, replica_groups=mesh['yl'=4,'x'=4,'z'=8,'yh'=2,'c'=2] {'yl','x'}, dimensions={0} | all-to-all | bytes 524288 | tf_op jit(solution)/shard_map/all_to_all | solution.py:21
  161.6 0.7 broadcast_in_dim.94
  162.4 9.4 %all-to-all-start.5 = ((bf16[16,64,128]{2,1,0:T(8,128)(2,1)}), bf16[16,64,128]{2,1,0:T(8,128)(2,1)S(1)}, u32[]{:S(2)}, u32[]{:S(2)}) async-start(bf16[16,64,128]{2,1,0:T(8,128)(2,1)} %broadcast_in_dim.94), calls=%async_computation.5 | async-start | bytes 524288 | tf_op jit(solution)/shard_map/all_to_all | solution.py:13
  171.8 0.0 all-gather.9.cloned.1.call-start
  171.8 12.6 %all-to-all-done.5 = bf16[16,64,128]{2,1,0:T(8,128)(2,1)S(1)} async-done(((bf16[16,64,128]{2,1,0:T(8,128)(2,1)}), bf16[16,64,128]{2,1,0:T(8,128)(2,1)S(1)}, u32[]{:S(2)}, u32[]{:S(2)}) %all-to-all-start.5) | async-done | bytes 262176 | tf_op jit(solution)/shard_map/all_to_all | solution.py:13
  184.4 4.8 %all_gather.27 = bf16[16,128,128]{2,1,0:T(8,128)(2,1)S(1)} all-gather(bf16[16,64,128]{2,1,0:T(8,128)(2,1)S(1)} %all-to-all-done.5), channel_id=1, replica_groups=mesh['yl'=4,'x'=4,'z'=8,'yh'=2,'c'=2] {'c'}, dimensions={1}, use_global_device_ids=true | all-gather | bytes 786432 | tf_op jit(solution)/shard_map/all_gather | solution.py:14
  189.2 1.3 fusion.15
  190.7 18.6 %all_to_all.63 = f32[16,64,128]{2,1,0:T(8,128)} all-to-all(f32[16,64,128]{2,1,0:T(8,128)S(1)} %broadcast_in_dim.96), channel_id=1, replica_groups=mesh['yl'=4,'x'=4,'z'=8,'yh'=2,'c'=2] {'z','yh'}, dimensions={0} | all-to-all | bytes 1048576 | tf_op jit(solution)/shard_map/all_to_all | solution.py:13
  209.3 0.0 all-gather.9.cloned.1.call-update
  209.3 18.9 %all-gather.9.cloned.1.call-done = f32[16,128,128]{2,1,0:T(8,128)} async-done(((f32[16,64,128]{2,1,0:T(8,128)}), f32[16,128,128]{2,1,0:T(8,128)}) %all-gather.9.cloned.1.call-update) | async-done | bytes 1048592 | tf_op jit(solution)/shard_map/all_gather | solution.py:14
  228.2 1.7 bitcast_convert_fusion.1
  230.0 15.8 %all_to_all.64 = bf16[16,64,128]{2,1,0:T(8,128)(2,1)S(1)} all-to-all(bf16[16,64,128]{2,1,0:T(8,128)(2,1)S(1)} %broadcast_in_dim.97), channel_id=1, replica_groups=mesh['yl'=4,'x'=4,'z'=8,'yh'=2,'c'=2] {'yl','x'}, dimensions={0} | all-to-all | bytes 524288 | tf_op jit(solution)/shard_map/all_to_all | solution.py:21
  245.7 0.7 broadcast_in_dim.99
  246.5 9.4 %all-to-all-start.8 = ((bf16[16,64,128]{2,1,0:T(8,128)(2,1)}), bf16[16,64,128]{2,1,0:T(8,128)(2,1)S(1)}, u32[]{:S(2)}, u32[]{:S(2)}) async-start(bf16[16,64,128]{2,1,0:T(8,128)(2,1)} %broadcast_in_dim.99), calls=%async_computation.8 | async-start | bytes 524288 | tf_op jit(solution)/shard_map/all_to_all | solution.py:13
  255.9 0.0 all-gather.11.cloned.1.call-start
  256.0 12.6 %all-to-all-done.8 = bf16[16,64,128]{2,1,0:T(8,128)(2,1)S(1)} async-done(((bf16[16,64,128]{2,1,0:T(8,128)(2,1)}), bf16[16,64,128]{2,1,0:T(8,128)(2,1)S(1)}, u32[]{:S(2)}, u32[]{:S(2)}) %all-to-all-start.8) | async-done | bytes 262176 | tf_op jit(solution)/shard_map/all_to_all | solution.py:13
  268.5 4.7 %all_gather.29 = bf16[16,128,128]{2,1,0:T(8,128)(2,1)S(1)} all-gather(bf16[16,64,128]{2,1,0:T(8,128)(2,1)S(1)} %all-to-all-done.8), channel_id=1, replica_groups=mesh['yl'=4,'x'=4,'z'=8,'yh'=2,'c'=2] {'c'}, dimensions={1}, use_global_device_ids=true | all-gather | bytes 786432 | tf_op jit(solution)/shard_map/all_gather | solution.py:14
  273.2 0.3 fusion.16
  273.6 18.6 %all_to_all.65 = f32[16,64,128]{2,1,0:T(8,128)} all-to-all(f32[16,64,128]{2,1,0:T(8,128)S(1)} %broadcast_in_dim.101), channel_id=1, replica_groups=mesh['yl'=4,'x'=4,'z'=8,'yh'=2,'c'=2] {'z','yh'}, dimensions={0} | all-to-all | bytes 1048576 | tf_op jit(solution)/shard_map/all_to_all | solution.py:13
  292.2 0.0 all-gather.11.cloned.1.call-update
  292.2 18.9 %all-gather.11.cloned.1.call-done = f32[16,128,128]{2,1,0:T(8,128)} async-done(((f32[16,64,128]{2,1,0:T(8,128)}), f32[16,128,128]{2,1,0:T(8,128)}) %all-gather.11.cloned.1.call-update) | async-done | bytes 1048592 | tf_op jit(solution)/shard_map/all_gather | solution.py:14
  311.2 1.7 bitcast_convert_fusion
  312.9 15.8 %all_to_all.66 = bf16[16,64,128]{2,1,0:T(8,128)(2,1)S(1)} all-to-all(bf16[16,64,128]{2,1,0:T(8,128)(2,1)S(1)} %broadcast_in_dim.102), channel_id=1, replica_groups=mesh['yl'=4,'x'=4,'z'=8,'yh'=2,'c'=2] {'yl','x'}, dimensions={0} | all-to-all | bytes 524288 | tf_op jit(solution)/shard_map/all_to_all | solution.py:21
  328.7 0.7 broadcast_in_dim.104
  329.4 9.4 %all-to-all-start.11 = ((bf16[16,64,128]{2,1,0:T(8,128)(2,1)}), bf16[16,64,128]{2,1,0:T(8,128)(2,1)S(1)}, u32[]{:S(2)}, u32[]{:S(2)}) async-start(bf16[16,64,128]{2,1,0:T(8,128)(2,1)} %broadcast_in_dim.104), calls=%async_computation.11 | async-start | bytes 524288 | tf_op jit(solution)/shard_map/all_to_all | solution.py:13
  338.8 12.6 %all-to-all-done.11 = bf16[16,64,128]{2,1,0:T(8,128)(2,1)S(1)} async-done(((bf16[16,64,128]{2,1,0:T(8,128)(2,1)}), bf16[16,64,128]{2,1,0:T(8,128)(2,1)S(1)}, u32[]{:S(2)}, u32[]{:S(2)}) %all-to-all-start.11) | async-done | bytes 262176 | tf_op jit(solution)/shard_map/all_to_all | solution.py:13
  351.5 4.7 %all_gather.31 = bf16[16,128,128]{2,1,0:T(8,128)(2,1)S(1)} all-gather(bf16[16,64,128]{2,1,0:T(8,128)(2,1)S(1)} %all-to-all-done.11), channel_id=1, replica_groups=mesh['yl'=4,'x'=4,'z'=8,'yh'=2,'c'=2] {'c'}, dimensions={1}, use_global_device_ids=true | all-gather | bytes 786432 | tf_op jit(solution)/shard_map/all_gather | solution.py:14
  356.1 0.3 fusion.17
  356.5 0.6 copy-done.4
  (30 shorter events, 0.4 us)
Async XLA Ops:
  6.5 51.3 %copy-start = (bf16[2,1,64,8192]{3,2,1,0:T(8,128)(2,1)S(1)}, bf16[2,1,64,8192]{3,2,1,0:T(8,128)(2,1)}, u32[]{:S(2)}) copy-start(bf16[2,1,64,8192]{3,2,1,0:T(8,128)(2,1)} %param.10) | copy-start | bytes 6291460
  6.5 51.3 %all-gather.5.cloned.1.call-start = ((), (), s32[]{:S(2)}) async-start(), calls=%async_computation.12 | async-start | bytes 1572864 | tf_op jit(solution)/shard_map/all_gather | solution.py:14
  60.9 16.0 %all-to-all-start.1 = ((bf16[16,64,128]{2,1,0:T(8,128)(2,1)}), bf16[16,64,128]{2,1,0:T(8,128)(2,1)S(1)}, u32[]{:S(2)}, u32[]{:S(2)}) async-start(bf16[16,64,128]{2,1,0:T(8,128)(2,1)} %broadcast_in_dim.87), calls=%async_computation.1 | async-start | bytes 524288 | tf_op jit(solution)/shard_map/all_to_all | solution.py:21
  77.6 22.1 %all-to-all-start.2 = ((bf16[16,64,128]{2,1,0:T(8,128)(2,1)}), bf16[16,64,128]{2,1,0:T(8,128)(2,1)S(1)}, u32[]{:S(2)}, u32[]{:S(2)}) async-start(bf16[16,64,128]{2,1,0:T(8,128)(2,1)} %broadcast_in_dim.89), calls=%async_computation.2 | async-start | bytes 524288 | tf_op jit(solution)/shard_map/all_to_all | solution.py:13
  87.0 18.8 %copy-start.1 = (f32[2,1,64,128]{3,2,1,0:T(8,128)S(1)}, f32[2,1,64,128]{3,2,1,0:T(8,128)}, u32[]{:S(2)}) copy-start(f32[2,1,64,128]{3,2,1,0:T(8,128)} %param.11) | copy-start | bytes 196612
  87.0 56.4 %all-gather.7.cloned.1.call-start = ((), (), s32[]{:S(2)}) async-start(), calls=%async_computation.13 | async-start | bytes 1572864 | tf_op jit(solution)/shard_map/all_gather | solution.py:14
  99.7 6.2 %copy-start.2 = (f32[64,128]{1,0:T(8,128)S(1)}, f32[64,128]{1,0:T(8,128)}, u32[]{:S(2)}) copy-start(f32[64,128]{1,0:T(8,128)} %get-tuple-element.64) | copy-start | bytes 98308
  162.4 22.1 %all-to-all-start.5 = ((bf16[16,64,128]{2,1,0:T(8,128)(2,1)}), bf16[16,64,128]{2,1,0:T(8,128)(2,1)S(1)}, u32[]{:S(2)}, u32[]{:S(2)}) async-start(bf16[16,64,128]{2,1,0:T(8,128)(2,1)} %broadcast_in_dim.94), calls=%async_computation.5 | async-start | bytes 524288 | tf_op jit(solution)/shard_map/all_to_all | solution.py:13
  171.8 56.4 %all-gather.9.cloned.1.call-start = ((), (), s32[]{:S(2)}) async-start(), calls=%async_computation.14 | async-start | bytes 1572864 | tf_op jit(solution)/shard_map/all_gather | solution.py:14
  184.4 6.2 %copy-start.3 = (f32[128,64]{0,1:T(8,128)S(1)}, f32[128,64]{0,1:T(8,128)}, u32[]{:S(2)}) copy-start(f32[128,64]{0,1:T(8,128)} %get-tuple-element.66) | copy-start | bytes 98308
  246.5 22.1 %all-to-all-start.8 = ((bf16[16,64,128]{2,1,0:T(8,128)(2,1)}), bf16[16,64,128]{2,1,0:T(8,128)(2,1)S(1)}, u32[]{:S(2)}, u32[]{:S(2)}) async-start(bf16[16,64,128]{2,1,0:T(8,128)(2,1)} %broadcast_in_dim.99), calls=%async_computation.8 | async-start | bytes 524288 | tf_op jit(solution)/shard_map/all_to_all | solution.py:13
  255.9 55.3 %all-gather.11.cloned.1.call-start = ((), (), s32[]{:S(2)}) async-start(), calls=%async_computation.15 | async-start | bytes 1572864 | tf_op jit(solution)/shard_map/all_gather | solution.py:14
  329.4 22.1 %all-to-all-start.11 = ((bf16[16,64,128]{2,1,0:T(8,128)(2,1)}), bf16[16,64,128]{2,1,0:T(8,128)(2,1)S(1)}, u32[]{:S(2)}, u32[]{:S(2)}) async-start(bf16[16,64,128]{2,1,0:T(8,128)(2,1)} %broadcast_in_dim.104), calls=%async_computation.11 | async-start | bytes 524288 | tf_op jit(solution)/shard_map/all_to_all | solution.py:13
  356.5 0.6 copy-start.4
Sparse Core Ops, SparseCore 0:
  38.2 19.5 all-gather.4
  124.7 18.7 all-gather.6
  209.4 18.7 all-gather.8
  292.3 18.7 all-gather.10

commit v2 on v1

v2 whole, which is shorter than its diff:
```python
import jax
import jax.numpy as jnp
from jax import lax
from jax.sharding import Mesh, PartitionSpec as P

BLK = ("yl", "x")
RHS = ("z", "yh", "c")
CHIPS = ("z", "yh")


def exchange(parts, axis):
    return lax.all_to_all(parts, axis, 0, 0, tiled=True)


def repeat(part, count):
    return jnp.broadcast_to(part[None], (count,) + part.shape)


def gather_chips(part):
    got = exchange(repeat(part, lax.axis_size(CHIPS)), CHIPS)
    return jnp.swapaxes(got, 0, 1).reshape(part.shape[0], -1)


def times(values, rows):
    return lax.dot_general(
        values, rows, (((1,), (1,)), ((), ())), preferred_element_type=jnp.float32
    )


def times_exact(values, rows):
    first = lax.reduce_precision(values, 8, 7)
    rest = values - first
    second = lax.reduce_precision(rest, 8, 7)
    third = rest - second
    terms = jnp.concatenate([first, second, third], 0).astype(jnp.bfloat16)
    a, b, c = jnp.split(times(terms, rows), 3, 0)
    return (c + b) + a


def body(factor, loads):
    xs, ys = lax.axis_size("x"), lax.axis_size("yl")
    cores = lax.axis_size("c")
    stored, given = factor[:, 0], loads[:, 0]
    share, width = stored.shape[1:]
    cases = given.shape[2]
    block = share * lax.axis_size(RHS)
    steps = width // block
    half = width // 2
    few = cases // (xs * cores)
    pair = cores * share

    start = lax.all_gather(stored[0, :, :block], "c", axis=0, tiled=True)
    left = lax.all_gather(stored[0, :, :half], ("x", "c"), axis=0)
    right = lax.all_gather(stored[0, :, half:], ("x", "c"), axis=0)
    below = lax.all_gather(stored[1], ("x", "c"), axis=0)
    left, right = left.reshape(xs, pair, half), right.reshape(xs, pair, half)

    def panel(row, column):
        source = left if column * block < half else right
        place = (column * block) % half
        return source[row, :, place : place + block]

    together = lax.all_gather(given[0], "c", axis=0, tiled=True).T
    mine = lax.dynamic_index_in_dim(
        together.reshape(xs, cores, few, pair), lax.axis_index("c"), 1, False
    )
    mine = mine.reshape(xs * few, pair)
    first = times_exact(gather_chips(mine), start)
    first = jnp.where(lax.axis_index("x") == 0, first, mine)
    state = list(exchange(first.reshape(xs, few, pair), "x"))

    sent = [state[0].astype(jnp.bfloat16)]
    for step in range(1, steps):
        whole = gather_chips(sent[step - 1])
        for row in range(step, steps):
            state[row] = state[row] - times(whole, panel(row, step - 1))
        state[step] = times_exact(gather_chips(state[step]), panel(step, step))
        sent.append(state[step].astype(jnp.bfloat16))

    shared = exchange(repeat(jnp.stack(sent), ys), "yl")[0]
    got = exchange(repeat(shared, lax.axis_size(CHIPS)), CHIPS)
    whole = got.transpose(2, 1, 0, 3).reshape(few, width)
    upper = times(whole[:, :half], left.reshape(xs * pair, half)) + times(
        whole[:, half:], right.reshape(xs * pair, half)
    )
    lower = times(whole, below.reshape(xs * pair, width))
    upper = jnp.swapaxes(upper.reshape(few, xs, pair), 0, 1)
    lower = jnp.swapaxes(lower.reshape(few, xs, pair), 0, 1)
    solved = lax.axis_index("yl") == 0
    upper = jnp.where(solved, jnp.stack(state), upper)
    both = jnp.stack([upper, lower], 1)[:, None]
    both = jnp.broadcast_to(both, (xs, cores) + both.shape[2:])
    both = both.reshape((xs * cores,) + both.shape[2:])
    back = exchange(both, ("x", "c"))
    back = jnp.swapaxes(back, 0, 1).reshape(2, cases, pair).transpose(0, 2, 1)
    back = lax.dynamic_slice_in_dim(back, lax.axis_index("c") * share, share, 1)
    top = jnp.where(solved, back[0], given[0] - back[0])
    return jnp.stack([top, given[1] - back[1]])[:, None]


def solution(mesh):
    fine = Mesh(mesh.devices.reshape(4, 4, 8, 2, 2), BLK + RHS)
    spec = P(None, BLK, RHS, None)
    return jax.shard_map(
        body, mesh=fine, in_specs=(spec, spec), out_specs=spec, check_vma=False
    )
```

time: 365 us -> 228 us (0.62)
  blocking collectives: 153 us -> 62.4 us
  waiting for transfers between devices: 136 us -> 72.5 us
  matrix products: 11.3 us -> 22.5 us
  local copies, waits for them, and re-layouts: 6.81 us -> 12.2 us
    all_to_all x7 -> x4, blocking collectives: 134 us -> 51.6 us  [exchange(): return lax.all_to_all(parts, axis, 0, 0, tiled=True)]
    all_gather x4 -> x3, waiting for transfers between devices: 76.5 us -> 0.04 us  [the longest x1 0.02 us: body(): right = lax.all_gather(stored[0, :, half:], ('x', 'c'), axis=0)]
    all_to_all x5 -> x7, waiting for transfers between devices: 59.3 us -> 71.7 us  [exchange(): return lax.all_to_all(parts, axis, 0, 0, tiled=True)]
    dot_general x8 -> x13, matrix products: 11.3 us -> 22.5 us  [times(): lax.dot_general(values, rows, (((1,), (1,)), ((), ())), preferred_element...]
    all_gather x4 -> x2, blocking collectives: 18.9 us -> 10.8 us  [the longest x1 8.38 us: body(): together = lax.all_gather(given[0], 'c', axis=0, tiled=True).T]
    slice x1 -> x4, local copies, waits for them, and re-layouts: 1.2 us -> 5.55 us  [the longest x1 2.31 us: body(): left = lax.all_gather(stored[0, :, :half], ('x', 'c'), axis=0)]
    all_to_all x5 -> x7, starting transfers between devices: 43.5 us -> 42.8 us  [exchange(): return lax.all_to_all(parts, axis, 0, 0, tiled=True)]
  transfers between devices with their start and end apart: 9 -> 10, of which waited for: 9 -> 7; matrix products, arithmetic and copies ran while one was open for 0% -> 11% of each run, Pallas kernels for 0% -> 0%
where the time goes in v2:
time: 228 us; the launch traced here: 226 us
  waiting for transfers between devices  72.5 us (32%)
  blocking collectives  62.4 us (27%)
  starting transfers between devices  42.9 us (19%)
  matrix products  22.5 us (10%)
  between operations  13.5 us (6%)
  local copies, waits for them, and re-layouts  12.2 us (5%)
    all_to_all x7, waiting for transfers between devices, exchange(): return lax.all_to_all(parts, axis, 0, 0, tiled=True)  71.7 us
    all_to_all x4, blocking collectives, exchange(): return lax.all_to_all(parts, axis, 0, 0, tiled=True)  51.6 us
    all_to_all x7, starting transfers between devices, exchange(): return lax.all_to_all(parts, axis, 0, 0, tiled=True)  42.8 us
    dot_general x13, matrix products, times(): lax.dot_general(values, rows, (((1,), (1,)), ((), ())), preferred_element...  22.5 us
    all_gather x1, blocking collectives, body(): together = lax.all_gather(given[0], 'c', axis=0, tiled=True).T  8.38 us
  transfers between devices with their start and end apart: 10, of which 7 were waited for; matrix products, arithmetic and copies ran while one was open for 11% of the time, Pallas kernels for 0%

profile of v2, /device:TPU:1, one launch (start us, length us, event | category | flops | bytes accessed | tf_op | source)
XLA Modules:
  0.0 226.3 jit_solution(11706260074547907412)
XLA Ops:
  6.5 2.3 %fusion.57 = (bf16[1,64,4096]{2,1,0:T(8,128)(2,1)}, bf16[1,64,4096]{2,1,0:T(8,128)(2,1)}) fusion(bf16[2,64,8192]{2,1,0:T(8,128)(2,1)} %bitcast.210), kind=kLoop, calls=%fused_computation.113 | loop fusion | bytes 2097152 | tf_op jit(solution)/shard_map/slice | solution.py:53
  8.9 0.7 all-gather.9.cloned.1.call-update
  9.7 2.3 %slice.83 = bf16[1,1,64,8192]{3,2,1,0:T(8,128)(2,1)} slice(bf16[2,1,64,8192]{3,2,1,0:T(8,128)(2,1)} %param.2), slice={[1:2], [0:1], [0:64], [0:8192]} | slice | bytes 2097152 | tf_op jit(solution)/shard_map/slice | solution.py:55
  12.0 8.4 %all-gather = f32[1,1,128,128]{3,1,0,2:T(1,128)S(1)} all-gather(f32[1,1,64,128]{3,1,0,2:T(1,128)S(1)} %bitcast.218), channel_id=2, replica_groups=mesh['yl'=4,'x'=4,'z'=8,'yh'=2,'c'=2] {'c'}, dimensions={2}, use_global_device_ids=true | all-gather | bytes 98304 | tf_op jit(solution)/shard_map/all_gather | solution.py:63
  20.5 0.9 broadcast_in_dim.33
  21.4 10.0 %all-to-all-start = ((f32[16,64,128]{2,1,0:T(8,128)}), f32[16,64,128]{2,1,0:T(8,128)S(1)}, u32[]{:S(2)}, u32[]{:S(2)}) async-start(f32[16,64,128]{2,1,0:T(8,128)} %broadcast_in_dim.33), calls=%async_computation | async-start | bytes 1048576 | tf_op jit(solution)/shard_map/all_to_all | solution.py:12
  31.4 1.0 slice.88
  32.4 2.4 %all-gather.1 = bf16[1,128,2048]{2,1,0:T(8,128)(2,1)S(1)} all-gather(bf16[1,64,2048]{2,1,0:T(8,128)(2,1)S(1)} %slice.88), channel_id=3, replica_groups=mesh['yl'=4,'x'=4,'z'=8,'yh'=2,'c'=2] {'c'}, dimensions={1}, use_global_device_ids=true | all-gather | bytes 786432 | tf_op jit(solution)/shard_map/all_gather | solution.py:52
  34.8 11.5 %all-to-all-done = f32[16,64,128]{2,1,0:T(8,128)S(1)} async-done(((f32[16,64,128]{2,1,0:T(8,128)}), f32[16,64,128]{2,1,0:T(8,128)S(1)}, u32[]{:S(2)}, u32[]{:S(2)}) %all-to-all-start) | async-done | bytes 524320 | tf_op jit(solution)/shard_map/all_to_all | solution.py:12
  46.3 0.1 reduce-precision_convert_fusion.1
  46.5 0.4 fusion.1
  46.9 8.1 %all_to_all.55 = f32[4,16,128]{2,1,0:T(8,128)S(1)} all-to-all(f32[4,16,128]{2,1,0:T(8,128)S(1)} %bitcast.220), channel_id=1, replica_groups=mesh['yl'=4,'x'=4,'z'=8,'yh'=2,'c'=2] {'x'}, dimensions={0} | all-to-all | bytes 65536 | tf_op jit(solution)/shard_map/all_to_all | solution.py:12
  55.0 20.7 %all_to_all.56 = bf16[16,16,128]{2,1,0:T(8,128)(2,1)S(1)} all-to-all(bf16[16,16,128]{2,1,0:T(8,128)(2,1)S(1)} %broadcast_in_dim.35), channel_id=1, replica_groups=mesh['yl'=4,'x'=4,'z'=8,'yh'=2,'c'=2] {'z','yh'}, dimensions={0} | all-to-all | bytes 131072 | tf_op jit(solution)/shard_map/all_to_all | solution.py:12
  75.7 1.3 convolution_subtract_fusion.5
  77.0 14.4 %all_to_all.57 = f32[16,16,128]{2,1,0:T(8,128)S(1)} all-to-all(f32[16,16,128]{2,1,0:T(8,128)S(1)} %broadcast_in_dim.36), channel_id=1, replica_groups=mesh['yl'=4,'x'=4,'z'=8,'yh'=2,'c'=2] {'z','yh'}, dimensions={0} | all-to-all | bytes 262144 | tf_op jit(solution)/shard_map/all_to_all | solution.py:12
  91.5 1.3 fusion.10
  92.8 0.6 broadcast_in_dim.37
  93.5 3.5 %all-to-all-start.4 = ((bf16[16,16,128]{2,1,0:T(8,128)(2,1)}), bf16[16,16,128]{2,1,0:T(8,128)(2,1)S(1)}, u32[]{:S(2)}, u32[]{:S(2)}) async-start(bf16[16,16,128]{2,1,0:T(8,128)(2,1)} %broadcast_in_dim.37), calls=%async_computation.4 | async-start | bytes 131072 | tf_op jit(solution)/shard_map/all_to_all | solution.py:12
  97.0 1.3 convolution_subtract_fusion.4
  98.3 10.2 %all-to-all-done.4 = bf16[16,16,128]{2,1,0:T(8,128)(2,1)S(1)} async-done(((bf16[16,16,128]{2,1,0:T(8,128)(2,1)}), bf16[16,16,128]{2,1,0:T(8,128)(2,1)S(1)}, u32[]{:S(2)}, u32[]{:S(2)}) %all-to-all-start.4) | async-done | bytes 65568 | tf_op jit(solution)/shard_map/all_to_all | solution.py:12
  108.4 1.3 convolution_subtract_fusion.3
  109.8 0.7 broadcast_in_dim.38
  110.4 3.5 %all-to-all-start.5 = ((f32[16,16,128]{2,1,0:T(8,128)}), f32[16,16,128]{2,1,0:T(8,128)S(1)}, u32[]{:S(2)}, u32[]{:S(2)}) async-start(f32[16,16,128]{2,1,0:T(8,128)} %broadcast_in_dim.38), calls=%async_computation.5 | async-start | bytes 262144 | tf_op jit(solution)/shard_map/all_to_all | solution.py:12
  114.0 1.3 convolution_subtract_fusion.2
  115.2 10.5 %all-to-all-done.5 = f32[16,16,128]{2,1,0:T(8,128)S(1)} async-done(((f32[16,16,128]{2,1,0:T(8,128)}), f32[16,16,128]{2,1,0:T(8,128)S(1)}, u32[]{:S(2)}, u32[]{:S(2)}) %all-to-all-start.5) | async-done | bytes 131104 | tf_op jit(solution)/shard_map/all_to_all | solution.py:12
  125.8 1.3 fusion.9
  127.2 0.6 broadcast_in_dim.78
  127.8 3.5 %all-to-all-start.6 = ((bf16[16,16,128]{2,1,0:T(8,128)(2,1)}), bf16[16,16,128]{2,1,0:T(8,128)(2,1)S(1)}, u32[]{:S(2)}, u32[]{:S(2)}) async-start(bf16[16,16,128]{2,1,0:T(8,128)(2,1)} %broadcast_in_dim.78), calls=%async_computation.6 | async-start | bytes 131072 | tf_op jit(solution)/shard_map/all_to_all | solution.py:12
  131.3 1.3 convolution_subtract_fusion.1
  132.6 10.2 %all-to-all-done.6 = bf16[16,16,128]{2,1,0:T(8,128)(2,1)S(1)} async-done(((bf16[16,16,128]{2,1,0:T(8,128)(2,1)}), bf16[16,16,128]{2,1,0:T(8,128)(2,1)S(1)}, u32[]{:S(2)}, u32[]{:S(2)}) %all-to-all-start.6) | async-done | bytes 65568 | tf_op jit(solution)/shard_map/all_to_all | solution.py:12
  142.8 1.3 convolution_subtract_fusion
  144.1 0.7 broadcast_in_dim.79
  144.8 3.5 %all-to-all-start.7 = ((f32[16,16,128]{2,1,0:T(8,128)}), f32[16,16,128]{2,1,0:T(8,128)S(1)}, u32[]{:S(2)}, u32[]{:S(2)}) async-start(f32[16,16,128]{2,1,0:T(8,128)} %broadcast_in_dim.79), calls=%async_computation.7 | async-start | bytes 262144 | tf_op jit(solution)/shard_map/all_to_all | solution.py:12
  148.3 11.8 %all-to-all-done.7 = f32[16,16,128]{2,1,0:T(8,128)S(1)} async-done(((f32[16,16,128]{2,1,0:T(8,128)}), f32[16,16,128]{2,1,0:T(8,128)S(1)}, u32[]{:S(2)}, u32[]{:S(2)}) %all-to-all-start.7) | async-done | bytes 131104 | tf_op jit(solution)/shard_map/all_to_all | solution.py:12
  160.1 1.3 fusion.8
  161.5 8.4 %all_to_all.58 = bf16[4,4,16,128]{3,1,2,0:T(4,128)(2,1)S(1)} all-to-all(bf16[4,4,16,128]{3,1,2,0:T(4,128)(2,1)S(1)} %broadcast_in_dim.82), channel_id=1, replica_groups=mesh['yl'=4,'x'=4,'z'=8,'yh'=2,'c'=2] {'yl'}, dimensions={0} | all-to-all | bytes 131072 | tf_op jit(solution)/shard_map/all_to_all | solution.py:12
  169.9 0.8 broadcast_in_dim.84
  170.7 3.5 %all-to-all-start.9 = ((bf16[16,4,16,128]{3,1,2,0:T(4,128)(2,1)}), bf16[16,4,16,128]{3,1,2,0:T(4,128)(2,1)S(1)}, u32[]{:S(2)}, u32[]{:S(2)}) async-start(bf16[16,4,16,128]{3,1,2,0:T(4,128)(2,1)} %broadcast_in_dim.84), calls=%async_computation.9 | async-start | bytes 524288 | tf_op jit(solution)/shard_map/all_to_all | solution.py:12
  174.2 12.5 %all-to-all-done.9 = bf16[16,4,16,128]{3,1,2,0:T(4,128)(2,1)S(1)} async-done(((bf16[16,4,16,128]{3,1,2,0:T(4,128)(2,1)}), bf16[16,4,16,128]{3,1,2,0:T(4,128)(2,1)S(1)}, u32[]{:S(2)}, u32[]{:S(2)}) %all-to-all-start.9) | async-done | bytes 262176 | tf_op jit(solution)/shard_map/all_to_all | solution.py:12
  186.7 0.2 copy.22
  187.0 0.2 copy.90
  187.2 3.5 %fusion.31 = f32[16,512]{1,0:T(8,128)S(1)} fusion(bf16[512,4096]{1,0:T(8,128)(2,1)} %bitcast.205, bf16[16,8192]{1,0:T(8,128)(2,1)S(1)} %bitcast.213), kind=kOutput, calls=%fused_computation.65 | convolution fusion | flops 67108864 | bytes 4358144 | tf_op jit(solution)/shard_map/dot_general | solution.py:25
  190.7 1.2 fusion
  192.0 5.6 %convolution_bitcast_fusion = f32[4,1,16,128]{3,2,0,1:T(8,128)S(1)} fusion(bf16[16,8192,1]{1,0,2:T(8,128)(2,1)S(1)} %reshape.86, bf16[4,128,8192]{2,1,0:T(8,128)(2,1)} %bitcast.198), kind=kOutput, calls=%fused_computation | convolution fusion | flops 134217728 | bytes 8683520 | tf_op jit(solution)/shard_map/dot_general | solution.py:25
  197.7 0.7 broadcast_in_dim.85
  198.3 15.3 %all-to-all-start.10 = ((f32[8,2,16,128]{3,2,1,0:T(8,128)}), f32[8,2,16,128]{3,2,1,0:T(8,128)S(1)}, u32[]{:S(2)}, u32[]{:S(2)}) async-start(f32[8,2,16,128]{3,2,1,0:T(8,128)} %bitcast.44), calls=%async_computation.10 | async-start | bytes 262144 | tf_op jit(solution)/shard_map/all_to_all | solution.py:12
  213.8 5.1 %all-to-all-done.10 = f32[8,2,16,128]{3,2,1,0:T(8,128)S(1)} async-done(((f32[8,2,16,128]{3,2,1,0:T(8,128)}), f32[8,2,16,128]{3,2,1,0:T(8,128)S(1)}, u32[]{:S(2)}, u32[]{:S(2)}) %all-to-all-start.10) | async-done | bytes 131104 | tf_op jit(solution)/shard_map/all_to_all | solution.py:12
  219.0 0.7 copy.27
  (44 shorter events, 1.0 us)
Async XLA Ops:
  6.5 5.4 %copy-start.2 = (f32[2,1,64,128]{3,2,1,0:T(8,128)S(1)}, f32[2,1,64,128]{3,2,1,0:T(8,128)}, u32[]{:S(2)}) copy-start(f32[2,1,64,128]{3,2,1,0:T(8,128)} %param.3) | copy-start | bytes 196612
  6.5 69.2 %all-gather.7.cloned.1.call-start = ((), (), s32[]{:S(2)}) async-start(), calls=%async_computation.11 | async-start | bytes 4718592 | tf_op jit(solution)/shard_map/all_gather | solution.py:53
  8.9 116.9 %all-gather.9.cloned.1.call-start = ((), (), s32[]{:S(2)}) async-start(), calls=%async_computation.12 | async-start | bytes 4718592 | tf_op jit(solution)/shard_map/all_gather | solution.py:54
  9.6 182.3 %all-gather.11.cloned.1.call-start = ((), (), s32[]{:S(2)}) async-start(), calls=%async_computation.13 | async-start | bytes 9437184 | tf_op jit(solution)/shard_map/all_gather | solution.py:55
  21.4 25.0 %all-to-all-start = ((f32[16,64,128]{2,1,0:T(8,128)}), f32[16,64,128]{2,1,0:T(8,128)S(1)}, u32[]{:S(2)}, u32[]{:S(2)}) async-start(f32[16,64,128]{2,1,0:T(8,128)} %broadcast_in_dim.33), calls=%async_computation | async-start | bytes 1048576 | tf_op jit(solution)/shard_map/all_to_all | solution.py:12
  55.0 119.3 %copy-start.1 = (f32[4,16,128]{2,1,0:T(8,128)}, f32[4,16,128]{2,1,0:T(8,128)S(1)}, u32[]{:S(2)}) copy-start(f32[4,16,128]{2,1,0:T(8,128)S(1)} %all_to_all.55) | copy-start | bytes 98308
  93.5 15.0 %all-to-all-start.4 = ((bf16[16,16,128]{2,1,0:T(8,128)(2,1)}), bf16[16,16,128]{2,1,0:T(8,128)(2,1)S(1)}, u32[]{:S(2)}, u32[]{:S(2)}) async-start(bf16[16,16,128]{2,1,0:T(8,128)(2,1)} %broadcast_in_dim.37), calls=%async_computation.4 | async-start | bytes 131072 | tf_op jit(solution)/shard_map/all_to_all | solution.py:12
  110.4 15.3 %all-to-all-start.5 = ((f32[16,16,128]{2,1,0:T(8,128)}), f32[16,16,128]{2,1,0:T(8,128)S(1)}, u32[]{:S(2)}, u32[]{:S(2)}) async-start(f32[16,16,128]{2,1,0:T(8,128)} %broadcast_in_dim.38), calls=%async_computation.5 | async-start | bytes 262144 | tf_op jit(solution)/shard_map/all_to_all | solution.py:12
  127.8 15.0 %all-to-all-start.6 = ((bf16[16,16,128]{2,1,0:T(8,128)(2,1)}), bf16[16,16,128]{2,1,0:T(8,128)(2,1)S(1)}, u32[]{:S(2)}, u32[]{:S(2)}) async-start(bf16[16,16,128]{2,1,0:T(8,128)(2,1)} %broadcast_in_dim.78), calls=%async_computation.6 | async-start | bytes 131072 | tf_op jit(solution)/shard_map/all_to_all | solution.py:12
  144.8 15.3 %all-to-all-start.7 = ((f32[16,16,128]{2,1,0:T(8,128)}), f32[16,16,128]{2,1,0:T(8,128)S(1)}, u32[]{:S(2)}, u32[]{:S(2)}) async-start(f32[16,16,128]{2,1,0:T(8,128)} %broadcast_in_dim.79), calls=%async_computation.7 | async-start | bytes 262144 | tf_op jit(solution)/shard_map/all_to_all | solution.py:12
  170.7 16.0 %all-to-all-start.9 = ((bf16[16,4,16,128]{3,1,2,0:T(4,128)(2,1)}), bf16[16,4,16,128]{3,1,2,0:T(4,128)(2,1)S(1)}, u32[]{:S(2)}, u32[]{:S(2)}) async-start(bf16[16,4,16,128]{3,1,2,0:T(4,128)(2,1)} %broadcast_in_dim.84), calls=%async_computation.9 | async-start | bytes 524288 | tf_op jit(solution)/shard_map/all_to_all | solution.py:12
  187.0 3.7 %copy-start = (bf16[8,64,4096]{2,1,0:T(8,128)(2,1)S(1)}, bf16[8,64,4096]{2,1,0:T(8,128)(2,1)}, u32[]{:S(2)}) copy-start(bf16[8,64,4096]{2,1,0:T(8,128)(2,1)} %all-gather.9.cloned.1.call-done) | copy-start | bytes 12582916
  187.2 4.7 %slice-start = ((f32[4,16,128]{2,1,0:T(8,128)}), f32[1,16,128]{2,1,0:T(8,128)S(1)}, s32[]{:S(2)}) async-start(f32[4,16,128]{2,1,0:T(8,128)} %copy-done.1), calls=%async_computation.14 | async-start | bytes 16384 | tf_op jit(solution)/shard_map/unstack | solution.py:70
  198.3 20.6 %all-to-all-start.10 = ((f32[8,2,16,128]{3,2,1,0:T(8,128)}), f32[8,2,16,128]{3,2,1,0:T(8,128)S(1)}, u32[]{:S(2)}, u32[]{:S(2)}) async-start(f32[8,2,16,128]{3,2,1,0:T(8,128)} %bitcast.44), calls=%async_computation.10 | async-start | bytes 262144 | tf_op jit(solution)/shard_map/all_to_all | solution.py:12
Sparse Core Ops, SparseCore 0:
  9.5 43.3 all-gather.6
  55.0 37.4 all-gather.8
  94.7 55.0 all-gather.10

commit v3 on v2

--- a/solution.py
+++ b/solution.py
@@ -49,40 +49,45 @@
     few = cases // (xs * cores)
     pair = cores * share
 
-    start = lax.all_gather(stored[0, :, :block], "c", axis=0, tiled=True)
-    left = lax.all_gather(stored[0, :, :half], ("x", "c"), axis=0)
-    right = lax.all_gather(stored[0, :, half:], ("x", "c"), axis=0)
-    below = lax.all_gather(stored[1], ("x", "c"), axis=0)
-    left, right = left.reshape(xs, pair, half), right.reshape(xs, pair, half)
+    def rows_of_line(part):
+        return lax.all_gather(part, ("x", "c"), axis=0).reshape(
+            xs, cores * part.shape[0], part.shape[1]
+        )
 
-    def panel(row, column):
-        source = left if column * block < half else right
-        place = (column * block) % half
-        return source[row, :, place : place + block]
+    def after(value, done):
+        return lax.optimization_barrier((value, done))[0][:, 0]
+
+    columns = [rows_of_line(stored[0, :, :block])]
 
     together = lax.all_gather(given[0], "c", axis=0, tiled=True).T
     mine = lax.dynamic_index_in_dim(
         together.reshape(xs, cores, few, pair), lax.axis_index("c"), 1, False
     )
-    mine = mine.reshape(xs * few, pair)
-    first = times_exact(gather_chips(mine), start)
-    first = jnp.where(lax.axis_index("x") == 0, first, mine)
-    state = list(exchange(first.reshape(xs, few, pair), "x"))
-
-    sent = [state[0].astype(jnp.bfloat16)]
-    for step in range(1, steps):
-        whole = gather_chips(sent[step - 1])
-        for row in range(step, steps):
-            state[row] = state[row] - times(whole, panel(row, step - 1))
-        state[step] = times_exact(gather_chips(state[step]), panel(step, step))
+    state = list(exchange(mine, "x"))
+    columns.append(rows_of_line(after(factor, state[0])[0, :, block:half]))
+    whole = gather_chips(state[0])
+    last = rows_of_line(after(factor, whole)[0, :, half:])
+    columns += [last[:, :, :block], last[:, :, block:]]
+    sent = []
+    for step in range(steps):
+        state[step] = times_exact(whole, columns[step][step])
         sent.append(state[step].astype(jnp.bfloat16))
+        if step + 1 == steps:
+            break
+        whole = gather_chips(sent[step])
+        if step == 0:
+            below = rows_of_line(after(factor, whole)[1])
+        for row in range(step + 1, steps):
+            state[row] = state[row] - times(whole, columns[step][row])
+        whole = gather_chips(state[step + 1])
 
     shared = exchange(repeat(jnp.stack(sent), ys), "yl")[0]
     got = exchange(repeat(shared, lax.axis_size(CHIPS)), CHIPS)
     whole = got.transpose(2, 1, 0, 3).reshape(few, width)
-    upper = times(whole[:, :half], left.reshape(xs * pair, half)) + times(
-        whole[:, half:], right.reshape(xs * pair, half)
-    )
+    upper = times(whole[:, half:], last.reshape(xs * pair, half))
+    for index in range(2):
+        part = whole[:, index * block : (index + 1) * block]
+        upper += times(part, columns[index].reshape(xs * pair, block))
     lower = times(whole, below.reshape(xs * pair, width))
     upper = jnp.swapaxes(upper.reshape(few, xs, pair), 0, 1)
     lower = jnp.swapaxes(lower.reshape(few, xs, pair), 0, 1)

time: 228 us -> 220 us (0.965)
  blocking collectives: 62.4 us -> 76.5 us
  waiting for transfers between devices: 72.5 us -> 62.2 us
  starting transfers between devices: 42.9 us -> 33.4 us
  matrix products: 22.5 us -> 16.3 us
  local copies, waits for them, and re-layouts: 12.2 us -> 16.4 us
    all_to_all x4 -> x5, blocking collectives: 51.6 us -> 68.1 us  [exchange(): return lax.all_to_all(parts, axis, 0, 0, tiled=True)]
    all_to_all x7 -> x6, waiting for transfers between devices: 71.7 us -> 59 us  [exchange(): return lax.all_to_all(parts, axis, 0, 0, tiled=True)]
    all_to_all x7 -> x6, starting transfers between devices: 42.8 us -> 33.3 us  [exchange(): return lax.all_to_all(parts, axis, 0, 0, tiled=True)]
    dot_general x13 -> x14, matrix products: 22.5 us -> 16.3 us  [times(): lax.dot_general(values, rows, (((1,), (1,)), ((), ())), preferred_element...]
    slice x3 -> x6, local copies, waits for them, and re-layouts: 5.55 us -> 10.7 us  [the longest x2 3.14 us: body(): state[row] = state[row] - times(whole, columns[step][row])]
    all_gather x3 -> x4, waiting for transfers between devices: 0.04 us -> 3.15 us  [rows_of_line(): lax.all_gather(part, ('x', 'c'), axis=0)]
    all_gather x1 -> x0, blocking collectives: 2.43 us -> none  [body(): start = lax.all_gather(stored[0, :, :block], 'c', axis=0, tiled=True)]
where the time goes in v3:
time: 220 us; the launch traced here: 218 us
  blocking collectives  76.5 us (35%)
  waiting for transfers between devices  62.2 us (28%)
  starting transfers between devices  33.4 us (15%)
  local copies, waits for them, and re-layouts  16.4 us (7%)
  matrix products  16.3 us (7%)
  between operations  13.5 us (6%)
    all_to_all x5, blocking collectives, exchange(): return lax.all_to_all(parts, axis, 0, 0, tiled=True)  68.1 us
    all_to_all x6, waiting for transfers between devices, exchange(): return lax.all_to_all(parts, axis, 0, 0, tiled=True)  59 us
    all_to_all x6, starting transfers between devices, exchange(): return lax.all_to_all(parts, axis, 0, 0, tiled=True)  33.3 us
    dot_general x14, matrix products, times(): lax.dot_general(values, rows, (((1,), (1,)), ((), ())), preferred_element...  16.3 us
    all_gather x1, blocking collectives, body(): together = lax.all_gather(given[0], 'c', axis=0, tiled=True).T  8.38 us
  transfers between devices with their start and end apart: 10, of which 7 were waited for; matrix products, arithmetic and copies ran while one was open for 11% of the time, Pallas kernels for 0%

profile of v3, /device:TPU:1, one launch (start us, length us, event | category | flops | bytes accessed | tf_op | source)
XLA Modules:
  0.0 218.5 jit_solution(12834547364375894575)
XLA Ops:
  6.5 1.7 slice.108
  8.3 1.7 slice.111
  10.1 1.9 slice.115
  12.0 2.3 %slice.103 = bf16[1,1,64,8192]{3,2,1,0:T(8,128)(2,1)} slice(bf16[2,1,64,8192]{3,2,1,0:T(8,128)(2,1)} %param.2), slice={[1:2], [0:1], [0:64], [0:8192]} | slice | bytes 2097152 | tf_op jit(solution)/shard_map/slice | solution.py:79
  14.3 8.4 %all-gather = f32[1,1,128,128]{3,1,0,2:T(1,128)S(1)} all-gather(f32[1,1,64,128]{3,1,0,2:T(1,128)S(1)} %bitcast.218), channel_id=2, replica_groups=mesh['yl'=4,'x'=4,'z'=8,'yh'=2,'c'=2] {'c'}, dimensions={2}, use_global_device_ids=true | all-gather | bytes 98304 | tf_op jit(solution)/shard_map/all_gather | solution.py:62
  22.8 6.7 %all_to_all.55 = f32[4,16,128]{2,1,0:T(8,128)S(1)} all-to-all(f32[4,16,128]{2,1,0:T(8,128)S(1)} %dynamic-slice_bitcast_fusion.1), channel_id=1, replica_groups=mesh['yl'=4,'x'=4,'z'=8,'yh'=2,'c'=2] {'x'}, dimensions={0} | all-to-all | bytes 65536 | tf_op jit(solution)/shard_map/all_to_all | solution.py:12
  29.5 23.1 %all_to_all.56 = f32[16,16,128]{2,1,0:T(8,128)S(1)} all-to-all(f32[16,16,128]{2,1,0:T(8,128)S(1)} %broadcast_in_dim.33), channel_id=1, replica_groups=mesh['yl'=4,'x'=4,'z'=8,'yh'=2,'c'=2] {'z','yh'}, dimensions={0} | all-to-all | bytes 262144 | tf_op jit(solution)/shard_map/all_to_all | solution.py:12
  52.7 1.7 fusion.53
  54.4 0.3 fusion.3
  54.7 16.7 %all_to_all.57 = bf16[16,16,128]{2,1,0:T(8,128)(2,1)S(1)} all-to-all(bf16[16,16,128]{2,1,0:T(8,128)(2,1)S(1)} %broadcast_in_dim.34), channel_id=1, replica_groups=mesh['yl'=4,'x'=4,'z'=8,'yh'=2,'c'=2] {'z','yh'}, dimensions={0} | all-to-all | bytes 131072 | tf_op jit(solution)/shard_map/all_to_all | solution.py:12
  71.4 0.2 convolution_subtract_fusion.5
  71.7 0.7 broadcast_in_dim.35
  72.3 3.5 %all-to-all-start.3 = ((f32[16,16,128]{2,1,0:T(8,128)}), f32[16,16,128]{2,1,0:T(8,128)S(1)}, u32[]{:S(2)}, u32[]{:S(2)}) async-start(f32[16,16,128]{2,1,0:T(8,128)} %broadcast_in_dim.35), calls=%async_computation.3 | async-start | bytes 262144 | tf_op jit(solution)/shard_map/all_to_all | solution.py:12
  75.9 3.1 %all-gather.9.cloned.1.call-done = bf16[8,64,2048]{2,1,0:T(8,128)(2,1)} async-done(((bf16[1,64,2048]{2,1,0:T(8,128)(2,1)}), bf16[8,64,2048]{2,1,0:T(8,128)(2,1)}) %all-gather.9.cloned.1.call-update) | async-done | bytes 2097168 | tf_op jit(solution)/shard_map/all_gather | solution.py:53
  79.0 1.5 fusion.52
  80.4 7.2 %all-to-all-done.3 = f32[16,16,128]{2,1,0:T(8,128)S(1)} async-done(((f32[16,16,128]{2,1,0:T(8,128)}), f32[16,16,128]{2,1,0:T(8,128)S(1)}, u32[]{:S(2)}, u32[]{:S(2)}) %all-to-all-start.3) | async-done | bytes 131104 | tf_op jit(solution)/shard_map/all_to_all | solution.py:12
  87.7 0.3 fusion.9
  88.0 0.6 broadcast_in_dim.36
  88.6 4.9 %all-to-all-start.4 = ((bf16[16,16,128]{2,1,0:T(8,128)(2,1)}), bf16[16,16,128]{2,1,0:T(8,128)(2,1)S(1)}, u32[]{:S(2)}, u32[]{:S(2)}) async-start(bf16[16,16,128]{2,1,0:T(8,128)(2,1)} %broadcast_in_dim.36), calls=%async_computation.4 | async-start | bytes 131072 | tf_op jit(solution)/shard_map/all_to_all | solution.py:12
  93.5 0.2 convolution_subtract_fusion.4
  93.8 11.3 %all-to-all-done.4 = bf16[16,16,128]{2,1,0:T(8,128)(2,1)S(1)} async-done(((bf16[16,16,128]{2,1,0:T(8,128)(2,1)}), bf16[16,16,128]{2,1,0:T(8,128)(2,1)S(1)}, u32[]{:S(2)}, u32[]{:S(2)}) %all-to-all-start.4) | async-done | bytes 65568 | tf_op jit(solution)/shard_map/all_to_all | solution.py:12
  105.1 0.2 convolution_subtract_fusion.3
  105.3 0.7 broadcast_in_dim.37
  106.0 3.5 %all-to-all-start.5 = ((f32[16,16,128]{2,1,0:T(8,128)}), f32[16,16,128]{2,1,0:T(8,128)S(1)}, u32[]{:S(2)}, u32[]{:S(2)}) async-start(f32[16,16,128]{2,1,0:T(8,128)} %broadcast_in_dim.37), calls=%async_computation.5 | async-start | bytes 262144 | tf_op jit(solution)/shard_map/all_to_all | solution.py:12
  109.5 0.2 convolution_subtract_fusion.2
  109.8 11.5 %all-to-all-done.5 = f32[16,16,128]{2,1,0:T(8,128)S(1)} async-done(((f32[16,16,128]{2,1,0:T(8,128)}), f32[16,16,128]{2,1,0:T(8,128)S(1)}, u32[]{:S(2)}, u32[]{:S(2)}) %all-to-all-start.5) | async-done | bytes 131104 | tf_op jit(solution)/shard_map/all_to_all | solution.py:12
  121.4 1.3 fusion.2
  122.7 0.6 broadcast_in_dim.38
  123.4 9.7 %all-to-all-start.6 = ((bf16[16,16,128]{2,1,0:T(8,128)(2,1)}), bf16[16,16,128]{2,1,0:T(8,128)(2,1)S(1)}, u32[]{:S(2)}, u32[]{:S(2)}) async-start(bf16[16,16,128]{2,1,0:T(8,128)(2,1)} %broadcast_in_dim.38), calls=%async_computation.6 | async-start | bytes 131072 | tf_op jit(solution)/shard_map/all_to_all | solution.py:12
  133.0 0.2 convolution_subtract_fusion.1
  133.3 11.4 %all-to-all-done.6 = bf16[16,16,128]{2,1,0:T(8,128)(2,1)S(1)} async-done(((bf16[16,16,128]{2,1,0:T(8,128)(2,1)}), bf16[16,16,128]{2,1,0:T(8,128)(2,1)S(1)}, u32[]{:S(2)}, u32[]{:S(2)}) %all-to-all-start.6) | async-done | bytes 65568 | tf_op jit(solution)/shard_map/all_to_all | solution.py:12
  144.7 1.3 convolution_subtract_fusion
  146.0 14.4 %all_to_all.58 = f32[16,16,128]{2,1,0:T(8,128)S(1)} all-to-all(f32[16,16,128]{2,1,0:T(8,128)S(1)} %broadcast_in_dim.78), channel_id=1, replica_groups=mesh['yl'=4,'x'=4,'z'=8,'yh'=2,'c'=2] {'z','yh'}, dimensions={0} | all-to-all | bytes 262144 | tf_op jit(solution)/shard_map/all_to_all | solution.py:12
  160.4 1.5 fusion.1
  162.0 7.2 %all_to_all.59 = bf16[4,4,16,128]{3,1,2,0:T(4,128)(2,1)S(1)} all-to-all(bf16[4,4,16,128]{3,1,2,0:T(4,128)(2,1)S(1)} %broadcast_in_dim.82), channel_id=1, replica_groups=mesh['yl'=4,'x'=4,'z'=8,'yh'=2,'c'=2] {'yl'}, dimensions={0} | all-to-all | bytes 131072 | tf_op jit(solution)/shard_map/all_to_all | solution.py:12
  169.2 0.8 broadcast_in_dim.84
  170.0 3.5 %all-to-all-start.9 = ((bf16[16,4,16,128]{3,1,2,0:T(4,128)(2,1)}), bf16[16,4,16,128]{3,1,2,0:T(4,128)(2,1)S(1)}, u32[]{:S(2)}, u32[]{:S(2)}) async-start(bf16[16,4,16,128]{3,1,2,0:T(4,128)(2,1)} %broadcast_in_dim.84), calls=%async_computation.9 | async-start | bytes 524288 | tf_op jit(solution)/shard_map/all_to_all | solution.py:12
  173.5 12.4 %all-to-all-done.9 = bf16[16,4,16,128]{3,1,2,0:T(4,128)(2,1)S(1)} async-done(((bf16[16,4,16,128]{3,1,2,0:T(4,128)(2,1)}), bf16[16,4,16,128]{3,1,2,0:T(4,128)(2,1)S(1)}, u32[]{:S(2)}, u32[]{:S(2)}) %all-to-all-start.9) | async-done | bytes 262176 | tf_op jit(solution)/shard_map/all_to_all | solution.py:12
  185.9 0.2 copy.22
  186.2 0.2 copy.83
  186.4 3.5 %fusion.29 = f32[16,512]{1,0:T(8,128)S(1)} fusion(bf16[512,4096]{1,0:T(8,128)(2,1)} %bitcast.201, bf16[16,8192]{1,0:T(8,128)(2,1)S(1)} %bitcast.211), kind=kOutput, calls=%fused_computation.59 | convolution fusion | flops 67108864 | bytes 4358144 | tf_op jit(solution)/shard_map/dot_general | solution.py:25
  189.9 0.7 convolution_add_fusion.1
  190.5 0.7 fusion
  191.3 5.6 %convolution_bitcast_fusion = f32[4,1,16,128]{3,2,0,1:T(8,128)S(1)} fusion(bf16[16,8192,1]{1,0,2:T(8,128)(2,1)S(1)} %reshape.89, bf16[4,128,8192]{2,1,0:T(8,128)(2,1)} %bitcast.195), kind=kOutput, calls=%fused_computation | convolution fusion | flops 134217728 | bytes 8683520 | tf_op jit(solution)/shard_map/dot_general | solution.py:25
  196.9 0.7 broadcast_in_dim.85
  197.6 8.2 %all-to-all-start.10 = ((f32[8,2,16,128]{3,2,1,0:T(8,128)}), f32[8,2,16,128]{3,2,1,0:T(8,128)S(1)}, u32[]{:S(2)}, u32[]{:S(2)}) async-start(f32[8,2,16,128]{3,2,1,0:T(8,128)} %bitcast.47), calls=%async_computation.10 | async-start | bytes 262144 | tf_op jit(solution)/shard_map/all_to_all | solution.py:12
  206.0 5.1 %all-to-all-done.10 = f32[8,2,16,128]{3,2,1,0:T(8,128)S(1)} async-done(((f32[8,2,16,128]{3,2,1,0:T(8,128)}), f32[8,2,16,128]{3,2,1,0:T(8,128)S(1)}, u32[]{:S(2)}, u32[]{:S(2)}) %all-to-all-start.10) | async-done | bytes 131104 | tf_op jit(solution)/shard_map/all_to_all | solution.py:12
  211.2 0.7 copy.27
  (46 shorter events, 1.1 us)
Async XLA Ops:
  6.5 7.8 %copy-start.2 = (f32[2,1,64,128]{3,2,1,0:T(8,128)S(1)}, f32[2,1,64,128]{3,2,1,0:T(8,128)}, u32[]{:S(2)}) copy-start(f32[2,1,64,128]{3,2,1,0:T(8,128)} %param.3) | copy-start | bytes 196612
  6.5 46.2 %all-gather.7.cloned.1.call-start = ((), (), s32[]{:S(2)}) async-start(), calls=%async_computation.11 | async-start | bytes 2359296 | tf_op jit(solution)/shard_map/all_gather | solution.py:53
  8.3 70.7 %all-gather.9.cloned.1.call-start = ((), (), s32[]{:S(2)}) async-start(), calls=%async_computation.12 | async-start | bytes 2359296 | tf_op jit(solution)/shard_map/all_gather | solution.py:53
  10.0 111.3 %all-gather.11.cloned.1.call-start = ((), (), s32[]{:S(2)}) async-start(), calls=%async_computation.13 | async-start | bytes 4718592 | tf_op jit(solution)/shard_map/all_gather | solution.py:53
  12.0 179.3 %all-gather.13.cloned.1.call-start = ((), (), s32[]{:S(2)}) async-start(), calls=%async_computation.14 | async-start | bytes 9437184 | tf_op jit(solution)/shard_map/all_gather | solution.py:53
  72.3 15.3 %all-to-all-start.3 = ((f32[16,16,128]{2,1,0:T(8,128)}), f32[16,16,128]{2,1,0:T(8,128)S(1)}, u32[]{:S(2)}, u32[]{:S(2)}) async-start(f32[16,16,128]{2,1,0:T(8,128)} %broadcast_in_dim.35), calls=%async_computation.3 | async-start | bytes 262144 | tf_op jit(solution)/shard_map/all_to_all | solution.py:12
  88.6 16.4 %all-to-all-start.4 = ((bf16[16,16,128]{2,1,0:T(8,128)(2,1)}), bf16[16,16,128]{2,1,0:T(8,128)(2,1)S(1)}, u32[]{:S(2)}, u32[]{:S(2)}) async-start(bf16[16,16,128]{2,1,0:T(8,128)(2,1)} %broadcast_in_dim.36), calls=%async_computation.4 | async-start | bytes 131072 | tf_op jit(solution)/shard_map/all_to_all | solution.py:12
  106.0 15.3 %all-to-all-start.5 = ((f32[16,16,128]{2,1,0:T(8,128)}), f32[16,16,128]{2,1,0:T(8,128)S(1)}, u32[]{:S(2)}, u32[]{:S(2)}) async-start(f32[16,16,128]{2,1,0:T(8,128)} %broadcast_in_dim.37), calls=%async_computation.5 | async-start | bytes 262144 | tf_op jit(solution)/shard_map/all_to_all | solution.py:12
  123.4 21.3 %all-to-all-start.6 = ((bf16[16,16,128]{2,1,0:T(8,128)(2,1)}), bf16[16,16,128]{2,1,0:T(8,128)(2,1)S(1)}, u32[]{:S(2)}, u32[]{:S(2)}) async-start(bf16[16,16,128]{2,1,0:T(8,128)(2,1)} %broadcast_in_dim.38), calls=%async_computation.6 | async-start | bytes 131072 | tf_op jit(solution)/shard_map/all_to_all | solution.py:12
  160.4 29.5 %copy-start = (bf16[8,64,2048]{2,1,0:T(8,128)(2,1)S(1)}, bf16[8,64,2048]{2,1,0:T(8,128)(2,1)}, u32[]{:S(2)}) copy-start(bf16[8,64,2048]{2,1,0:T(8,128)(2,1)} %all-gather.7.cloned.1.call-done) | copy-start | bytes 6291460
  170.0 15.9 %all-to-all-start.9 = ((bf16[16,4,16,128]{3,1,2,0:T(4,128)(2,1)}), bf16[16,4,16,128]{3,1,2,0:T(4,128)(2,1)S(1)}, u32[]{:S(2)}, u32[]{:S(2)}) async-start(bf16[16,4,16,128]{3,1,2,0:T(4,128)(2,1)} %broadcast_in_dim.84), calls=%async_computation.9 | async-start | bytes 524288 | tf_op jit(solution)/shard_map/all_to_all | solution.py:12
  186.2 4.3 %copy-start.1 = (bf16[8,64,2048]{2,1,0:T(8,128)(2,1)S(1)}, bf16[8,64,2048]{2,1,0:T(8,128)(2,1)}, u32[]{:S(2)}) copy-start(bf16[8,64,2048]{2,1,0:T(8,128)(2,1)} %all-gather.9.cloned.1.call-done) | copy-start | bytes 6291460
  197.6 13.5 %all-to-all-start.10 = ((f32[8,2,16,128]{3,2,1,0:T(8,128)}), f32[8,2,16,128]{3,2,1,0:T(8,128)S(1)}, u32[]{:S(2)}, u32[]{:S(2)}) async-start(f32[8,2,16,128]{3,2,1,0:T(8,128)} %bitcast.47), calls=%async_computation.10 | async-start | bytes 262144 | tf_op jit(solution)/shard_map/all_to_all | solution.py:12
Sparse Core Ops, SparseCore 0:
  9.5 36.3 all-gather.6
  48.1 30.8 all-gather.8
  81.1 37.7 all-gather.10
  120.9 55.0 all-gather.12

commit v4 on v2

v4 whole, which is shorter than its diff:
```python
import jax
import jax.numpy as jnp
from jax import lax
from jax.sharding import Mesh, PartitionSpec as P

BLK = ("yl", "x")
RHS = ("z", "yh", "c")
CHIPS = ("z", "yh")


def exchange(parts, axis):
    return lax.all_to_all(parts, axis, 0, 0, tiled=True)


def repeat(part, count):
    return jnp.broadcast_to(part[None], (count,) + part.shape)


def gather_chips(part):
    got = exchange(repeat(part, lax.axis_size(CHIPS)), CHIPS)
    return jnp.swapaxes(got, 0, 1).reshape(part.shape[0], -1)


def times(values, rows):
    return lax.dot_general(
        values, rows, (((1,), (1,)), ((), ())), preferred_element_type=jnp.float32
    )


def times_exact(values, rows):
    first = lax.reduce_precision(values, 8, 7)
    rest = values - first
    second = lax.reduce_precision(rest, 8, 7)
    third = rest - second
    terms = jnp.concatenate([first, second, third], 0).astype(jnp.bfloat16)
    a, b, c = jnp.split(times(terms, rows), 3, 0)
    return (c + b) + a


def body(factor, loads):
    xs, cores = lax.axis_size("x"), lax.axis_size("c")
    stored, given = factor[:, 0], loads[:, 0]
    share, width = stored.shape[1:]
    cases = given.shape[2]
    block = share * lax.axis_size(RHS)
    steps = width // block
    half = width // 2
    few = cases // (xs * cores)
    pair = cores * share

    def rows_of_line(part):
        return lax.all_gather(part, ("x", "c"), axis=0).reshape(
            xs, cores * part.shape[0], part.shape[1]
        )

    left = rows_of_line(stored[0, :, :half])

    together = lax.all_gather(given[0], "c", axis=0, tiled=True).T
    mine = lax.dynamic_index_in_dim(
        together.reshape(xs, cores, few, pair), lax.axis_index("c"), 1, False
    )
    mine = mine.reshape(xs * few, pair)
    def column(step):
        source = left if step * block < half else right
        place = (step * block) % half
        return source[:, :, place : place + block]

    start = lax.all_gather(stored[0, :, :block], "c", axis=0, tiled=True)
    whole = gather_chips(mine)
    first = times_exact(whole, start)
    first = jnp.where(lax.axis_index("x") == 0, first, mine)
    state = exchange(first.reshape(xs, few, pair), "x")

    none = jnp.minimum(jnp.abs(first[0, 0]), 0.0).astype(jnp.int32)
    right = rows_of_line(lax.dynamic_slice_in_dim(stored[0], half + none, half, 1))
    below = rows_of_line(lax.dynamic_index_in_dim(stored, 1 + none, 0, False))

    solved, sent = [state[0]], [state[0].astype(jnp.bfloat16)]
    state = state[1:]
    for step in range(1, steps):
        whole = gather_chips(sent[-1])
        rows = column(step - 1)[step:].reshape(-1, block)
        update = times(whole, rows).reshape(few, steps - step, pair)
        state = state - jnp.swapaxes(update, 0, 1)
        solved.append(times_exact(gather_chips(state[0]), column(step)[step]))
        sent.append(solved[-1].astype(jnp.bfloat16))
        state = state[1:]

    height = ("yl", "yh")
    halves = lax.axis_size("yh")
    shared = jnp.concatenate(sent, 0)
    shared = exchange(repeat(shared, lax.axis_size(height)), height)[:halves]
    shared = shared.reshape(-1, pair)
    got = exchange(repeat(shared, lax.axis_size("z")), "z")
    got = got.reshape(-1, halves, steps, few, pair)
    whole = got.transpose(3, 2, 0, 1, 4).reshape(few, width)
    upper = times(whole[:, :half], left.reshape(xs * pair, half)) + times(
        whole[:, half:], right.reshape(xs * pair, half)
    )
    lower = times(whole, below.reshape(xs * pair, width))
    upper = jnp.swapaxes(upper.reshape(few, xs, pair), 0, 1)
    lower = jnp.swapaxes(lower.reshape(few, xs, pair), 0, 1)
    owner = lax.axis_index("yl") == 0
    upper = jnp.where(owner, jnp.stack(solved), upper)
    both = jnp.stack([upper, lower], 1)[:, None]
    both = jnp.broadcast_to(both, (xs, cores) + both.shape[2:])
    both = both.reshape((xs * cores,) + both.shape[2:])
    back = exchange(both, ("x", "c"))
    back = jnp.swapaxes(back, 0, 1).reshape(2, cases, pair).transpose(0, 2, 1)
    back = lax.dynamic_slice_in_dim(back, lax.axis_index("c") * share, share, 1)
    top = jnp.where(owner, back[0], given[0] - back[0])
    return jnp.stack([top, given[1] - back[1]])[:, None]


def solution(mesh):
    fine = Mesh(mesh.devices.reshape(4, 4, 8, 2, 2), BLK + RHS)
    spec = P(None, BLK, RHS, None)
    return jax.shard_map(
        body, mesh=fine, in_specs=(spec, spec), out_specs=spec, check_vma=False
    )
```

time: 228 us -> 223 us (0.978)
  blocking collectives: 62.4 us -> 122 us
  waiting for transfers between devices: 72.5 us -> 26.4 us
  starting transfers between devices: 42.9 us -> 29 us
  matrix products: 22.5 us -> 19.7 us
    all_to_all x4 -> x8, blocking collectives: 51.6 us -> 111 us  [exchange(): return lax.all_to_all(parts, axis, 0, 0, tiled=True)]
    all_to_all x7 -> x3, waiting for transfers between devices: 71.7 us -> 25.6 us  [exchange(): return lax.all_to_all(parts, axis, 0, 0, tiled=True)]
    all_to_all x7 -> x3, starting transfers between devices: 42.8 us -> 28.9 us  [exchange(): return lax.all_to_all(parts, axis, 0, 0, tiled=True)]
    dot_general x13 -> x10, matrix products: 22.5 us -> 19.7 us  [times(): lax.dot_general(values, rows, (((1,), (1,)), ((), ())), preferred_element...]
    broadcast_in_dim x11 -> x12, local copies, waits for them, and re-layouts: 4.35 us -> 1.78 us  [repeat(): return jnp.broadcast_to(part[None], (count,) + part.shape)]
    slice x2 -> x5, local copies, waits for them, and re-layouts: 4.57 us -> 2.41 us  [the longest x1 1.89 us: body(): left = rows_of_line(stored[0, :, :half])]
  transfers between devices with their start and end apart: 10 -> 6, of which waited for: 7 -> 3; matrix products, arithmetic and copies ran while one was open for 11% -> 10% of each run, Pallas kernels for 0% -> 0%
where the time goes in v4:
time: 223 us; the launch traced here: 222 us
  blocking collectives  122 us (55%)
  starting transfers between devices  29 us (13%)
  waiting for transfers between devices  26.4 us (12%)
  matrix products  19.7 us (9%)
  between operations  14.1 us (6%)
  local copies, waits for them, and re-layouts  10.8 us (5%)
    all_to_all x8, blocking collectives, exchange(): return lax.all_to_all(parts, axis, 0, 0, tiled=True)  111 us
    all_to_all x3, starting transfers between devices, exchange(): return lax.all_to_all(parts, axis, 0, 0, tiled=True)  28.9 us
    all_to_all x3, waiting for transfers between devices, exchange(): return lax.all_to_all(parts, axis, 0, 0, tiled=True)  25.6 us
    dot_general x10, matrix products, times(): lax.dot_general(values, rows, (((1,), (1,)), ((), ())), preferred_element...  19.7 us
    all_gather x1, blocking collectives, body(): together = lax.all_gather(given[0], 'c', axis=0, tiled=True).T  8.37 us
  transfers between devices with their start and end apart: 6, of which 3 were waited for; matrix products, arithmetic and copies ran while one was open for 10% of the time, Pallas kernels for 0%

profile of v4, /device:TPU:1, one launch (start us, length us, event | category | flops | bytes accessed | tf_op | source)
XLA Modules:
  0.0 222.0 jit_solution(6767508241366107884)
XLA Ops:
  6.5 1.9 slice.113
  8.5 0.9 fusion.60
  9.4 8.4 %all-gather = f32[1,1,128,128]{3,1,0,2:T(1,128)S(1)} all-gather(f32[1,1,64,128]{3,1,0,2:T(1,128)S(1)} %bitcast.172), channel_id=2, replica_groups=mesh['yl'=4,'x'=4,'z'=8,'yh'=2,'c'=2] {'c'}, dimensions={2}, use_global_device_ids=true | all-gather | bytes 98304 | tf_op jit(solution)/shard_map/all_gather | solution.py:58
  17.8 0.1 copy.12
  17.9 0.9 broadcast_in_dim.35
  18.8 10.0 %all-to-all-start = ((f32[16,64,128]{2,1,0:T(8,128)}), f32[16,64,128]{2,1,0:T(8,128)S(1)}, u32[]{:S(2)}, u32[]{:S(2)}) async-start(f32[16,64,128]{2,1,0:T(8,128)} %broadcast_in_dim.35), calls=%async_computation | async-start | bytes 1048576 | tf_op jit(solution)/shard_map/all_to_all | solution.py:12
  28.8 0.0 all-gather.10.cloned.1.call-start
  28.9 1.0 slice.110
  29.9 2.6 %all-gather.1 = bf16[1,128,2048]{2,1,0:T(8,128)(2,1)S(1)} all-gather(bf16[1,64,2048]{2,1,0:T(8,128)(2,1)S(1)} %slice.110), channel_id=3, replica_groups=mesh['yl'=4,'x'=4,'z'=8,'yh'=2,'c'=2] {'c'}, dimensions={1}, use_global_device_ids=true | all-gather | bytes 786432 | tf_op jit(solution)/shard_map/all_gather | solution.py:68
  32.5 11.3 %all-to-all-done = f32[16,64,128]{2,1,0:T(8,128)S(1)} async-done(((f32[16,64,128]{2,1,0:T(8,128)}), f32[16,64,128]{2,1,0:T(8,128)S(1)}, u32[]{:S(2)}, u32[]{:S(2)}) %all-to-all-start) | async-done | bytes 524320 | tf_op jit(solution)/shard_map/all_to_all | solution.py:12
  43.8 0.1 reduce-precision_convert_fusion.1
  43.9 0.4 fusion.13
  44.3 0.5 slice.120
  45.5 1.1 constant_dynamic-slice_fusion
  46.6 1.0 constant_dynamic-slice_fusion.1
  47.6 0.0 all-gather.12.cloned.1.call-start
  47.7 0.7 all-gather.12.cloned.1.call-update
  48.4 8.1 %all_to_all.55 = f32[4,16,128]{2,1,0:T(8,128)S(1)} all-to-all(f32[4,16,128]{2,1,0:T(8,128)S(1)} %bitcast.176), channel_id=1, replica_groups=mesh['yl'=4,'x'=4,'z'=8,'yh'=2,'c'=2] {'x'}, dimensions={0} | all-to-all | bytes 65536 | tf_op jit(solution)/shard_map/all_to_all | solution.py:12
  56.5 20.7 %all_to_all.56 = bf16[16,16,128]{2,1,0:T(8,128)(2,1)S(1)} all-to-all(bf16[16,16,128]{2,1,0:T(8,128)(2,1)S(1)} %broadcast_in_dim.73), channel_id=1, replica_groups=mesh['yl'=4,'x'=4,'z'=8,'yh'=2,'c'=2] {'z','yh'}, dimensions={0} | all-to-all | bytes 131072 | tf_op jit(solution)/shard_map/all_to_all | solution.py:12
  77.3 0.0 all-gather.8.cloned.1.call-done
  77.3 1.9 fusion.6
  79.3 14.4 %all_to_all.57 = f32[16,16,128]{2,1,0:T(8,128)S(1)} all-to-all(f32[16,16,128]{2,1,0:T(8,128)S(1)} %broadcast_in_dim.75), channel_id=1, replica_groups=mesh['yl'=4,'x'=4,'z'=8,'yh'=2,'c'=2] {'z','yh'}, dimensions={0} | all-to-all | bytes 262144 | tf_op jit(solution)/shard_map/all_to_all | solution.py:12
  93.7 1.3 fusion.22
  95.1 14.2 %all_to_all.58 = bf16[16,16,128]{2,1,0:T(8,128)(2,1)S(1)} all-to-all(bf16[16,16,128]{2,1,0:T(8,128)(2,1)S(1)} %broadcast_in_dim.76), channel_id=1, replica_groups=mesh['yl'=4,'x'=4,'z'=8,'yh'=2,'c'=2] {'z','yh'}, dimensions={0} | all-to-all | bytes 131072 | tf_op jit(solution)/shard_map/all_to_all | solution.py:12
  109.4 1.7 fusion.9
  111.2 14.5 %all_to_all.59 = f32[16,16,128]{2,1,0:T(8,128)S(1)} all-to-all(f32[16,16,128]{2,1,0:T(8,128)S(1)} %broadcast_in_dim.78), channel_id=1, replica_groups=mesh['yl'=4,'x'=4,'z'=8,'yh'=2,'c'=2] {'z','yh'}, dimensions={0} | all-to-all | bytes 262144 | tf_op jit(solution)/shard_map/all_to_all | solution.py:12
  125.7 1.3 fusion.21
  127.1 14.1 %all_to_all.60 = bf16[16,16,128]{2,1,0:T(8,128)(2,1)S(1)} all-to-all(bf16[16,16,128]{2,1,0:T(8,128)(2,1)S(1)} %broadcast_in_dim.79), channel_id=1, replica_groups=mesh['yl'=4,'x'=4,'z'=8,'yh'=2,'c'=2] {'z','yh'}, dimensions={0} | all-to-all | bytes 131072 | tf_op jit(solution)/shard_map/all_to_all | solution.py:12
  141.3 1.3 fusion.11
  142.6 14.4 %all_to_all.61 = f32[16,16,128]{2,1,0:T(8,128)S(1)} all-to-all(f32[16,16,128]{2,1,0:T(8,128)S(1)} %broadcast_in_dim.81), channel_id=1, replica_groups=mesh['yl'=4,'x'=4,'z'=8,'yh'=2,'c'=2] {'z','yh'}, dimensions={0} | all-to-all | bytes 262144 | tf_op jit(solution)/shard_map/all_to_all | solution.py:12
  157.0 1.3 fusion.20
  158.4 10.2 %all_to_all.62 = bf16[8,64,128]{2,1,0:T(8,128)(2,1)S(1)} all-to-all(bf16[8,64,128]{2,1,0:T(8,128)(2,1)S(1)} %broadcast_in_dim.82), channel_id=1, replica_groups=mesh['yl'=4,'x'=4,'z'=8,'yh'=2,'c'=2] {'yl','yh'}, dimensions={0} | all-to-all | bytes 262144 | tf_op jit(solution)/shard_map/all_to_all | solution.py:12
  168.6 0.7 broadcast_in_dim.84
  169.4 3.4 %all-to-all-start.9 = ((bf16[8,128,128]{2,1,0:T(8,128)(2,1)}), bf16[8,128,128]{2,1,0:T(8,128)(2,1)S(1)}, u32[]{:S(2)}, u32[]{:S(2)}) async-start(bf16[8,128,128]{2,1,0:T(8,128)(2,1)} %broadcast_in_dim.84), calls=%async_computation.9 | async-start | bytes 524288 | tf_op jit(solution)/shard_map/all_to_all | solution.py:12
  172.8 9.2 %all-to-all-done.9 = bf16[8,128,128]{2,1,0:T(8,128)(2,1)S(1)} async-done(((bf16[8,128,128]{2,1,0:T(8,128)(2,1)}), bf16[8,128,128]{2,1,0:T(8,128)(2,1)S(1)}, u32[]{:S(2)}, u32[]{:S(2)}) %all-to-all-start.9) | async-done | bytes 262176 | tf_op jit(solution)/shard_map/all_to_all | solution.py:12
  182.0 0.3 copy.20
  182.3 0.2 reshape.108
  182.5 0.2 reshape.121
  182.7 3.5 %fusion.43 = f32[16,512]{1,0:T(8,128)S(1)} fusion(bf16[512,4096]{1,0:T(8,128)(2,1)} %bitcast.161, bf16[16,8192]{1,0:T(8,128)(2,1)S(1)} %reshape.108), kind=kOutput, calls=%fused_computation.63 | convolution fusion | flops 67108864 | bytes 4358144 | tf_op jit(solution)/shard_map/dot_general | solution.py:25
  186.2 1.2 fusion.2
  187.5 5.6 %convolution_bitcast_fusion = f32[4,1,16,128]{3,2,0,1:T(8,128)S(1)} fusion(bf16[16,8192,1]{1,0,2:T(8,128)(2,1)S(1)} %reshape.121, bf16[4,128,8192]{2,1,0:T(8,128)(2,1)} %bitcast.162), kind=kOutput, calls=%fused_computation.2 | convolution fusion | flops 134217728 | bytes 8683520 | tf_op jit(solution)/shard_map/dot_general | solution.py:25
  193.2 0.7 broadcast_in_dim.85
  193.8 15.5 %all-to-all-start.10 = ((f32[8,2,16,128]{3,2,1,0:T(8,128)}), f32[8,2,16,128]{3,2,1,0:T(8,128)S(1)}, u32[]{:S(2)}, u32[]{:S(2)}) async-start(f32[8,2,16,128]{3,2,1,0:T(8,128)} %bitcast.44), calls=%async_computation.10 | async-start | bytes 262144 | tf_op jit(solution)/shard_map/all_to_all | solution.py:12
  209.3 0.1 copy.26
  209.4 0.1 copy.27
  209.5 5.1 %all-to-all-done.10 = f32[8,2,16,128]{3,2,1,0:T(8,128)S(1)} async-done(((f32[8,2,16,128]{3,2,1,0:T(8,128)}), f32[8,2,16,128]{3,2,1,0:T(8,128)S(1)}, u32[]{:S(2)}, u32[]{:S(2)}) %all-to-all-start.10) | async-done | bytes 131104 | tf_op jit(solution)/shard_map/all_to_all | solution.py:12
  214.6 0.1 dynamic-slice_bitcast_fusion
  214.8 0.7 copy.25
  (43 shorter events, 0.6 us)
Async XLA Ops:
  6.5 70.8 %all-gather.8.cloned.1.call-start = ((), (), s32[]{:S(2)}) async-start(), calls=%async_computation.11 | async-start | bytes 4718592 | tf_op jit(solution)/shard_map/all_gather | solution.py:52
  8.4 37.0 %copy-start.1 = (bf16[2,1,64,8192]{3,2,1,0:T(8,128)(2,1)S(1)}, bf16[2,1,64,8192]{3,2,1,0:T(8,128)(2,1)}, u32[]{:S(2)}) copy-start(bf16[2,1,64,8192]{3,2,1,0:T(8,128)(2,1)} %param.2) | copy-start | bytes 6291460
  18.8 25.0 %all-to-all-start = ((f32[16,64,128]{2,1,0:T(8,128)}), f32[16,64,128]{2,1,0:T(8,128)S(1)}, u32[]{:S(2)}, u32[]{:S(2)}) async-start(f32[16,64,128]{2,1,0:T(8,128)} %broadcast_in_dim.35), calls=%async_computation | async-start | bytes 1048576 | tf_op jit(solution)/shard_map/all_to_all | solution.py:12
  28.8 96.9 %all-gather.10.cloned.1.call-start = ((), (), s32[]{:S(2)}) async-start(), calls=%async_computation.12 | async-start | bytes 4718592 | tf_op jit(solution)/shard_map/all_gather | solution.py:52
  47.6 139.8 %all-gather.12.cloned.1.call-start = ((), (), s32[]{:S(2)}) async-start(), calls=%async_computation.13 | async-start | bytes 9437184 | tf_op jit(solution)/shard_map/all_gather | solution.py:52
  56.5 116.3 %copy-start.2 = (f32[4,16,128]{2,1,0:T(8,128)}, f32[4,16,128]{2,1,0:T(8,128)S(1)}, u32[]{:S(2)}) copy-start(f32[4,16,128]{2,1,0:T(8,128)S(1)} %all_to_all.55) | copy-start | bytes 98308
  169.4 12.7 %all-to-all-start.9 = ((bf16[8,128,128]{2,1,0:T(8,128)(2,1)}), bf16[8,128,128]{2,1,0:T(8,128)(2,1)S(1)}, u32[]{:S(2)}, u32[]{:S(2)}) async-start(bf16[8,128,128]{2,1,0:T(8,128)(2,1)} %broadcast_in_dim.84), calls=%async_computation.9 | async-start | bytes 524288 | tf_op jit(solution)/shard_map/all_to_all | solution.py:12
  182.7 3.5 %copy-start = (bf16[8,1,64,4096]{3,2,1,0:T(8,128)(2,1)S(1)}, bf16[8,1,64,4096]{3,2,1,0:T(8,128)(2,1)}, u32[]{:S(2)}) copy-start(bf16[8,1,64,4096]{3,2,1,0:T(8,128)(2,1)} %all-gather.10.cloned.1.call-done) | copy-start | bytes 12582916
  182.7 4.7 %slice-start = ((f32[4,16,128]{2,1,0:T(8,128)}), f32[1,16,128]{2,1,0:T(8,128)S(1)}, s32[]{:S(2)}) async-start(f32[4,16,128]{2,1,0:T(8,128)} %copy-done.2), calls=%async_computation.14 | async-start | bytes 16384 | tf_op jit(solution)/shard_map/slice | solution.py:78
  193.8 20.8 %all-to-all-start.10 = ((f32[8,2,16,128]{3,2,1,0:T(8,128)}), f32[8,2,16,128]{3,2,1,0:T(8,128)S(1)}, u32[]{:S(2)}, u32[]{:S(2)}) async-start(f32[8,2,16,128]{3,2,1,0:T(8,128)} %bitcast.44), calls=%async_computation.10 | async-start | bytes 262144 | tf_op jit(solution)/shard_map/all_to_all | solution.py:12
Sparse Core Ops, SparseCore 0:
  9.5 43.3 all-gather.7
  55.0 37.4 all-gather.9
  94.7 55.0 all-gather.11

commit v5 on v4

v5 whole, which is shorter than its diff:
```python
import functools

import jax
import jax.numpy as jnp
from jax import lax
from jax.experimental import pallas as pl
from jax.experimental.pallas import tpu as pltpu
from jax.sharding import Mesh, PartitionSpec as P

BLK = ("yl", "x")
RHS = ("z", "yh", "c")
CHIPS = ("z", "yh")


def exchange(parts, axis):
    return lax.all_to_all(parts, axis, 0, 0, tiled=True)


def repeat(part, count):
    return jnp.broadcast_to(part[None], (count,) + part.shape)


def gather_chips(part):
    got = exchange(repeat(part, lax.axis_size(CHIPS)), CHIPS)
    return jnp.swapaxes(got, 0, 1).reshape(part.shape[0], -1)


def times(values, rows):
    return lax.dot_general(
        values, rows, (((1,), (1,)), ((), ())), preferred_element_type=jnp.float32
    )


def times_exact(values, rows):
    first = lax.reduce_precision(values, 8, 7)
    rest = values - first
    second = lax.reduce_precision(rest, 8, 7)
    third = rest - second
    terms = jnp.concatenate([first, second, third], 0).astype(jnp.bfloat16)
    a, b, c = jnp.split(times(terms, rows), 3, 0)
    return (c + b) + a


TILE, SLOTS = 1024, 6


def spread_kernel(plan, whole_ref, early_ref, all_ref, out_ref, held, sems):
    def copy(n):
        source, index, place, _ = plan[n]
        ref = (all_ref if source else early_ref).at[:, index, :, place : place + TILE]
        return pltpu.make_async_copy(ref, held.at[n % SLOTS], sems.at[n % SLOTS])

    for n in range(SLOTS):
        copy(n).start()
    total = [None, None]
    for n, (_, index, _, column) in enumerate(plan):
        copy(n).wait()
        rows = held[n % SLOTS].reshape(-1, TILE)
        part = times(whole_ref[:, column : column + TILE], rows)
        total[index] = part if total[index] is None else total[index] + part
        if n + SLOTS < len(plan):
            copy(n + SLOTS).start()
    for index in range(2):
        out_ref[index] = total[index]


def spread(whole, early, everything):
    few, width = whole.shape
    lines, _, share, wide = early.shape
    plan = [(0, 0, place, place) for place in range(0, wide, TILE)]
    plan += [(1, 0, place, place) for place in range(wide, width, TILE)]
    plan += [(1, 1, place, place) for place in range(0, width, TILE)]
    count = 2 * lines * share * width
    return pl.pallas_call(
        functools.partial(spread_kernel, plan),
        out_shape=jax.ShapeDtypeStruct((2, few, lines * share), jnp.float32),
        in_specs=[
            pl.BlockSpec(memory_space=pltpu.VMEM),
            pl.BlockSpec(memory_space=pl.ANY),
            pl.BlockSpec(memory_space=pl.ANY),
        ],
        out_specs=pl.BlockSpec(memory_space=pltpu.VMEM),
        scratch_shapes=[
            pltpu.VMEM((SLOTS, lines, share, TILE), jnp.bfloat16),
            pltpu.SemaphoreType.DMA((SLOTS,)),
        ],
        compiler_params=pltpu.CompilerParams(vmem_limit_bytes=60 * 2**20),
        cost_estimate=pl.CostEstimate(
            flops=2 * few * count, bytes_accessed=2 * count, transcendentals=0
        ),
    )(whole, early, everything)


def body(factor, loads):
    xs, cores = lax.axis_size("x"), lax.axis_size("c")
    stored, given = factor[:, 0], loads[:, 0]
    share, width = stored.shape[1:]
    cases = given.shape[2]
    block = share * lax.axis_size(RHS)
    steps = width // block
    few = cases // (xs * cores)
    pair = cores * share

    wide = 3 * block
    early = lax.all_gather(factor[:1, 0, :, :wide], ("x", "c"), axis=0)
    everything = lax.all_gather(stored, ("x", "c"), axis=0)

    def panel(row, column):
        if column * block < wide:
            source = early[:, 0, :, column * block : (column + 1) * block]
        else:
            source = everything[:, 0, :, column * block : (column + 1) * block]
        return source.reshape(xs, pair, block)[row:].reshape(-1, block)

    together = lax.all_gather(given[0], "c", axis=0, tiled=True).T
    mine = lax.dynamic_index_in_dim(
        together.reshape(xs, cores, few, pair), lax.axis_index("c"), 1, False
    )
    mine = mine.reshape(xs * few, pair)
    start = lax.all_gather(stored[0, :, :block], "c", axis=0, tiled=True)
    whole = gather_chips(mine)
    first = times_exact(whole, start)
    first = jnp.where(lax.axis_index("x") == 0, first, mine)
    state = exchange(first.reshape(xs, few, pair), "x")

    solved, sent = [state[0]], [state[0].astype(jnp.bfloat16)]
    state = state[1:]
    for step in range(1, steps):
        whole = gather_chips(sent[-1])
        update = times(whole, panel(step, step - 1))
        update = update.reshape(few, steps - step, pair)
        state = state - jnp.swapaxes(update, 0, 1)
        solved.append(times_exact(gather_chips(state[0]), panel(step, step)[:pair]))
        sent.append(solved[-1].astype(jnp.bfloat16))
        state = state[1:]

    shared = jnp.concatenate(sent, 0)
    shared = exchange(repeat(shared, lax.axis_size("yl")), "yl")[0]
    got = exchange(repeat(shared, lax.axis_size(CHIPS)), CHIPS)
    got = got.reshape(-1, steps, few, pair)
    whole = got.transpose(2, 1, 0, 3).reshape(few, width)
    update = spread(whole, early, everything)
    upper, lower = jnp.swapaxes(update.reshape(2, few, xs, pair), 1, 2)
    owner = lax.axis_index("yl") == 0
    upper = jnp.where(owner, jnp.stack(solved), upper)
    both = jnp.stack([upper, lower], 1)[:, None]
    both = jnp.broadcast_to(both, (xs, cores) + both.shape[2:])
    both = both.reshape((xs * cores,) + both.shape[2:])
    back = exchange(both, ("x", "c"))
    back = jnp.swapaxes(back, 0, 1).reshape(2, cases, pair).transpose(0, 2, 1)
    back = lax.dynamic_slice_in_dim(back, lax.axis_index("c") * share, share, 1)
    top = jnp.where(owner, back[0], given[0] - back[0])
    return jnp.stack([top, given[1] - back[1]])[:, None]


def solution(mesh):
    fine = Mesh(mesh.devices.reshape(4, 4, 8, 2, 2), BLK + RHS)
    spec = P(None, BLK, RHS, None)
    return jax.shard_map(
        body, mesh=fine, in_specs=(spec, spec), out_specs=spec, check_vma=False
    )
```

time: 223 us -> 220 us (0.987)
  blocking collectives: 122 us -> 92.1 us
  waiting for transfers between devices: 26.4 us -> 52.4 us
  matrix products: 19.7 us -> 2.36 us
  Pallas kernels: 0 us -> 8.18 us
  local copies, waits for them, and re-layouts: 10.8 us -> 15.7 us
  starting transfers between devices: 29 us -> 33.9 us
    all_to_all x8 -> x6, blocking collectives: 111 us -> 80.9 us  [exchange(): return lax.all_to_all(parts, axis, 0, 0, tiled=True)]
    all_to_all x3 -> x5, waiting for transfers between devices: 25.6 us -> 48.8 us  [exchange(): return lax.all_to_all(parts, axis, 0, 0, tiled=True)]
    dot_general x10 -> x7, matrix products: 19.7 us -> 2.36 us  [times(): lax.dot_general(values, rows, (((1,), (1,)), ((), ())), preferred_element...]
    pallas_call x0 -> x1, Pallas kernels: none -> 8.18 us  [spread(): pl.pallas_call(functools.partial(spread_kernel, plan), out_shape=jax.Shap...]
    slice x5, local copies, waits for them, and re-layouts: 2.41 us -> 7.89 us  [the longest x3 4.08 us: panel(): return source.reshape(xs, pair, block)[row:].reshape(-1, block)]
    all_to_all x3 -> x5, starting transfers between devices: 28.9 us -> 33.8 us  [exchange(): return lax.all_to_all(parts, axis, 0, 0, tiled=True)]
    all_gather x3 -> x2, waiting for transfers between devices: 0.06 us -> 2.88 us  [the longest x1 2.86 us: body(): everything = lax.all_gather(stored, ('x', 'c'), axis=0)]
  transfers between devices with their start and end apart: 6 -> 7, of which waited for: 3 -> 6; matrix products, arithmetic and copies ran while one was open for 10% -> 5% of each run, Pallas kernels for 0% -> 0%
where the time goes in v5:
time: 220 us; the launch traced here: 219 us
  blocking collectives  92.1 us (42%)
  waiting for transfers between devices  52.4 us (24%)
  starting transfers between devices  33.9 us (15%)
  local copies, waits for them, and re-layouts  15.7 us (7%)
  between operations  13.7 us (6%)
  Pallas kernels  8.18 us (4%)
  matrix products  2.36 us (1%)
    all_to_all x6, blocking collectives, exchange(): return lax.all_to_all(parts, axis, 0, 0, tiled=True)  80.9 us
    all_to_all x5, waiting for transfers between devices, exchange(): return lax.all_to_all(parts, axis, 0, 0, tiled=True)  48.8 us
    all_to_all x5, starting transfers between devices, exchange(): return lax.all_to_all(parts, axis, 0, 0, tiled=True)  33.8 us
    all_gather x1, blocking collectives, body(): together = lax.all_gather(given[0], 'c', axis=0, tiled=True).T  8.37 us
    pallas_call x1, Pallas kernels, spread(): pl.pallas_call(functools.partial(spread_kernel, plan), out_shape=jax.Shap...  8.18 us
  transfers between devices with their start and end apart: 7, of which 6 were waited for; matrix products, arithmetic and copies ran while one was open for 5% of the time, Pallas kernels for 0%

profile of v5, /device:TPU:1, one launch (start us, length us, event | category | flops | bytes accessed | tf_op | source)
XLA Modules:
  0.0 218.6 jit_solution(591359632138436318)
XLA Ops:
  6.5 2.1 slice.94
  8.7 0.7 all-gather.8.cloned.1.call-update
  9.5 8.4 %all-gather = f32[1,1,128,128]{3,1,0,2:T(1,128)S(1)} all-gather(f32[1,1,64,128]{3,1,0,2:T(1,128)S(1)} %bitcast.163), channel_id=2, replica_groups=mesh['yl'=4,'x'=4,'z'=8,'yh'=2,'c'=2] {'c'}, dimensions={2}, use_global_device_ids=true | all-gather | bytes 98304 | tf_op jit(solution)/shard_map/all_gather | solution.py:115
  17.8 0.1 copy.16
  17.9 0.8 broadcast_in_dim.35
  18.8 10.0 %all-to-all-start = ((f32[16,64,128]{2,1,0:T(8,128)}), f32[16,64,128]{2,1,0:T(8,128)S(1)}, u32[]{:S(2)}, u32[]{:S(2)}) async-start(f32[16,64,128]{2,1,0:T(8,128)} %broadcast_in_dim.35), calls=%async_computation | async-start | bytes 1048576 | tf_op jit(solution)/shard_map/all_to_all | solution.py:16
  28.8 1.0 slice.111
  29.8 2.8 %all-gather.1 = bf16[1,128,2048]{2,1,0:T(8,128)(2,1)S(1)} all-gather(bf16[1,64,2048]{2,1,0:T(8,128)(2,1)S(1)} %slice.111), channel_id=3, replica_groups=mesh['yl'=4,'x'=4,'z'=8,'yh'=2,'c'=2] {'c'}, dimensions={1}, use_global_device_ids=true | all-gather | bytes 786432 | tf_op jit(solution)/shard_map/all_gather | solution.py:120
  32.6 11.2 %all-to-all-done = f32[16,64,128]{2,1,0:T(8,128)S(1)} async-done(((f32[16,64,128]{2,1,0:T(8,128)}), f32[16,64,128]{2,1,0:T(8,128)S(1)}, u32[]{:S(2)}, u32[]{:S(2)}) %all-to-all-start) | async-done | bytes 524320 | tf_op jit(solution)/shard_map/all_to_all | solution.py:16
  43.8 0.1 reduce-precision_convert_fusion.1
  43.9 0.4 fusion.4
  44.3 8.5 %all_to_all.55 = f32[4,16,128]{2,1,0:T(8,128)S(1)} all-to-all(f32[4,16,128]{2,1,0:T(8,128)S(1)} %bitcast.167), channel_id=1, replica_groups=mesh['yl'=4,'x'=4,'z'=8,'yh'=2,'c'=2] {'x'}, dimensions={0} | all-to-all | bytes 65536 | tf_op jit(solution)/shard_map/all_to_all | solution.py:16
  52.8 20.7 %all_to_all.56 = bf16[16,16,128]{2,1,0:T(8,128)(2,1)S(1)} all-to-all(bf16[16,16,128]{2,1,0:T(8,128)(2,1)S(1)} %broadcast_in_dim.73), channel_id=1, replica_groups=mesh['yl'=4,'x'=4,'z'=8,'yh'=2,'c'=2] {'z','yh'}, dimensions={0} | all-to-all | bytes 131072 | tf_op jit(solution)/shard_map/all_to_all | solution.py:16
  73.6 1.5 slice.114
  75.1 0.5 fusion
  75.6 0.7 broadcast_in_dim.75
  76.3 3.5 %all-to-all-start.3 = ((f32[16,16,128]{2,1,0:T(8,128)}), f32[16,16,128]{2,1,0:T(8,128)S(1)}, u32[]{:S(2)}, u32[]{:S(2)}) async-start(f32[16,16,128]{2,1,0:T(8,128)} %broadcast_in_dim.75), calls=%async_computation.3 | async-start | bytes 262144 | tf_op jit(solution)/shard_map/all_to_all | solution.py:16
  79.8 1.7 fusion.48
  81.6 10.0 %all-to-all-done.3 = f32[16,16,128]{2,1,0:T(8,128)S(1)} async-done(((f32[16,16,128]{2,1,0:T(8,128)}), f32[16,16,128]{2,1,0:T(8,128)S(1)}, u32[]{:S(2)}, u32[]{:S(2)}) %all-to-all-start.3) | async-done | bytes 131104 | tf_op jit(solution)/shard_map/all_to_all | solution.py:16
  91.7 0.3 fusion.12
  92.0 0.6 broadcast_in_dim.76
  92.6 3.5 %all-to-all-start.4 = ((bf16[16,16,128]{2,1,0:T(8,128)(2,1)}), bf16[16,16,128]{2,1,0:T(8,128)(2,1)S(1)}, u32[]{:S(2)}, u32[]{:S(2)}) async-start(bf16[16,16,128]{2,1,0:T(8,128)(2,1)} %broadcast_in_dim.76), calls=%async_computation.4 | async-start | bytes 131072 | tf_op jit(solution)/shard_map/all_to_all | solution.py:16
  96.1 1.5 slice.118
  97.6 10.0 %all-to-all-done.4 = bf16[16,16,128]{2,1,0:T(8,128)(2,1)S(1)} async-done(((bf16[16,16,128]{2,1,0:T(8,128)(2,1)}), bf16[16,16,128]{2,1,0:T(8,128)(2,1)S(1)}, u32[]{:S(2)}, u32[]{:S(2)}) %all-to-all-start.4) | async-done | bytes 65568 | tf_op jit(solution)/shard_map/all_to_all | solution.py:16
  107.6 0.4 fusion.1
  108.1 14.4 %all_to_all.57 = f32[16,16,128]{2,1,0:T(8,128)S(1)} all-to-all(f32[16,16,128]{2,1,0:T(8,128)S(1)} %broadcast_in_dim.78), channel_id=1, replica_groups=mesh['yl'=4,'x'=4,'z'=8,'yh'=2,'c'=2] {'z','yh'}, dimensions={0} | all-to-all | bytes 262144 | tf_op jit(solution)/shard_map/all_to_all | solution.py:16
  122.5 0.3 fusion.18
  122.8 14.2 %all_to_all.58 = bf16[16,16,128]{2,1,0:T(8,128)(2,1)S(1)} all-to-all(bf16[16,16,128]{2,1,0:T(8,128)(2,1)S(1)} %broadcast_in_dim.79), channel_id=1, replica_groups=mesh['yl'=4,'x'=4,'z'=8,'yh'=2,'c'=2] {'z','yh'}, dimensions={0} | all-to-all | bytes 131072 | tf_op jit(solution)/shard_map/all_to_all | solution.py:16
  137.0 0.2 fusion.3
  137.3 14.4 %all_to_all.59 = f32[16,16,128]{2,1,0:T(8,128)S(1)} all-to-all(f32[16,16,128]{2,1,0:T(8,128)S(1)} %broadcast_in_dim.81), channel_id=1, replica_groups=mesh['yl'=4,'x'=4,'z'=8,'yh'=2,'c'=2] {'z','yh'}, dimensions={0} | all-to-all | bytes 262144 | tf_op jit(solution)/shard_map/all_to_all | solution.py:16
  151.7 2.9 %all-gather.8.cloned.1.call-done = bf16[16,1,64,8192]{3,2,1,0:T(8,128)(2,1)} async-done(((bf16[2,1,64,8192]{3,2,1,0:T(8,128)(2,1)}), bf16[16,1,64,8192]{3,2,1,0:T(8,128)(2,1)}) %all-gather.8.cloned.1.call-update) | async-done | bytes 16777232 | tf_op jit(solution)/shard_map/all_gather | solution.py:106
  154.6 1.1 slice.123
  155.7 0.3 fusion.24
  156.0 8.7 %all_to_all.60 = bf16[4,64,128]{2,1,0:T(8,128)(2,1)S(1)} all-to-all(bf16[4,64,128]{2,1,0:T(8,128)(2,1)S(1)} %broadcast_in_dim.82), channel_id=1, replica_groups=mesh['yl'=4,'x'=4,'z'=8,'yh'=2,'c'=2] {'yl'}, dimensions={0} | all-to-all | bytes 131072 | tf_op jit(solution)/shard_map/all_to_all | solution.py:16
  164.7 0.8 broadcast_in_dim.84
  165.5 10.4 %all-to-all-start.9 = ((bf16[16,64,128]{2,1,0:T(8,128)(2,1)}), bf16[16,64,128]{2,1,0:T(8,128)(2,1)S(1)}, u32[]{:S(2)}, u32[]{:S(2)}) async-start(bf16[16,64,128]{2,1,0:T(8,128)(2,1)} %broadcast_in_dim.84), calls=%async_computation.9 | async-start | bytes 524288 | tf_op jit(solution)/shard_map/all_to_all | solution.py:16
  176.0 12.5 %all-to-all-done.9 = bf16[16,64,128]{2,1,0:T(8,128)(2,1)S(1)} async-done(((bf16[16,64,128]{2,1,0:T(8,128)(2,1)}), bf16[16,64,128]{2,1,0:T(8,128)(2,1)S(1)}, u32[]{:S(2)}, u32[]{:S(2)}) %all-to-all-start.9) | async-done | bytes 262176 | tf_op jit(solution)/shard_map/all_to_all | solution.py:16
  188.5 0.2 copy.24
  188.7 0.9 copy.70
  189.6 8.2 %shard_map.28 = f32[2,16,512]{2,1,0:T(8,128)} custom-call(bf16[16,8192]{1,0:T(8,128)(2,1)} %bitcast.155, bf16[8,1,64,6144]{3,2,1,0:T(8,128)(2,1)} %all-gather.6.cloned.1.call-done.early_ref, bf16[8,2,64,8192]{3,2,1,0:T(8,128)(2,1)} %bitcast.150), custom_call_target="tpu_custom_call" | custom-call | flops 268435456 | bytes 16777216 | tf_op jit(solution)/shard_map/pallas_call | solution.py:74
  197.8 0.8 bitcast_bitcast_fusion
  198.7 0.7 broadcast_in_dim.85
  199.3 6.3 %all-to-all-start.10 = ((f32[8,2,16,128]{3,2,1,0:T(8,128)}), f32[8,2,16,128]{3,2,1,0:T(8,128)S(1)}, u32[]{:S(2)}, u32[]{:S(2)}) async-start(f32[8,2,16,128]{3,2,1,0:T(8,128)} %bitcast.39), calls=%async_computation.10 | async-start | bytes 262144 | tf_op jit(solution)/shard_map/all_to_all | solution.py:16
  205.6 0.1 copy.30
  205.7 0.1 copy.31
  205.8 5.1 %all-to-all-done.10 = f32[8,2,16,128]{3,2,1,0:T(8,128)S(1)} async-done(((f32[8,2,16,128]{3,2,1,0:T(8,128)}), f32[8,2,16,128]{3,2,1,0:T(8,128)S(1)}, u32[]{:S(2)}, u32[]{:S(2)}) %all-to-all-start.10) | async-done | bytes 131104 | tf_op jit(solution)/shard_map/all_to_all | solution.py:16
  210.9 0.1 dynamic-slice_bitcast_fusion
  211.1 0.7 copy.29
  (36 shorter events, 0.5 us)
Async XLA Ops:
  6.5 67.1 %all-gather.6.cloned.1.call-start = ((), (), s32[]{:S(2)}) async-start(), calls=%async_computation.11 | async-start | bytes 7077888 | tf_op jit(solution)/shard_map/all_gather | solution.py:105
  8.6 0.8 copy-start
  8.6 146.0 %all-gather.8.cloned.1.call-start = ((), (), s32[]{:S(2)}) async-start(), calls=%async_computation.12 | async-start | bytes 18874368 | tf_op jit(solution)/shard_map/all_gather | solution.py:106
  18.8 25.0 %all-to-all-start = ((f32[16,64,128]{2,1,0:T(8,128)}), f32[16,64,128]{2,1,0:T(8,128)S(1)}, u32[]{:S(2)}, u32[]{:S(2)}) async-start(f32[16,64,128]{2,1,0:T(8,128)} %broadcast_in_dim.35), calls=%async_computation | async-start | bytes 1048576 | tf_op jit(solution)/shard_map/all_to_all | solution.py:16
  76.3 15.3 %all-to-all-start.3 = ((f32[16,16,128]{2,1,0:T(8,128)}), f32[16,16,128]{2,1,0:T(8,128)S(1)}, u32[]{:S(2)}, u32[]{:S(2)}) async-start(f32[16,16,128]{2,1,0:T(8,128)} %broadcast_in_dim.75), calls=%async_computation.3 | async-start | bytes 262144 | tf_op jit(solution)/shard_map/all_to_all | solution.py:16
  92.6 15.0 %all-to-all-start.4 = ((bf16[16,16,128]{2,1,0:T(8,128)(2,1)}), bf16[16,16,128]{2,1,0:T(8,128)(2,1)S(1)}, u32[]{:S(2)}, u32[]{:S(2)}) async-start(bf16[16,16,128]{2,1,0:T(8,128)(2,1)} %broadcast_in_dim.76), calls=%async_computation.4 | async-start | bytes 131072 | tf_op jit(solution)/shard_map/all_to_all | solution.py:16
  165.5 23.0 %all-to-all-start.9 = ((bf16[16,64,128]{2,1,0:T(8,128)(2,1)}), bf16[16,64,128]{2,1,0:T(8,128)(2,1)S(1)}, u32[]{:S(2)}, u32[]{:S(2)}) async-start(bf16[16,64,128]{2,1,0:T(8,128)(2,1)} %broadcast_in_dim.84), calls=%async_computation.9 | async-start | bytes 524288 | tf_op jit(solution)/shard_map/all_to_all | solution.py:16
  199.3 11.6 %all-to-all-start.10 = ((f32[8,2,16,128]{3,2,1,0:T(8,128)}), f32[8,2,16,128]{3,2,1,0:T(8,128)S(1)}, u32[]{:S(2)}, u32[]{:S(2)}) async-start(f32[8,2,16,128]{3,2,1,0:T(8,128)} %bitcast.39), calls=%async_computation.10 | async-start | bytes 262144 | tf_op jit(solution)/shard_map/all_to_all | solution.py:16
Sparse Core Ops, SparseCore 0:
  9.5 52.4 all-gather.5
  64.2 90.4 all-gather.7

commit v6 on v5

v6 whole, which is shorter than its diff:
```python
import functools

import jax
import jax.numpy as jnp
from jax import lax
from jax.experimental import pallas as pl
from jax.experimental.pallas import tpu as pltpu
from jax.sharding import Mesh, PartitionSpec as P

BLK = ("yl", "x")
RHS = ("z", "yh", "c")
CHIPS = ("z", "yh")


def exchange(parts, axis):
    return lax.all_to_all(parts, axis, 0, 0, tiled=True)


def repeat(part, count):
    return jnp.broadcast_to(part[None], (count,) + part.shape)


def gather_chips(part):
    got = exchange(repeat(part, lax.axis_size(CHIPS)), CHIPS)
    return jnp.swapaxes(got, 0, 1).reshape(part.shape[0], -1)


def times(values, rows):
    return lax.dot_general(
        values, rows, (((1,), (1,)), ((), ())), preferred_element_type=jnp.float32
    )


def times_exact(values, rows):
    first = lax.reduce_precision(values, 8, 7)
    rest = values - first
    second = lax.reduce_precision(rest, 8, 7)
    third = rest - second
    terms = jnp.concatenate([first, second, third], 0).astype(jnp.bfloat16)
    a, b, c = jnp.split(times(terms, rows), 3, 0)
    return (c + b) + a


TILE, SLOTS = 1024, 6


def stream(plan, early_ref, late_ref, held, sems, cases_of):
    def copy(n):
        index, place = plan[n]
        ref = (late_ref if index else early_ref).at[:, :, place : place + TILE]
        return pltpu.make_async_copy(ref, held.at[n % SLOTS], sems.at[n % SLOTS])

    for n in range(min(SLOTS, len(plan))):
        copy(n).start()
    total = [None, None]
    for n, (index, place) in enumerate(plan):
        copy(n).wait()
        part = times(cases_of(place), held[n % SLOTS].reshape(-1, TILE))
        total[index] = part if total[index] is None else total[index] + part
        if n + SLOTS < len(plan):
            copy(n + SLOTS).start()
    return total


def first_kernel(plan, *refs):
    *whole, early_ref, late_ref, out_ref, held, sems = refs
    block = whole[0].shape[1]

    def cases_of(place):
        start = place % block
        return whole[place // block][:, start : start + TILE]

    total = stream(plan, early_ref, late_ref, held, sems, cases_of)
    for index in range(2):
        out_ref[index] = total[index]


def last_kernel(plan, owner_ref, got, sofar, solved, early_ref, late_ref, out, held, sems):
    pair = got.shape[2]
    xs = solved.shape[0]

    def cases_of(place):
        chip = (place - plan[0][1]) // pair
        return jnp.concatenate([got[chip + n] for n in range(TILE // pair)], 1)

    total = stream(plan, early_ref, late_ref, held, sems, cases_of)
    owner = owner_ref[0] == 0
    for x in range(xs):
        for index in range(2):
            span = slice(x * pair, (x + 1) * pair)
            value = sofar[index, :, span] + total[index][:, span]
            if index == 0:
                value = jnp.where(owner, solved[x], value)
            for core in range(out.shape[0] // xs):
                out[x * (out.shape[0] // xs) + core, index] = value


def streaming(kernel, plan, early, out_shape, spaces):
    lines, share, _ = early.shape
    count = len(plan) * lines * share * TILE
    few = out_shape[-2]
    return pl.pallas_call(
        functools.partial(kernel, plan),
        out_shape=jax.ShapeDtypeStruct(out_shape, jnp.float32),
        in_specs=[pl.BlockSpec(memory_space=space) for space in spaces],
        out_specs=pl.BlockSpec(memory_space=pltpu.VMEM),
        scratch_shapes=[
            pltpu.VMEM((SLOTS, lines, share, TILE), jnp.bfloat16),
            pltpu.SemaphoreType.DMA((SLOTS,)),
        ],
        compiler_params=pltpu.CompilerParams(vmem_limit_bytes=60 * 2**20),
        cost_estimate=pl.CostEstimate(
            flops=2 * few * count, bytes_accessed=2 * count, transcendentals=0
        ),
    )


def body(factor, loads):
    xs, cores = lax.axis_size("x"), lax.axis_size("c")
    stored, given = factor[:, 0], loads[:, 0]
    share, width = stored.shape[1:]
    cases = given.shape[2]
    block = share * lax.axis_size(RHS)
    steps = width // block
    few = cases // (xs * cores)
    pair = cores * share

    early = lax.all_gather(stored[0], ("x", "c"), axis=0)
    late = lax.all_gather(stored[1], ("x", "c"), axis=0)

    def panel(row, column):
        part = early[:, :, column * block : (column + 1) * block]
        return part.reshape(xs, pair, block)[row:].reshape(-1, block)

    def to_all(part):
        planes = ("yl",) + CHIPS
        got = exchange(repeat(part, lax.axis_size(planes)), planes)
        return got[: lax.axis_size(CHIPS)]

    together = lax.all_gather(given[0], "c", axis=0, tiled=True).T
    mine = lax.dynamic_index_in_dim(
        together.reshape(xs, cores, few, pair), lax.axis_index("c"), 1, False
    )
    mine = mine.reshape(xs * few, pair)
    start = lax.all_gather(stored[0, :, :block], "c", axis=0, tiled=True)
    whole = gather_chips(mine)
    first = times_exact(whole, start)
    first = jnp.where(lax.axis_index("x") == 0, first, mine)
    state = exchange(first.reshape(xs, few, pair), "x")

    solved, known = [state[0]], []
    state = state[1:]
    for step in range(1, steps):
        got = to_all(solved[-1].astype(jnp.bfloat16))
        known.append(jnp.swapaxes(got, 0, 1).reshape(few, block))
        update = times(known[-1], panel(step, step - 1))
        update = update.reshape(few, steps - step, pair)
        state = state - jnp.swapaxes(update, 0, 1)
        solved.append(times_exact(gather_chips(state[0]), panel(step, step)[:pair]))
        state = state[1:]

    got = to_all(solved[-1].astype(jnp.bfloat16))
    plan = [
        [(index, place) for place in range(*span, TILE) for index in range(2)]
        for span in ((0, width - block), (width - block, width))
    ]
    sofar = streaming(
        first_kernel,
        plan[0],
        early,
        (2, few, xs * pair),
        [pltpu.VMEM] * len(known) + [pl.ANY] * 2,
    )(*known, early, late)
    both = streaming(
        last_kernel,
        plan[1],
        early,
        (xs * cores, 2, few, pair),
        [pltpu.SMEM] + [pltpu.VMEM] * 3 + [pl.ANY] * 2,
    )(lax.axis_index("yl")[None], got, sofar, jnp.stack(solved), early, late)
    back = exchange(both, ("x", "c"))
    owner = lax.axis_index("yl") == 0
    back = jnp.swapaxes(back, 0, 1).reshape(2, cases, pair).transpose(0, 2, 1)
    back = lax.dynamic_slice_in_dim(back, lax.axis_index("c") * share, share, 1)
    top = jnp.where(owner, back[0], given[0] - back[0])
    return jnp.stack([top, given[1] - back[1]])[:, None]


def solution(mesh):
    fine = Mesh(mesh.devices.reshape(4, 4, 8, 2, 2), BLK + RHS)
    spec = P(None, BLK, RHS, None)
    return jax.shard_map(
        body, mesh=fine, in_specs=(spec, spec), out_specs=spec, check_vma=False
    )
```

time: 220 us -> 216 us (0.982)
  blocking collectives: 92.1 us -> 75.8 us
  starting transfers between devices: 33.9 us -> 41.2 us
  Pallas kernels: 8.18 us -> 11.7 us
    all_to_all x6 -> x4, blocking collectives: 80.9 us -> 64.6 us  [exchange(): return lax.all_to_all(parts, axis, 0, 0, tiled=True)]
    all_to_all x5 -> x6, starting transfers between devices: 33.8 us -> 41.2 us  [exchange(): return lax.all_to_all(parts, axis, 0, 0, tiled=True)]
    pallas_call x1 -> x2, Pallas kernels: 8.18 us -> 11.7 us  [the longest x1 6.98 us: body(): streaming(first_kernel, plan[0], early, (2, few, xs * pair), [pltpu.VMEM]...]
    all_to_all x5 -> x6, waiting for transfers between devices: 48.8 us -> 52.3 us  [exchange(): return lax.all_to_all(parts, axis, 0, 0, tiled=True)]
    all_gather x2, waiting for transfers between devices: 2.88 us -> 0.02 us  [the longest x1 0.02 us: body(): early = lax.all_gather(stored[0], ('x', 'c'), axis=0)]
    slice x4 -> x6, local copies, waits for them, and re-layouts: 6.15 us -> 6.52 us  [the longest x1 3.07 us: body(): late = lax.all_gather(stored[1], ('x', 'c'), axis=0)]
  transfers between devices with their start and end apart: 7 -> 8, of which waited for: 6 -> 6; matrix products, arithmetic and copies ran while one was open for 5% -> 7% of each run, Pallas kernels for 0% -> 3%
where the time goes in v6:
time: 216 us; the launch traced here: 215 us
  blocking collectives  75.8 us (35%)
  waiting for transfers between devices  53 us (25%)
  starting transfers between devices  41.2 us (19%)
  local copies, waits for them, and re-layouts  16.3 us (8%)
  between operations  13.7 us (6%)
  Pallas kernels  11.7 us (5%)
  matrix products  2.36 us (1%)
    all_to_all x4, blocking collectives, exchange(): return lax.all_to_all(parts, axis, 0, 0, tiled=True)  64.6 us
    all_to_all x6, waiting for transfers between devices, exchange(): return lax.all_to_all(parts, axis, 0, 0, tiled=True)  52.3 us
    all_to_all x6, starting transfers between devices, exchange(): return lax.all_to_all(parts, axis, 0, 0, tiled=True)  41.2 us
    all_gather x1, blocking collectives, body(): together = lax.all_gather(given[0], 'c', axis=0, tiled=True).T  8.37 us
    pallas_call x1, Pallas kernels, body(): streaming(first_kernel, plan[0], early, (2, few, xs * pair), [pltpu.VMEM]...  6.98 us
    pallas_call x1, Pallas kernels, body(): streaming(last_kernel, plan[1], early, (xs * cores, 2, few, pair), [pltpu...  4.75 us
  transfers between devices with their start and end apart: 8, of which 6 were waited for; matrix products, arithmetic and copies ran while one was open for 7% of the time, Pallas kernels for 3%

profile of v6, /device:TPU:1, one launch (start us, length us, event | category | flops | bytes accessed | tf_op | source)
XLA Modules:
  0.0 215.0 jit_solution(10693261117160331996)
XLA Ops:
  6.5 3.1 %fusion.45 = (bf16[1,1,64,8192]{3,2,1,0:T(8,128)(2,1)}, bf16[1,1,64,8192]{3,2,1,0:T(8,128)(2,1)}) fusion(bf16[2,1,64,8192]{3,2,1,0:T(8,128)(2,1)} %param.2), kind=kLoop, calls=%fused_computation.89 | loop fusion | bytes 4194304 | tf_op jit(solution)/shard_map/slice | solution.py:129
  9.7 0.7 all-gather.9.cloned.1.call-update
  10.5 8.4 %all-gather = f32[1,1,128,128]{3,1,0,2:T(1,128)S(1)} all-gather(f32[1,1,64,128]{3,1,0,2:T(1,128)S(1)} %bitcast.152), channel_id=2, replica_groups=mesh['yl'=4,'x'=4,'z'=8,'yh'=2,'c'=2] {'c'}, dimensions={2}, use_global_device_ids=true | all-gather | bytes 98304 | tf_op jit(solution)/shard_map/all_gather | solution.py:140
  18.9 0.9 broadcast_in_dim.62
  19.8 10.0 %all-to-all-start = ((f32[16,64,128]{2,1,0:T(8,128)}), f32[16,64,128]{2,1,0:T(8,128)S(1)}, u32[]{:S(2)}, u32[]{:S(2)}) async-start(f32[16,64,128]{2,1,0:T(8,128)} %broadcast_in_dim.62), calls=%async_computation | async-start | bytes 1048576 | tf_op jit(solution)/shard_map/all_to_all | solution.py:16
  29.8 1.0 slice.134
  30.8 2.8 %all-gather.1 = bf16[1,128,2048]{2,1,0:T(8,128)(2,1)S(1)} all-gather(bf16[1,64,2048]{2,1,0:T(8,128)(2,1)S(1)} %slice.134), channel_id=3, replica_groups=mesh['yl'=4,'x'=4,'z'=8,'yh'=2,'c'=2] {'c'}, dimensions={1}, use_global_device_ids=true | all-gather | bytes 786432 | tf_op jit(solution)/shard_map/all_gather | solution.py:145
  33.7 11.1 %all-to-all-done = f32[16,64,128]{2,1,0:T(8,128)S(1)} async-done(((f32[16,64,128]{2,1,0:T(8,128)}), f32[16,64,128]{2,1,0:T(8,128)S(1)}, u32[]{:S(2)}, u32[]{:S(2)}) %all-to-all-start) | async-done | bytes 524320 | tf_op jit(solution)/shard_map/all_to_all | solution.py:16
  44.8 0.1 reduce-precision_convert_fusion.1
  44.9 0.4 fusion.4
  45.3 8.5 %all_to_all.50 = f32[4,16,128]{2,1,0:T(8,128)S(1)} all-to-all(f32[4,16,128]{2,1,0:T(8,128)S(1)} %bitcast.156), channel_id=1, replica_groups=mesh['yl'=4,'x'=4,'z'=8,'yh'=2,'c'=2] {'x'}, dimensions={0} | all-to-all | bytes 65536 | tf_op jit(solution)/shard_map/all_to_all | solution.py:16
  53.9 23.9 %all_to_all.51 = bf16[64,16,128]{2,1,0:T(8,128)(2,1)S(1)} all-to-all(bf16[64,16,128]{2,1,0:T(8,128)(2,1)S(1)} %broadcast_in_dim.64), channel_id=1, replica_groups=mesh['yl'=4,'x'=4,'z'=8,'yh'=2,'c'=2] {'yl','z','yh'}, dimensions={0} | all-to-all | bytes 524288 | tf_op jit(solution)/shard_map/all_to_all | solution.py:16
  77.9 1.5 slice.138
  79.4 0.5 fusion
  79.9 0.7 broadcast_in_dim.66
  80.6 5.3 %all-to-all-start.3 = ((f32[16,16,128]{2,1,0:T(8,128)}), f32[16,16,128]{2,1,0:T(8,128)S(1)}, u32[]{:S(2)}, u32[]{:S(2)}) async-start(f32[16,16,128]{2,1,0:T(8,128)} %broadcast_in_dim.66), calls=%async_computation.3 | async-start | bytes 262144 | tf_op jit(solution)/shard_map/all_to_all | solution.py:16
  85.9 1.8 fusion.44
  87.7 10.1 %all-to-all-done.3 = f32[16,16,128]{2,1,0:T(8,128)S(1)} async-done(((f32[16,16,128]{2,1,0:T(8,128)}), f32[16,16,128]{2,1,0:T(8,128)S(1)}, u32[]{:S(2)}, u32[]{:S(2)}) %all-to-all-start.3) | async-done | bytes 131104 | tf_op jit(solution)/shard_map/all_to_all | solution.py:16
  97.8 0.3 fusion.12
  98.1 0.7 broadcast_in_dim.67
  98.8 4.6 %all-to-all-start.4 = ((bf16[64,16,128]{2,1,0:T(8,128)(2,1)}), bf16[64,16,128]{2,1,0:T(8,128)(2,1)S(1)}, u32[]{:S(2)}, u32[]{:S(2)}) async-start(bf16[64,16,128]{2,1,0:T(8,128)(2,1)} %broadcast_in_dim.67), calls=%async_computation.4 | async-start | bytes 524288 | tf_op jit(solution)/shard_map/all_to_all | solution.py:16
  103.4 1.3 slice.143
  104.7 11.3 %all-to-all-done.4 = bf16[64,16,128]{2,1,0:T(8,128)(2,1)S(1)} async-done(((bf16[64,16,128]{2,1,0:T(8,128)(2,1)}), bf16[64,16,128]{2,1,0:T(8,128)(2,1)S(1)}, u32[]{:S(2)}, u32[]{:S(2)}) %all-to-all-start.4) | async-done | bytes 262176 | tf_op jit(solution)/shard_map/all_to_all | solution.py:16
  116.2 0.4 fusion.1
  116.6 14.6 %all_to_all.52 = f32[16,16,128]{2,1,0:T(8,128)S(1)} all-to-all(f32[16,16,128]{2,1,0:T(8,128)S(1)} %broadcast_in_dim.69), channel_id=1, replica_groups=mesh['yl'=4,'x'=4,'z'=8,'yh'=2,'c'=2] {'z','yh'}, dimensions={0} | all-to-all | bytes 262144 | tf_op jit(solution)/shard_map/all_to_all | solution.py:16
  131.2 0.3 fusion.18
  131.5 17.7 %all_to_all.53 = bf16[64,16,128]{2,1,0:T(8,128)(2,1)S(1)} all-to-all(bf16[64,16,128]{2,1,0:T(8,128)(2,1)S(1)} %broadcast_in_dim.70), channel_id=1, replica_groups=mesh['yl'=4,'x'=4,'z'=8,'yh'=2,'c'=2] {'yl','z','yh'}, dimensions={0} | all-to-all | bytes 524288 | tf_op jit(solution)/shard_map/all_to_all | solution.py:16
  149.2 0.2 fusion.3
  149.5 0.7 broadcast_in_dim.72
  150.2 3.5 %all-to-all-start.7 = ((f32[16,16,128]{2,1,0:T(8,128)}), f32[16,16,128]{2,1,0:T(8,128)S(1)}, u32[]{:S(2)}, u32[]{:S(2)}) async-start(f32[16,16,128]{2,1,0:T(8,128)} %broadcast_in_dim.72), calls=%async_computation.7 | async-start | bytes 262144 | tf_op jit(solution)/shard_map/all_to_all | solution.py:16
  153.7 0.6 copy.64
  154.3 0.6 copy.63
  155.0 10.5 %all-to-all-done.7 = f32[16,16,128]{2,1,0:T(8,128)S(1)} async-done(((f32[16,16,128]{2,1,0:T(8,128)}), f32[16,16,128]{2,1,0:T(8,128)S(1)}, u32[]{:S(2)}, u32[]{:S(2)}) %all-to-all-start.7) | async-done | bytes 131104 | tf_op jit(solution)/shard_map/all_to_all | solution.py:16
  165.5 0.3 fusion.24
  165.8 0.7 broadcast_in_dim.73
  166.5 4.6 %all-to-all-start.8 = ((bf16[64,16,128]{2,1,0:T(8,128)(2,1)}), bf16[64,16,128]{2,1,0:T(8,128)(2,1)S(1)}, u32[]{:S(2)}, u32[]{:S(2)}) async-start(bf16[64,16,128]{2,1,0:T(8,128)(2,1)} %broadcast_in_dim.73), calls=%async_computation.8 | async-start | bytes 524288 | tf_op jit(solution)/shard_map/all_to_all | solution.py:16
  171.1 0.6 copy_bitcast_fusion.2.refs_2_
  171.8 7.0 %shard_map.28.sofar = f32[2,16,512]{2,1,0:T(8,128)} custom-call(bf16[16,2048]{1,0:T(8,128)(2,1)} %bitcast.153, bf16[16,2048]{1,0:T(8,128)(2,1)} %bitcast.154, bf16[16,2048]{1,0:T(8,128)(2,1)} %copy_bitcast_fusion.2.refs_2_, bf16[8,64,8192]{2,1,0:T(8,128)(2,1)} %bitcast.138, bf16[8,64,8192]{2,1,0:T(8,128)(2,1)} %bitcast.140), custom_call_target="tpu_custom_call" | custom-call | flops 201326592 | bytes 12582912 | tf_op jit(solution)/shard_map/pallas_call | solution.py:167
  178.8 0.6 pad_maximum_fusion.solved
  179.4 4.1 %all-to-all-done.8 = bf16[64,16,128]{2,1,0:T(8,128)(2,1)S(1)} async-done(((bf16[64,16,128]{2,1,0:T(8,128)(2,1)}), bf16[64,16,128]{2,1,0:T(8,128)(2,1)S(1)}, u32[]{:S(2)}, u32[]{:S(2)}) %all-to-all-start.8) | async-done | bytes 262176 | tf_op jit(solution)/shard_map/all_to_all | solution.py:16
  183.5 0.6 slice.150.got
  184.2 4.8 %shard_map.29 = f32[8,2,16,128]{3,2,1,0:T(8,128)} custom-call(s32[1]{0:T(128)} %bitcast.owner_ref, bf16[16,16,128]{2,1,0:T(8,128)(2,1)} %slice.150.got, f32[2,16,512]{2,1,0:T(8,128)} %shard_map.28.sofar, f32[4,16,128]{2,1,0:T(8,128)} %pad_maximum_fusion.solved, bf16[8,64,8192]{2,1,0:T(8,128)(2,1)} %bitcast.139, bf16[8,64,8192]{2,1,0:T(8,128)(2,1)} %bitcast.141), custom_call_target="tpu_custom_call" | custom-call | flops 67108864 | bytes 4194304 | tf_op jit(solution)/shard_map/pallas_call | solution.py:174
  188.9 13.1 %all-to-all-start.9 = ((f32[8,2,16,128]{3,2,1,0:T(8,128)}), f32[8,2,16,128]{3,2,1,0:T(8,128)S(1)}, u32[]{:S(2)}, u32[]{:S(2)}) async-start(f32[8,2,16,128]{3,2,1,0:T(8,128)} %shard_map.29), calls=%async_computation.9 | async-start | bytes 262144 | tf_op jit(solution)/shard_map/all_to_all | solution.py:16
  202.0 0.1 copy.25
  202.1 0.1 copy.26
  202.2 5.1 %all-to-all-done.9 = f32[8,2,16,128]{3,2,1,0:T(8,128)S(1)} async-done(((f32[8,2,16,128]{3,2,1,0:T(8,128)}), f32[8,2,16,128]{3,2,1,0:T(8,128)S(1)}, u32[]{:S(2)}, u32[]{:S(2)}) %all-to-all-start.9) | async-done | bytes 131104 | tf_op jit(solution)/shard_map/all_to_all | solution.py:16
  207.3 0.1 dynamic-slice_bitcast_fusion
  207.5 0.7 copy.24
  (36 shorter events, 0.7 us)
Async XLA Ops:
  6.5 71.3 %all-gather.7.cloned.1.call-start = ((), (), s32[]{:S(2)}) async-start(), calls=%async_computation.10 | async-start | bytes 9437184 | tf_op jit(solution)/shard_map/all_gather | solution.py:128
  9.6 0.8 copy-start.1
  9.6 162.2 %all-gather.9.cloned.1.call-start = ((), (), s32[]{:S(2)}) async-start(), calls=%async_computation.11 | async-start | bytes 9437184 | tf_op jit(solution)/shard_map/all_gather | solution.py:129
  19.8 25.0 %all-to-all-start = ((f32[16,64,128]{2,1,0:T(8,128)}), f32[16,64,128]{2,1,0:T(8,128)S(1)}, u32[]{:S(2)}, u32[]{:S(2)}) async-start(f32[16,64,128]{2,1,0:T(8,128)} %broadcast_in_dim.62), calls=%async_computation | async-start | bytes 1048576 | tf_op jit(solution)/shard_map/all_to_all | solution.py:16
  53.8 99.9 %copy-start = (f32[4,16,128]{2,1,0:T(8,128)}, f32[4,16,128]{2,1,0:T(8,128)S(1)}, u32[]{:S(2)}) copy-start(f32[4,16,128]{2,1,0:T(8,128)S(1)} %all_to_all.50) | copy-start | bytes 98308
  80.6 17.2 %all-to-all-start.3 = ((f32[16,16,128]{2,1,0:T(8,128)}), f32[16,16,128]{2,1,0:T(8,128)S(1)}, u32[]{:S(2)}, u32[]{:S(2)}) async-start(f32[16,16,128]{2,1,0:T(8,128)} %broadcast_in_dim.66), calls=%async_computation.3 | async-start | bytes 262144 | tf_op jit(solution)/shard_map/all_to_all | solution.py:16
  98.8 17.3 %all-to-all-start.4 = ((bf16[64,16,128]{2,1,0:T(8,128)(2,1)}), bf16[64,16,128]{2,1,0:T(8,128)(2,1)S(1)}, u32[]{:S(2)}, u32[]{:S(2)}) async-start(bf16[64,16,128]{2,1,0:T(8,128)(2,1)} %broadcast_in_dim.67), calls=%async_computation.4 | async-start | bytes 524288 | tf_op jit(solution)/shard_map/all_to_all | solution.py:16
  150.2 15.3 %all-to-all-start.7 = ((f32[16,16,128]{2,1,0:T(8,128)}), f32[16,16,128]{2,1,0:T(8,128)S(1)}, u32[]{:S(2)}, u32[]{:S(2)}) async-start(f32[16,16,128]{2,1,0:T(8,128)} %broadcast_in_dim.72), calls=%async_computation.7 | async-start | bytes 262144 | tf_op jit(solution)/shard_map/all_to_all | solution.py:16
  166.5 17.0 %all-to-all-start.8 = ((bf16[64,16,128]{2,1,0:T(8,128)(2,1)}), bf16[64,16,128]{2,1,0:T(8,128)(2,1)S(1)}, u32[]{:S(2)}, u32[]{:S(2)}) async-start(bf16[64,16,128]{2,1,0:T(8,128)(2,1)} %broadcast_in_dim.73), calls=%async_computation.8 | async-start | bytes 524288 | tf_op jit(solution)/shard_map/all_to_all | solution.py:16
  171.8 7.0 %slice-start = ((f32[4,16,128]{2,1,0:T(8,128)}), f32[1,16,128]{2,1,0:T(8,128)S(1)}, s32[]{:S(2)}) async-start(f32[4,16,128]{2,1,0:T(8,128)} %copy-done), calls=%async_computation.12 | async-start | bytes 16384 | tf_op jit(solution)/shard_map/slice | solution.py:151
  188.9 18.4 %all-to-all-start.9 = ((f32[8,2,16,128]{3,2,1,0:T(8,128)}), f32[8,2,16,128]{3,2,1,0:T(8,128)S(1)}, u32[]{:S(2)}, u32[]{:S(2)}) async-start(f32[8,2,16,128]{3,2,1,0:T(8,128)} %shard_map.29), calls=%async_computation.9 | async-start | bytes 262144 | tf_op jit(solution)/shard_map/all_to_all | solution.py:16
Sparse Core Ops, SparseCore 0:
  9.8 61.2 all-gather.6
  73.2 55.2 all-gather.8

commit v7 on v6

--- a/solution.py
+++ b/solution.py
@@ -44,10 +44,15 @@
 TILE, SLOTS = 1024, 6
 
 
-def stream(plan, early_ref, late_ref, held, sems, cases_of):
+def stream(plan, sources, held, sems, cases_of):
     def copy(n):
         index, place = plan[n]
-        ref = (late_ref if index else early_ref).at[:, :, place : place + TILE]
+        early, late = sources
+        wide = early.shape[2]
+        width = (early.shape[2] + late.shape[2]) // 2
+        source = late if index or place >= wide else early
+        start = place if source is early else place - wide + index * width
+        ref = source.at[:, :, start : start + TILE]
         return pltpu.make_async_copy(ref, held.at[n % SLOTS], sems.at[n % SLOTS])
 
     for n in range(min(SLOTS, len(plan))):
@@ -63,40 +68,41 @@
 
 
 def first_kernel(plan, *refs):
-    *whole, early_ref, late_ref, out_ref, held, sems = refs
+    *whole, early, late, out_ref, held, sems = refs
     block = whole[0].shape[1]
 
     def cases_of(place):
         start = place % block
         return whole[place // block][:, start : start + TILE]
 
-    total = stream(plan, early_ref, late_ref, held, sems, cases_of)
+    total = stream(plan, (early, late), held, sems, cases_of)
     for index in range(2):
         out_ref[index] = total[index]
 
 
-def last_kernel(plan, owner_ref, got, sofar, solved, early_ref, late_ref, out, held, sems):
+def last_kernel(plan, owner_ref, got, sofar, solved, early, late, out, *scratch):
+    held, sems = scratch
     pair = got.shape[2]
-    xs = solved.shape[0]
+    xs = solved.shape[0] + 1
 
     def cases_of(place):
         chip = (place - plan[0][1]) // pair
         return jnp.concatenate([got[chip + n] for n in range(TILE // pair)], 1)
 
-    total = stream(plan, early_ref, late_ref, held, sems, cases_of)
+    total = stream(plan, (early, late), held, sems, cases_of)
     owner = owner_ref[0] == 0
     for x in range(xs):
         for index in range(2):
             span = slice(x * pair, (x + 1) * pair)
             value = sofar[index, :, span] + total[index][:, span]
-            if index == 0:
-                value = jnp.where(owner, solved[x], value)
+            if index == 0 and x > 0:
+                value = jnp.where(owner, solved[x - 1], value)
             for core in range(out.shape[0] // xs):
                 out[x * (out.shape[0] // xs) + core, index] = value
 
 
-def streaming(kernel, plan, early, out_shape, spaces):
-    lines, share, _ = early.shape
+def streaming(kernel, plan, sources, out_shape, spaces):
+    lines, share, _ = sources[0].shape
     count = len(plan) * lines * share * TILE
     few = out_shape[-2]
     return pl.pallas_call(
@@ -125,17 +131,22 @@
     few = cases // (xs * cores)
     pair = cores * share
 
-    early = lax.all_gather(stored[0], ("x", "c"), axis=0)
-    late = lax.all_gather(stored[1], ("x", "c"), axis=0)
+    wide = width - block
+    early = lax.all_gather(stored[0, :, :wide], ("x", "c"), axis=0)
+    late = jnp.concatenate([stored[0, :, wide:], stored[1]], 1)
+    late = lax.all_gather(late, ("x", "c"), axis=0)
 
     def panel(row, column):
-        part = early[:, :, column * block : (column + 1) * block]
+        start = column * block
+        part = late[:, :, :block] if start == wide else early[:, :, start : start + block]
         return part.reshape(xs, pair, block)[row:].reshape(-1, block)
+
+    chips = lax.axis_size(CHIPS)
 
     def to_all(part):
         planes = ("yl",) + CHIPS
         got = exchange(repeat(part, lax.axis_size(planes)), planes)
-        return got[: lax.axis_size(CHIPS)]
+        return got[:chips]
 
     together = lax.all_gather(given[0], "c", axis=0, tiled=True).T
     mine = lax.dynamic_index_in_dim(
@@ -144,45 +155,62 @@
     mine = mine.reshape(xs * few, pair)
     start = lax.all_gather(stored[0, :, :block], "c", axis=0, tiled=True)
     whole = gather_chips(mine)
+    state = lax.all_gather(mine, "x", axis=0).reshape(xs, xs, few, pair)[1:]
+    state = lax.dynamic_index_in_dim(state, lax.axis_index("x"), 1, False)
     first = times_exact(whole, start)
-    first = jnp.where(lax.axis_index("x") == 0, first, mine)
-    state = exchange(first.reshape(xs, few, pair), "x")
-
-    solved, known = [state[0]], []
-    state = state[1:]
+    opened = lax.all_gather(first.reshape(xs, few, pair), "c", axis=1)
+    opened = opened.reshape(cases, pair).T
+    parts = first.astype(jnp.bfloat16).reshape(xs, 1, few, pair)
+    parts = jnp.broadcast_to(parts, (xs, chips, few, pair))
+    got = exchange(parts.reshape(xs * chips, few, pair), ("x",) + CHIPS)[:chips]
+    whole = jnp.swapaxes(got, 0, 1).reshape(few, block)
+
+    solved, known = [], []
+    sent = [lax.dynamic_index_in_dim(got, lax.axis_index(CHIPS), 0, False)]
     for step in range(1, steps):
-        got = to_all(solved[-1].astype(jnp.bfloat16))
-        known.append(jnp.swapaxes(got, 0, 1).reshape(few, block))
-        update = times(known[-1], panel(step, step - 1))
+        update = times(whole, panel(step, step - 1))
         update = update.reshape(few, steps - step, pair)
         state = state - jnp.swapaxes(update, 0, 1)
         solved.append(times_exact(gather_chips(state[0]), panel(step, step)[:pair]))
         state = state[1:]
-
-    got = to_all(solved[-1].astype(jnp.bfloat16))
+        sent.append(solved[-1].astype(jnp.bfloat16))
+        if step == 1:
+            both = to_all(jnp.concatenate(sent, 0))
+            got = both[:, few:]
+            known.append(jnp.swapaxes(both[:, :few], 0, 1).reshape(few, block))
+        else:
+            got = to_all(sent[-1])
+        if step + 1 < steps:
+            whole = jnp.swapaxes(got, 0, 1).reshape(few, block)
+            known.append(whole)
+
     plan = [
         [(index, place) for place in range(*span, TILE) for index in range(2)]
         for span in ((0, width - block), (width - block, width))
     ]
+    gathered = [early, late]
     sofar = streaming(
         first_kernel,
         plan[0],
-        early,
+        gathered,
         (2, few, xs * pair),
         [pltpu.VMEM] * len(known) + [pl.ANY] * 2,
-    )(*known, early, late)
+    )(*known, *gathered)
     both = streaming(
         last_kernel,
         plan[1],
-        early,
+        gathered,
         (xs * cores, 2, few, pair),
         [pltpu.SMEM] + [pltpu.VMEM] * 3 + [pl.ANY] * 2,
-    )(lax.axis_index("yl")[None], got, sofar, jnp.stack(solved), early, late)
+    )(lax.axis_index("yl")[None], got, sofar, jnp.stack(solved), *gathered)
     back = exchange(both, ("x", "c"))
     owner = lax.axis_index("yl") == 0
     back = jnp.swapaxes(back, 0, 1).reshape(2, cases, pair).transpose(0, 2, 1)
-    back = lax.dynamic_slice_in_dim(back, lax.axis_index("c") * share, share, 1)
-    top = jnp.where(owner, back[0], given[0] - back[0])
+    place = lax.axis_index("c") * share
+    back = lax.dynamic_slice_in_dim(back, place, share, 1)
+    opened = lax.dynamic_slice_in_dim(opened, place, share, 0)
+    result = jnp.where(lax.axis_index("x") == 0, opened, back[0])
+    top = jnp.where(owner, result, given[0] - back[0])
     return jnp.stack([top, given[1] - back[1]])[:, None]
 
 

time: 216 us -> 221 us (1.023)
  blocking collectives: 75.8 us -> 38.1 us
  starting transfers between devices: 41.2 us -> 65.2 us
  waiting for transfers between devices: 53 us -> 70.4 us
    all_to_all x4 -> x1, blocking collectives: 64.6 us -> 14.7 us  [exchange(): return lax.all_to_all(parts, axis, 0, 0, tiled=True)]
    all_to_all x6 -> x8, starting transfers between devices: 41.2 us -> 65.2 us  [exchange(): return lax.all_to_all(parts, axis, 0, 0, tiled=True)]
    all_to_all x6 -> x8, waiting for transfers between devices: 52.3 us -> 70.4 us  [exchange(): return lax.all_to_all(parts, axis, 0, 0, tiled=True)]
    all_gather x0 -> x2, blocking collectives: none -> 12.2 us  [the longest x1 10.4 us: body(): state = lax.all_gather(mine, 'x', axis=0).reshape(xs, xs, few, pair)[1:]]
    broadcast_in_dim x11 -> x9, local copies, waits for them, and re-layouts: 3.8 us -> 4.6 us  [repeat(): return jnp.broadcast_to(part[None], (count,) + part.shape)]
  transfers between devices with their start and end apart: 8 -> 10, of which waited for: 6 -> 8; matrix products, arithmetic and copies ran while one was open for 7% -> 7% of each run, Pallas kernels for 3% -> 3%
where the time goes in v7:
time: 221 us; the launch traced here: 220 us
  waiting for transfers between devices  70.4 us (32%)
  starting transfers between devices  65.2 us (30%)
  blocking collectives  38.1 us (17%)
  local copies, waits for them, and re-layouts  16.4 us (7%)
  between operations  13.8 us (6%)
  Pallas kernels  11.7 us (5%)
  matrix products  2.35 us (1%)
    all_to_all x8, waiting for transfers between devices, exchange(): return lax.all_to_all(parts, axis, 0, 0, tiled=True)  70.4 us
    all_to_all x8, starting transfers between devices, exchange(): return lax.all_to_all(parts, axis, 0, 0, tiled=True)  65.2 us
    all_to_all x1, blocking collectives, exchange(): return lax.all_to_all(parts, axis, 0, 0, tiled=True)  14.7 us
    all_gather x1, blocking collectives, body(): state = lax.all_gather(mine, 'x', axis=0).reshape(xs, xs, few, pair)[1:]  10.4 us
    all_gather x1, blocking collectives, body(): together = lax.all_gather(given[0], 'c', axis=0, tiled=True).T  8.38 us
    pallas_call x1, Pallas kernels, body(): streaming(first_kernel, plan[0], gathered, (2, few, xs * pair), [pltpu.VM...  6.96 us
    pallas_call x1, Pallas kernels, body(): streaming(last_kernel, plan[1], gathered, (xs * cores, 2, few, pair), [pl...  4.74 us
    broadcast_in_dim x9, local copies, waits for them, and re-layouts, repeat(): return jnp.broadcast_to(part[None], (count,) + part.shape)  4.6 us
  transfers between devices with their start and end apart: 10, of which 8 were waited for; matrix products, arithmetic and copies ran while one was open for 7% of the time, Pallas kernels for 3%

profile of v7, /device:TPU:1, one launch (start us, length us, event | category | flops | bytes accessed | tf_op | source)
XLA Modules:
  0.0 220.1 jit_solution(17711257349781284164)
XLA Ops:
  6.5 2.2 %slice.141 = bf16[1,64,6144]{2,1,0:T(8,128)(2,1)} slice(bf16[2,64,8192]{2,1,0:T(8,128)(2,1)} %bitcast.164), slice={[0:1], [0:64], [0:6144]} | slice | bytes 1572864 | tf_op jit(solution)/shard_map/slice | solution.py:135
  9.0 1.2 pad_maximum_fusion
  10.2 8.4 %all-gather = f32[1,1,128,128]{3,1,0,2:T(1,128)S(1)} all-gather(f32[1,1,64,128]{3,1,0,2:T(1,128)S(1)} %bitcast.174), channel_id=2, replica_groups=mesh['yl'=4,'x'=4,'z'=8,'yh'=2,'c'=2] {'c'}, dimensions={2}, use_global_device_ids=true | all-gather | bytes 98304 | tf_op jit(solution)/shard_map/all_gather | solution.py:151
  18.7 0.9 broadcast_in_dim.60
  19.5 10.0 %all-to-all-start = ((f32[16,64,128]{2,1,0:T(8,128)}), f32[16,64,128]{2,1,0:T(8,128)S(1)}, u32[]{:S(2)}, u32[]{:S(2)}) async-start(f32[16,64,128]{2,1,0:T(8,128)} %broadcast_in_dim.60), calls=%async_computation | async-start | bytes 1048576 | tf_op jit(solution)/shard_map/all_to_all | solution.py:16
  29.6 2.8 %all-gather.1 = bf16[1,128,2048]{2,1,0:T(8,128)(2,1)S(1)} all-gather(bf16[1,64,2048]{2,1,0:T(8,128)(2,1)S(1)} %get-tuple-element.10), channel_id=3, replica_groups=mesh['yl'=4,'x'=4,'z'=8,'yh'=2,'c'=2] {'c'}, dimensions={1}, use_global_device_ids=true | all-gather | bytes 786432 | tf_op jit(solution)/shard_map/all_gather | solution.py:156
  32.4 12.2 %all-to-all-done = f32[16,64,128]{2,1,0:T(8,128)S(1)} async-done(((f32[16,64,128]{2,1,0:T(8,128)}), f32[16,64,128]{2,1,0:T(8,128)S(1)}, u32[]{:S(2)}, u32[]{:S(2)}) %all-to-all-start) | async-done | bytes 524320 | tf_op jit(solution)/shard_map/all_to_all | solution.py:16
  44.7 0.4 fusion.4
  45.0 0.8 broadcast_in_dim.63
  45.8 12.8 %all-to-all-start.1 = ((bf16[64,16,128]{2,1,0:T(8,128)(2,1)}), bf16[64,16,128]{2,1,0:T(8,128)(2,1)S(1)}, u32[]{:S(2)}, u32[]{:S(2)}) async-start(bf16[64,16,128]{2,1,0:T(8,128)(2,1)} %bitcast.16), calls=%async_computation.1 | async-start | bytes 524288 | tf_op jit(solution)/shard_map/all_to_all | solution.py:16
  58.6 10.4 %all_gather.24 = f32[4,64,128]{2,1,0:T(8,128)S(1)} all-gather(f32[1,64,128]{2,1,0:T(8,128)S(1)} %bitcast.173), channel_id=1, replica_groups=mesh['yl'=4,'x'=4,'z'=8,'yh'=2,'c'=2] {'x'}, dimensions={0}, use_global_device_ids=true | all-gather | bytes 163840 | tf_op jit(solution)/shard_map/all_gather | solution.py:158
  69.0 3.1 %all-to-all-done.1 = bf16[64,16,128]{2,1,0:T(8,128)(2,1)S(1)} async-done(((bf16[64,16,128]{2,1,0:T(8,128)(2,1)}), bf16[64,16,128]{2,1,0:T(8,128)(2,1)S(1)}, u32[]{:S(2)}, u32[]{:S(2)}) %all-to-all-start.1) | async-done | bytes 262176 | tf_op jit(solution)/shard_map/all_to_all | solution.py:16
  72.3 1.5 slice.142
  73.8 0.5 fusion
  74.3 0.7 broadcast_in_dim.65
  75.0 8.4 %all-to-all-start.2 = ((f32[16,16,128]{2,1,0:T(8,128)}), f32[16,16,128]{2,1,0:T(8,128)S(1)}, u32[]{:S(2)}, u32[]{:S(2)}) async-start(f32[16,16,128]{2,1,0:T(8,128)} %broadcast_in_dim.65), calls=%async_computation.2 | async-start | bytes 262144 | tf_op jit(solution)/shard_map/all_to_all | solution.py:16
  83.3 1.5 fusion.46
  84.8 10.4 %all-to-all-done.2 = f32[16,16,128]{2,1,0:T(8,128)S(1)} async-done(((f32[16,16,128]{2,1,0:T(8,128)}), f32[16,16,128]{2,1,0:T(8,128)S(1)}, u32[]{:S(2)}, u32[]{:S(2)}) %all-to-all-start.2) | async-done | bytes 131104 | tf_op jit(solution)/shard_map/all_to_all | solution.py:16
  95.2 0.3 fusion.12
  95.5 0.9 broadcast_in_dim.66
  96.4 4.8 %all-to-all-start.3 = ((bf16[64,32,128]{2,1,0:T(8,128)(2,1)}), bf16[64,32,128]{2,1,0:T(8,128)(2,1)S(1)}, u32[]{:S(2)}, u32[]{:S(2)}) async-start(bf16[64,32,128]{2,1,0:T(8,128)(2,1)} %broadcast_in_dim.66), calls=%async_computation.3 | async-start | bytes 1048576 | tf_op jit(solution)/shard_map/all_to_all | solution.py:16
  101.2 1.4 slice.147
  102.7 13.7 %all-to-all-done.3 = bf16[64,32,128]{2,1,0:T(8,128)(2,1)S(1)} async-done(((bf16[64,32,128]{2,1,0:T(8,128)(2,1)}), bf16[64,32,128]{2,1,0:T(8,128)(2,1)S(1)}, u32[]{:S(2)}, u32[]{:S(2)}) %all-to-all-start.3) | async-done | bytes 524320 | tf_op jit(solution)/shard_map/all_to_all | solution.py:16
  116.5 0.4 fusion.1
  116.9 14.7 %all_to_all.45 = f32[16,16,128]{2,1,0:T(8,128)S(1)} all-to-all(f32[16,16,128]{2,1,0:T(8,128)S(1)} %broadcast_in_dim.68), channel_id=1, replica_groups=mesh['yl'=4,'x'=4,'z'=8,'yh'=2,'c'=2] {'z','yh'}, dimensions={0} | all-to-all | bytes 262144 | tf_op jit(solution)/shard_map/all_to_all | solution.py:16
  131.6 0.3 fusion.18
  131.9 0.7 broadcast_in_dim.69
  132.7 5.4 %all-to-all-start.5 = ((bf16[64,16,128]{2,1,0:T(8,128)(2,1)}), bf16[64,16,128]{2,1,0:T(8,128)(2,1)S(1)}, u32[]{:S(2)}, u32[]{:S(2)}) async-start(bf16[64,16,128]{2,1,0:T(8,128)(2,1)} %broadcast_in_dim.69), calls=%async_computation.5 | async-start | bytes 524288 | tf_op jit(solution)/shard_map/all_to_all | solution.py:16
  138.1 12.5 %all-to-all-done.5 = bf16[64,16,128]{2,1,0:T(8,128)(2,1)S(1)} async-done(((bf16[64,16,128]{2,1,0:T(8,128)(2,1)}), bf16[64,16,128]{2,1,0:T(8,128)(2,1)S(1)}, u32[]{:S(2)}, u32[]{:S(2)}) %all-to-all-start.5) | async-done | bytes 262176 | tf_op jit(solution)/shard_map/all_to_all | solution.py:16
  150.6 0.2 fusion.3
  150.8 0.7 broadcast_in_dim.71
  151.5 3.5 %all-to-all-start.6 = ((f32[16,16,128]{2,1,0:T(8,128)}), f32[16,16,128]{2,1,0:T(8,128)S(1)}, u32[]{:S(2)}, u32[]{:S(2)}) async-start(f32[16,16,128]{2,1,0:T(8,128)} %broadcast_in_dim.71), calls=%async_computation.6 | async-start | bytes 262144 | tf_op jit(solution)/shard_map/all_to_all | solution.py:16
  155.0 0.7 copy_bitcast_fusion
  155.6 11.1 %all-to-all-done.6 = f32[16,16,128]{2,1,0:T(8,128)S(1)} async-done(((f32[16,16,128]{2,1,0:T(8,128)}), f32[16,16,128]{2,1,0:T(8,128)S(1)}, u32[]{:S(2)}, u32[]{:S(2)}) %all-to-all-start.6) | async-done | bytes 131104 | tf_op jit(solution)/shard_map/all_to_all | solution.py:16
  166.8 1.1 slice.154
  167.9 0.3 fusion.24
  168.2 0.7 broadcast_in_dim.72
  169.0 4.6 %all-to-all-start.7 = ((bf16[64,16,128]{2,1,0:T(8,128)(2,1)}), bf16[64,16,128]{2,1,0:T(8,128)(2,1)S(1)}, u32[]{:S(2)}, u32[]{:S(2)}) async-start(bf16[64,16,128]{2,1,0:T(8,128)(2,1)} %broadcast_in_dim.72), calls=%async_computation.7 | async-start | bytes 524288 | tf_op jit(solution)/shard_map/all_to_all | solution.py:16
  173.6 0.6 copy_bitcast_fusion.2.refs_2_
  174.2 7.0 %shard_map.28.sofar = f32[2,16,512]{2,1,0:T(8,128)} custom-call(bf16[16,2048]{1,0:T(8,128)(2,1)} %get-tuple-element.38.refs_0_, bf16[16,2048]{1,0:T(8,128)(2,1)} %get-tuple-element.37.refs_1_, bf16[16,2048]{1,0:T(8,128)(2,1)} %copy_bitcast_fusion.2.refs_2_, bf16[8,64,6144]{2,1,0:T(8,128)(2,1)} %all-gather.6.cloned.1.call-done.refs_3_.early, ...), custom_call_target="tpu_custom_call" | custom-call | flops 201326592 | bytes 12582912 | tf_op jit(solution)/shard_map/pallas_call | solution.py:192
  181.2 0.6 pad_maximum_fusion.1.solved
  181.8 4.2 %all-to-all-done.7 = bf16[64,16,128]{2,1,0:T(8,128)(2,1)S(1)} async-done(((bf16[64,16,128]{2,1,0:T(8,128)(2,1)}), bf16[64,16,128]{2,1,0:T(8,128)(2,1)S(1)}, u32[]{:S(2)}, u32[]{:S(2)}) %all-to-all-start.7) | async-done | bytes 262176 | tf_op jit(solution)/shard_map/all_to_all | solution.py:16
  185.9 0.6 slice.155.got
  186.6 4.7 %shard_map.29 = f32[8,2,16,128]{3,2,1,0:T(8,128)} custom-call(s32[1]{0:T(128)} %bitcast.11.owner_ref, bf16[16,16,128]{2,1,0:T(8,128)(2,1)} %slice.155.got, f32[2,16,512]{2,1,0:T(8,128)} %shard_map.28.sofar, f32[3,16,128]{2,1,0:T(8,128)} %pad_maximum_fusion.1.solved, bf16[8,64,6144]{2,1,0:T(8,128)(2,1)} %all-gather.6.cloned.1.call-done.refs_3_.early, ...), custom_call_target="tpu_custom_call" | custom-call | flops 67108864 | bytes 4194304 | tf_op jit(solution)/shard_map/pallas_call | solution.py:199
  191.3 15.7 %all-to-all-start.8 = ((f32[8,2,16,128]{3,2,1,0:T(8,128)}), f32[8,2,16,128]{3,2,1,0:T(8,128)S(1)}, u32[]{:S(2)}, u32[]{:S(2)}) async-start(f32[8,2,16,128]{3,2,1,0:T(8,128)} %shard_map.29), calls=%async_computation.8 | async-start | bytes 262144 | tf_op jit(solution)/shard_map/all_to_all | solution.py:16
  207.2 1.9 all_gather.23
  209.0 3.2 %all-to-all-done.8 = f32[8,2,16,128]{3,2,1,0:T(8,128)S(1)} async-done(((f32[8,2,16,128]{3,2,1,0:T(8,128)}), f32[8,2,16,128]{3,2,1,0:T(8,128)S(1)}, u32[]{:S(2)}, u32[]{:S(2)}) %all-to-all-start.8) | async-done | bytes 131104 | tf_op jit(solution)/shard_map/all_to_all | solution.py:16
  212.5 0.7 copy.25
  (42 shorter events, 1.2 us)
Async XLA Ops:
  6.5 2.3 %copy-start = (bf16[2,1,64,8192]{3,2,1,0:T(8,128)(2,1)S(1)}, bf16[2,1,64,8192]{3,2,1,0:T(8,128)(2,1)}, u32[]{:S(2)}) copy-start(bf16[2,1,64,8192]{3,2,1,0:T(8,128)(2,1)} %param.2) | copy-start | bytes 6291460
  6.5 65.7 %all-gather.6.cloned.1.call-start = ((), (), s32[]{:S(2)}) async-start(), calls=%async_computation.9 | async-start | bytes 7077888 | tf_op jit(solution)/shard_map/all_gather | solution.py:135
  8.8 158.1 %all-gather.8.cloned.1.call-start = ((), (), s32[]{:S(2)}) async-start(), calls=%async_computation.10 | async-start | bytes 11796480 | tf_op jit(solution)/shard_map/all_gather | solution.py:137
  9.0 1.2 copy-start.1
  19.5 25.0 %all-to-all-start = ((f32[16,64,128]{2,1,0:T(8,128)}), f32[16,64,128]{2,1,0:T(8,128)S(1)}, u32[]{:S(2)}, u32[]{:S(2)}) async-start(f32[16,64,128]{2,1,0:T(8,128)} %broadcast_in_dim.60), calls=%async_computation | async-start | bytes 1048576 | tf_op jit(solution)/shard_map/all_to_all | solution.py:16
  45.8 26.3 %all-to-all-start.1 = ((bf16[64,16,128]{2,1,0:T(8,128)(2,1)}), bf16[64,16,128]{2,1,0:T(8,128)(2,1)S(1)}, u32[]{:S(2)}, u32[]{:S(2)}) async-start(bf16[64,16,128]{2,1,0:T(8,128)(2,1)} %bitcast.16), calls=%async_computation.1 | async-start | bytes 524288 | tf_op jit(solution)/shard_map/all_to_all | solution.py:16
  75.0 20.2 %all-to-all-start.2 = ((f32[16,16,128]{2,1,0:T(8,128)}), f32[16,16,128]{2,1,0:T(8,128)S(1)}, u32[]{:S(2)}, u32[]{:S(2)}) async-start(f32[16,16,128]{2,1,0:T(8,128)} %broadcast_in_dim.65), calls=%async_computation.2 | async-start | bytes 262144 | tf_op jit(solution)/shard_map/all_to_all | solution.py:16
  96.4 20.0 %all-to-all-start.3 = ((bf16[64,32,128]{2,1,0:T(8,128)(2,1)}), bf16[64,32,128]{2,1,0:T(8,128)(2,1)S(1)}, u32[]{:S(2)}, u32[]{:S(2)}) async-start(bf16[64,32,128]{2,1,0:T(8,128)(2,1)} %broadcast_in_dim.66), calls=%async_computation.3 | async-start | bytes 1048576 | tf_op jit(solution)/shard_map/all_to_all | solution.py:16
  132.7 17.9 %all-to-all-start.5 = ((bf16[64,16,128]{2,1,0:T(8,128)(2,1)}), bf16[64,16,128]{2,1,0:T(8,128)(2,1)S(1)}, u32[]{:S(2)}, u32[]{:S(2)}) async-start(bf16[64,16,128]{2,1,0:T(8,128)(2,1)} %broadcast_in_dim.69), calls=%async_computation.5 | async-start | bytes 524288 | tf_op jit(solution)/shard_map/all_to_all | solution.py:16
  151.5 15.3 %all-to-all-start.6 = ((f32[16,16,128]{2,1,0:T(8,128)}), f32[16,16,128]{2,1,0:T(8,128)S(1)}, u32[]{:S(2)}, u32[]{:S(2)}) async-start(f32[16,16,128]{2,1,0:T(8,128)} %broadcast_in_dim.71), calls=%async_computation.6 | async-start | bytes 262144 | tf_op jit(solution)/shard_map/all_to_all | solution.py:16
  169.0 17.0 %all-to-all-start.7 = ((bf16[64,16,128]{2,1,0:T(8,128)(2,1)}), bf16[64,16,128]{2,1,0:T(8,128)(2,1)S(1)}, u32[]{:S(2)}, u32[]{:S(2)}) async-start(bf16[64,16,128]{2,1,0:T(8,128)(2,1)} %broadcast_in_dim.72), calls=%async_computation.7 | async-start | bytes 524288 | tf_op jit(solution)/shard_map/all_to_all | solution.py:16
  191.3 20.9 %all-to-all-start.8 = ((f32[8,2,16,128]{3,2,1,0:T(8,128)}), f32[8,2,16,128]{3,2,1,0:T(8,128)S(1)}, u32[]{:S(2)}, u32[]{:S(2)}) async-start(f32[8,2,16,128]{3,2,1,0:T(8,128)} %shard_map.29), calls=%async_computation.8 | async-start | bytes 262144 | tf_op jit(solution)/shard_map/all_to_all | solution.py:16
Sparse Core Ops, SparseCore 0:
  9.5 52.1 all-gather.5
  63.8 63.9 all-gather.7

commit v8 on v6

--- a/solution.py
+++ b/solution.py
@@ -18,11 +18,6 @@
 
 def repeat(part, count):
     return jnp.broadcast_to(part[None], (count,) + part.shape)
-
-
-def gather_chips(part):
-    got = exchange(repeat(part, lax.axis_size(CHIPS)), CHIPS)
-    return jnp.swapaxes(got, 0, 1).reshape(part.shape[0], -1)
 
 
 def times(values, rows):
@@ -44,10 +39,17 @@
 TILE, SLOTS = 1024, 6
 
 
-def stream(plan, early_ref, late_ref, held, sems, cases_of):
+def stream(plan, sources, held, sems, cases_of):
+    width = sum(source.shape[2] for source in sources) // 2
+
     def copy(n):
         index, place = plan[n]
-        ref = (late_ref if index else early_ref).at[:, :, place : place + TILE]
+        start = place + index * width
+        for source in sources:
+            if start < source.shape[2]:
+                break
+            start -= source.shape[2]
+        ref = source.at[:, :, start : start + TILE]
         return pltpu.make_async_copy(ref, held.at[n % SLOTS], sems.at[n % SLOTS])
 
     for n in range(min(SLOTS, len(plan))):
@@ -63,19 +65,20 @@
 
 
 def first_kernel(plan, *refs):
-    *whole, early_ref, late_ref, out_ref, held, sems = refs
+    whole, sources, (out_ref, held, sems) = refs[:3], refs[3:-3], refs[-3:]
     block = whole[0].shape[1]
 
     def cases_of(place):
         start = place % block
         return whole[place // block][:, start : start + TILE]
 
-    total = stream(plan, early_ref, late_ref, held, sems, cases_of)
+    total = stream(plan, sources, held, sems, cases_of)
     for index in range(2):
         out_ref[index] = total[index]
 
 
-def last_kernel(plan, owner_ref, got, sofar, solved, early_ref, late_ref, out, held, sems):
+def last_kernel(plan, owner_ref, got, sofar, solved, *refs):
+    sources, (out, held, sems) = refs[:-3], refs[-3:]
     pair = got.shape[2]
     xs = solved.shape[0]
 
@@ -83,7 +86,7 @@
         chip = (place - plan[0][1]) // pair
         return jnp.concatenate([got[chip + n] for n in range(TILE // pair)], 1)
 
-    total = stream(plan, early_ref, late_ref, held, sems, cases_of)
+    total = stream(plan, sources, held, sems, cases_of)
     owner = owner_ref[0] == 0
     for x in range(xs):
         for index in range(2):
@@ -95,8 +98,8 @@
                 out[x * (out.shape[0] // xs) + core, index] = value
 
 
-def streaming(kernel, plan, early, out_shape, spaces):
-    lines, share, _ = early.shape
+def streaming(kernel, plan, sources, out_shape, spaces):
+    lines, share, _ = sources[0].shape
     count = len(plan) * lines * share * TILE
     few = out_shape[-2]
     return pl.pallas_call(
@@ -125,41 +128,52 @@
     few = cases // (xs * cores)
     pair = cores * share
 
-    early = lax.all_gather(stored[0], ("x", "c"), axis=0)
-    late = lax.all_gather(stored[1], ("x", "c"), axis=0)
+    def rows_of_line(part):
+        return lax.all_gather(part, ("x", "c"), axis=0)
+
+    last = width - block
+    gathered = [
+        rows_of_line(stored[0, :, :block]),
+        rows_of_line(stored[0, :, block:last]),
+        rows_of_line(jnp.concatenate([stored[0, :, last:], stored[1]], 1)),
+    ]
 
     def panel(row, column):
-        part = early[:, :, column * block : (column + 1) * block]
+        source = gathered[0 if column == 0 else 1 if column < steps - 1 else 2]
+        start = (column - 1) * block if 0 < column < steps - 1 else 0
+        part = source[:, :, start : start + block]
         return part.reshape(xs, pair, block)[row:].reshape(-1, block)
+
+    chips = lax.axis_size(CHIPS)
 
     def to_all(part):
         planes = ("yl",) + CHIPS
         got = exchange(repeat(part, lax.axis_size(planes)), planes)
-        return got[: lax.axis_size(CHIPS)]
+        return got[:chips]
 
     together = lax.all_gather(given[0], "c", axis=0, tiled=True).T
     mine = lax.dynamic_index_in_dim(
         together.reshape(xs, cores, few, pair), lax.axis_index("c"), 1, False
     )
-    mine = mine.reshape(xs * few, pair)
-    start = lax.all_gather(stored[0, :, :block], "c", axis=0, tiled=True)
-    whole = gather_chips(mine)
-    first = times_exact(whole, start)
-    first = jnp.where(lax.axis_index("x") == 0, first, mine)
-    state = exchange(first.reshape(xs, few, pair), "x")
-
-    solved, known = [state[0]], []
-    state = state[1:]
-    for step in range(1, steps):
+    parts = jnp.broadcast_to(mine[:, None], (xs, chips, few, pair))
+    got = exchange(parts.reshape(xs * chips, few, pair), ("x",) + CHIPS)[:chips]
+    state = lax.all_gather(mine, "x", axis=0)[1:]
+    state = lax.dynamic_index_in_dim(state, lax.axis_index("x"), 1, False)
+
+    solved, known = [], []
+    for step in range(steps):
+        whole = jnp.swapaxes(got, 0, 1).reshape(few, block)
+        solved.append(times_exact(whole, panel(step, step)[:pair]))
         got = to_all(solved[-1].astype(jnp.bfloat16))
+        if step + 1 == steps:
+            break
         known.append(jnp.swapaxes(got, 0, 1).reshape(few, block))
-        update = times(known[-1], panel(step, step - 1))
-        update = update.reshape(few, steps - step, pair)
+        update = times(known[-1], panel(step + 1, step))
+        update = update.reshape(few, steps - step - 1, pair)
         state = state - jnp.swapaxes(update, 0, 1)
-        solved.append(times_exact(gather_chips(state[0]), panel(step, step)[:pair]))
+        got = exchange(repeat(state[0], chips), CHIPS)
         state = state[1:]
 
-    got = to_all(solved[-1].astype(jnp.bfloat16))
     plan = [
         [(index, place) for place in range(*span, TILE) for index in range(2)]
         for span in ((0, width - block), (width - block, width))
@@ -167,21 +181,22 @@
     sofar = streaming(
         first_kernel,
         plan[0],
-        early,
+        gathered,
         (2, few, xs * pair),
-        [pltpu.VMEM] * len(known) + [pl.ANY] * 2,
-    )(*known, early, late)
+        [pltpu.VMEM] * len(known) + [pl.ANY] * len(gathered),
+    )(*known, *gathered)
     both = streaming(
         last_kernel,
         plan[1],
-        early,
+        gathered,
         (xs * cores, 2, few, pair),
-        [pltpu.SMEM] + [pltpu.VMEM] * 3 + [pl.ANY] * 2,
-    )(lax.axis_index("yl")[None], got, sofar, jnp.stack(solved), early, late)
+        [pltpu.SMEM] + [pltpu.VMEM] * 3 + [pl.ANY] * len(gathered),
+    )(lax.axis_index("yl")[None], got, sofar, jnp.stack(solved), *gathered)
     back = exchange(both, ("x", "c"))
     owner = lax.axis_index("yl") == 0
     back = jnp.swapaxes(back, 0, 1).reshape(2, cases, pair).transpose(0, 2, 1)
-    back = lax.dynamic_slice_in_dim(back, lax.axis_index("c") * share, share, 1)
+    place = lax.axis_index("c") * share
+    back = lax.dynamic_slice_in_dim(back, place, share, 1)
     top = jnp.where(owner, back[0], given[0] - back[0])
     return jnp.stack([top, given[1] - back[1]])[:, None]
 

time: 216 us -> 220 us (1.019)
  blocking collectives: 75.8 us -> 103 us
  waiting for transfers between devices: 53 us -> 33.4 us
  starting transfers between devices: 41.2 us -> 37.4 us
    all_to_all x4, blocking collectives: 64.6 us -> 83.9 us  [exchange(): return lax.all_to_all(parts, axis, 0, 0, tiled=True)]
    all_to_all x6 -> x5, waiting for transfers between devices: 52.3 us -> 33.3 us  [exchange(): return lax.all_to_all(parts, axis, 0, 0, tiled=True)]
    all_gather x1, blocking collectives: 2.81 us -> 10.7 us  [body(): state = lax.all_gather(mine, 'x', axis=0)[1:]]
    all_to_all x6 -> x5, starting transfers between devices: 41.2 us -> 37.3 us  [exchange(): return lax.all_to_all(parts, axis, 0, 0, tiled=True)]
  transfers between devices with their start and end apart: 8 -> 8, of which waited for: 6 -> 5; matrix products, arithmetic and copies ran while one was open for 7% -> 7% of each run, Pallas kernels for 3% -> 3%
where the time goes in v8:
time: 220 us; the launch traced here: 219 us
  blocking collectives  103 us (47%)
  starting transfers between devices  37.4 us (17%)
  waiting for transfers between devices  33.4 us (15%)
  local copies, waits for them, and re-layouts  15.8 us (7%)
  between operations  13.5 us (6%)
  Pallas kernels  11.7 us (5%)
  matrix products  2.31 us (1%)
    all_to_all x4, blocking collectives, exchange(): return lax.all_to_all(parts, axis, 0, 0, tiled=True)  83.9 us
    all_to_all x5, starting transfers between devices, exchange(): return lax.all_to_all(parts, axis, 0, 0, tiled=True)  37.3 us
    all_to_all x5, waiting for transfers between devices, exchange(): return lax.all_to_all(parts, axis, 0, 0, tiled=True)  33.3 us
    all_gather x1, blocking collectives, body(): state = lax.all_gather(mine, 'x', axis=0)[1:]  10.7 us
    all_gather x1, blocking collectives, body(): together = lax.all_gather(given[0], 'c', axis=0, tiled=True).T  8.38 us
    pallas_call x1, Pallas kernels, body(): streaming(first_kernel, plan[0], gathered, (2, few, xs * pair), [pltpu.VM...  6.96 us
    pallas_call x1, Pallas kernels, body(): streaming(last_kernel, plan[1], gathered, (xs * cores, 2, few, pair), [pl...  4.76 us
  transfers between devices with their start and end apart: 8, of which 5 were waited for; matrix products, arithmetic and copies ran while one was open for 7% of the time, Pallas kernels for 3%

profile of v8, /device:TPU:1, one launch (start us, length us, event | category | flops | bytes accessed | tf_op | source)
XLA Modules:
  0.0 219.0 jit_solution(7615263894826464317)
XLA Ops:
  6.5 1.9 fusion.45
  8.5 1.9 slice.146
  10.4 0.0 all-gather.11.cloned.1.call-start
  10.5 0.1 slice_bitcast_fusion
  10.6 1.2 pad_maximum_fusion
  11.8 8.4 %all-gather = f32[1,1,128,128]{3,1,0,2:T(1,128)S(1)} all-gather(f32[1,1,64,128]{3,1,0,2:T(1,128)S(1)} %bitcast.157), channel_id=2, replica_groups=mesh['yl'=4,'x'=4,'z'=8,'yh'=2,'c'=2] {'c'}, dimensions={2}, use_global_device_ids=true | all-gather | bytes 98304 | tf_op jit(solution)/shard_map/all_gather | solution.py:154
  20.2 0.1 copy.10
  20.4 31.2 %all_to_all.45 = f32[64,16,128]{2,1,0:T(8,128)S(1)} all-to-all(f32[64,16,128]{2,1,0:T(8,128)S(1)} %bitcast.148), channel_id=1, replica_groups=mesh['yl'=4,'x'=4,'z'=8,'yh'=2,'c'=2] {'x','z','yh'}, dimensions={0} | all-to-all | bytes 1048576 | tf_op jit(solution)/shard_map/all_to_all | solution.py:16
  51.6 1.1 slice.141
  52.7 0.3 fusion.4
  53.0 0.7 broadcast_in_dim.62
  53.7 11.2 %all-to-all-start.1 = ((bf16[64,16,128]{2,1,0:T(8,128)(2,1)}), bf16[64,16,128]{2,1,0:T(8,128)(2,1)S(1)}, u32[]{:S(2)}, u32[]{:S(2)}) async-start(bf16[64,16,128]{2,1,0:T(8,128)(2,1)} %broadcast_in_dim.62), calls=%async_computation.1 | async-start | bytes 524288 | tf_op jit(solution)/shard_map/all_to_all | solution.py:16
  65.0 10.7 %all-gather.1 = f32[16,1,16,128]{3,2,1,0:T(8,128)S(1)} all-gather(f32[4,1,16,128]{3,2,1,0:T(8,128)S(1)} %constant_dynamic-slice_fusion), channel_id=3, replica_groups=mesh['yl'=4,'x'=4,'z'=8,'yh'=2,'c'=2] {'x'}, dimensions={0}, use_global_device_ids=true | all-gather | bytes 163840 | tf_op jit(solution)/shard_map/all_gather | solution.py:160
  75.6 2.8 %all-to-all-done.1 = bf16[64,16,128]{2,1,0:T(8,128)(2,1)S(1)} async-done(((bf16[64,16,128]{2,1,0:T(8,128)(2,1)}), bf16[64,16,128]{2,1,0:T(8,128)(2,1)S(1)}, u32[]{:S(2)}, u32[]{:S(2)}) %all-to-all-start.1) | async-done | bytes 262176 | tf_op jit(solution)/shard_map/all_to_all | solution.py:16
  78.5 0.5 fusion
  79.0 20.0 %all_to_all.46 = f32[16,16,128]{2,1,0:T(8,128)S(1)} all-to-all(f32[16,16,128]{2,1,0:T(8,128)S(1)} %broadcast_in_dim.64), channel_id=1, replica_groups=mesh['yl'=4,'x'=4,'z'=8,'yh'=2,'c'=2] {'z','yh'}, dimensions={0} | all-to-all | bytes 262144 | tf_op jit(solution)/shard_map/all_to_all | solution.py:16
  99.1 1.5 fusion.44
  100.6 0.3 fusion.10
  100.9 0.7 broadcast_in_dim.65
  101.7 4.6 %all-to-all-start.3 = ((bf16[64,16,128]{2,1,0:T(8,128)(2,1)}), bf16[64,16,128]{2,1,0:T(8,128)(2,1)S(1)}, u32[]{:S(2)}, u32[]{:S(2)}) async-start(bf16[64,16,128]{2,1,0:T(8,128)(2,1)} %broadcast_in_dim.65), calls=%async_computation.3 | async-start | bytes 524288 | tf_op jit(solution)/shard_map/all_to_all | solution.py:16
  106.3 1.4 slice.149
  107.7 11.0 %all-to-all-done.3 = bf16[64,16,128]{2,1,0:T(8,128)(2,1)S(1)} async-done(((bf16[64,16,128]{2,1,0:T(8,128)(2,1)}), bf16[64,16,128]{2,1,0:T(8,128)(2,1)S(1)}, u32[]{:S(2)}, u32[]{:S(2)}) %all-to-all-start.3) | async-done | bytes 262176 | tf_op jit(solution)/shard_map/all_to_all | solution.py:16
  118.8 0.4 fusion.1
  119.2 14.7 %all_to_all.47 = f32[16,16,128]{2,1,0:T(8,128)S(1)} all-to-all(f32[16,16,128]{2,1,0:T(8,128)S(1)} %broadcast_in_dim.67), channel_id=1, replica_groups=mesh['yl'=4,'x'=4,'z'=8,'yh'=2,'c'=2] {'z','yh'}, dimensions={0} | all-to-all | bytes 262144 | tf_op jit(solution)/shard_map/all_to_all | solution.py:16
  133.9 0.3 fusion.16
  134.3 18.0 %all_to_all.48 = bf16[64,16,128]{2,1,0:T(8,128)(2,1)S(1)} all-to-all(bf16[64,16,128]{2,1,0:T(8,128)(2,1)S(1)} %broadcast_in_dim.68), channel_id=1, replica_groups=mesh['yl'=4,'x'=4,'z'=8,'yh'=2,'c'=2] {'yl','z','yh'}, dimensions={0} | all-to-all | bytes 524288 | tf_op jit(solution)/shard_map/all_to_all | solution.py:16
  152.3 0.3 fusion.3
  152.6 0.7 broadcast_in_dim.70
  153.2 3.5 %all-to-all-start.6 = ((f32[16,16,128]{2,1,0:T(8,128)}), f32[16,16,128]{2,1,0:T(8,128)S(1)}, u32[]{:S(2)}, u32[]{:S(2)}) async-start(f32[16,16,128]{2,1,0:T(8,128)} %broadcast_in_dim.70), calls=%async_computation.6 | async-start | bytes 262144 | tf_op jit(solution)/shard_map/all_to_all | solution.py:16
  156.8 0.6 copy.61
  157.4 0.6 copy.60
  158.0 10.5 %all-to-all-done.6 = f32[16,16,128]{2,1,0:T(8,128)S(1)} async-done(((f32[16,16,128]{2,1,0:T(8,128)}), f32[16,16,128]{2,1,0:T(8,128)S(1)}, u32[]{:S(2)}, u32[]{:S(2)}) %all-to-all-start.6) | async-done | bytes 131104 | tf_op jit(solution)/shard_map/all_to_all | solution.py:16
  168.6 1.1 slice.156
  169.7 0.3 fusion.22
  170.0 0.7 broadcast_in_dim.71
  170.7 4.8 %all-to-all-start.7 = ((bf16[64,16,128]{2,1,0:T(8,128)(2,1)}), bf16[64,16,128]{2,1,0:T(8,128)(2,1)S(1)}, u32[]{:S(2)}, u32[]{:S(2)}) async-start(bf16[64,16,128]{2,1,0:T(8,128)(2,1)} %broadcast_in_dim.71), calls=%async_computation.7 | async-start | bytes 524288 | tf_op jit(solution)/shard_map/all_to_all | solution.py:16
  175.5 0.6 copy_bitcast_fusion.2.refs_2_
  176.2 7.0 %shard_map.28.sofar = f32[2,16,512]{2,1,0:T(8,128)} custom-call(bf16[16,2048]{1,0:T(8,128)(2,1)} %bitcast.158, bf16[16,2048]{1,0:T(8,128)(2,1)} %bitcast.159, bf16[16,2048]{1,0:T(8,128)(2,1)} %copy_bitcast_fusion.2.refs_2_, bf16[8,64,2048]{2,1,0:T(8,128)(2,1)} %all-gather.7.cloned.1.call-done.refs_3_.refs_0_, ...), custom_call_target="tpu_custom_call" | custom-call | flops 201326592 | bytes 12582912 | tf_op jit(solution)/shard_map/pallas_call | solution.py:181
  183.1 0.6 pad_maximum_fusion.1.solved
  183.8 3.9 %all-to-all-done.7 = bf16[64,16,128]{2,1,0:T(8,128)(2,1)S(1)} async-done(((bf16[64,16,128]{2,1,0:T(8,128)(2,1)}), bf16[64,16,128]{2,1,0:T(8,128)(2,1)S(1)}, u32[]{:S(2)}, u32[]{:S(2)}) %all-to-all-start.7) | async-done | bytes 262176 | tf_op jit(solution)/shard_map/all_to_all | solution.py:16
  187.7 0.6 slice.157.got
  188.4 4.8 %shard_map.29 = f32[8,2,16,128]{3,2,1,0:T(8,128)} custom-call(s32[1]{0:T(128)} %bitcast.owner_ref, bf16[16,16,128]{2,1,0:T(8,128)(2,1)} %slice.157.got, f32[2,16,512]{2,1,0:T(8,128)} %shard_map.28.sofar, f32[4,16,128]{2,1,0:T(8,128)} %pad_maximum_fusion.1.solved, bf16[8,64,2048]{2,1,0:T(8,128)(2,1)} %all-gather.7.cloned.1.call-done.refs_3_.refs_0_, ...), custom_call_target="tpu_custom_call" | custom-call | flops 67108864 | bytes 4194304 | tf_op jit(solution)/shard_map/pallas_call | solution.py:188
  193.1 13.1 %all-to-all-start.8 = ((f32[8,2,16,128]{3,2,1,0:T(8,128)}), f32[8,2,16,128]{3,2,1,0:T(8,128)S(1)}, u32[]{:S(2)}, u32[]{:S(2)}) async-start(f32[8,2,16,128]{3,2,1,0:T(8,128)} %shard_map.29), calls=%async_computation.8 | async-start | bytes 262144 | tf_op jit(solution)/shard_map/all_to_all | solution.py:16
  206.3 0.1 copy.22
  206.4 0.1 copy.23
  206.5 5.1 %all-to-all-done.8 = f32[8,2,16,128]{3,2,1,0:T(8,128)S(1)} async-done(((f32[8,2,16,128]{3,2,1,0:T(8,128)}), f32[8,2,16,128]{3,2,1,0:T(8,128)S(1)}, u32[]{:S(2)}, u32[]{:S(2)}) %all-to-all-start.8) | async-done | bytes 131104 | tf_op jit(solution)/shard_map/all_to_all | solution.py:16
  211.6 0.1 dynamic-slice_bitcast_fusion
  211.7 0.7 copy.21
  (41 shorter events, 0.7 us)
Async XLA Ops:
  6.5 4.0 %copy-start = (bf16[2,1,64,8192]{3,2,1,0:T(8,128)(2,1)S(1)}, bf16[2,1,64,8192]{3,2,1,0:T(8,128)(2,1)}, u32[]{:S(2)}) copy-start(bf16[2,1,64,8192]{3,2,1,0:T(8,128)(2,1)} %param.2) | copy-start | bytes 6291460
  6.5 45.0 %all-gather.7.cloned.1.call-start = ((), (), s32[]{:S(2)}) async-start(), calls=%async_computation.9 | async-start | bytes 2359296 | tf_op jit(solution)/shard_map/all_gather | solution.py:132
  8.5 90.6 %all-gather.9.cloned.1.call-start = ((), (), s32[]{:S(2)}) async-start(), calls=%async_computation.10 | async-start | bytes 4718592 | tf_op jit(solution)/shard_map/all_gather | solution.py:132
  10.4 158.2 %all-gather.11.cloned.1.call-start = ((), (), s32[]{:S(2)}) async-start(), calls=%async_computation.11 | async-start | bytes 11796480 | tf_op jit(solution)/shard_map/all_gather | solution.py:132
  10.6 1.2 copy-start.1
  53.7 24.7 %all-to-all-start.1 = ((bf16[64,16,128]{2,1,0:T(8,128)(2,1)}), bf16[64,16,128]{2,1,0:T(8,128)(2,1)S(1)}, u32[]{:S(2)}, u32[]{:S(2)}) async-start(bf16[64,16,128]{2,1,0:T(8,128)(2,1)} %broadcast_in_dim.62), calls=%async_computation.1 | async-start | bytes 524288 | tf_op jit(solution)/shard_map/all_to_all | solution.py:16
  64.9 13.6 %slice-start = ((bf16[8,64,2048]{2,1,0:T(8,128)(2,1)}), bf16[6,64,2048]{2,1,0:T(8,128)(2,1)S(1)}, s32[]{:S(2)}) async-start(bf16[8,64,2048]{2,1,0:T(8,128)(2,1)} %all-gather.7.cloned.1.call-done.refs_3_.refs_0_), calls=%async_computation.12 | async-start | bytes 3145728 | tf_op jit(solution)/shard_map/slice | solution.py:145
  101.7 17.0 %all-to-all-start.3 = ((bf16[64,16,128]{2,1,0:T(8,128)(2,1)}), bf16[64,16,128]{2,1,0:T(8,128)(2,1)S(1)}, u32[]{:S(2)}, u32[]{:S(2)}) async-start(bf16[64,16,128]{2,1,0:T(8,128)(2,1)} %broadcast_in_dim.65), calls=%async_computation.3 | async-start | bytes 524288 | tf_op jit(solution)/shard_map/all_to_all | solution.py:16
  153.2 15.3 %all-to-all-start.6 = ((f32[16,16,128]{2,1,0:T(8,128)}), f32[16,16,128]{2,1,0:T(8,128)S(1)}, u32[]{:S(2)}, u32[]{:S(2)}) async-start(f32[16,16,128]{2,1,0:T(8,128)} %broadcast_in_dim.70), calls=%async_computation.6 | async-start | bytes 262144 | tf_op jit(solution)/shard_map/all_to_all | solution.py:16
  170.7 17.0 %all-to-all-start.7 = ((bf16[64,16,128]{2,1,0:T(8,128)(2,1)}), bf16[64,16,128]{2,1,0:T(8,128)(2,1)S(1)}, u32[]{:S(2)}, u32[]{:S(2)}) async-start(bf16[64,16,128]{2,1,0:T(8,128)(2,1)} %broadcast_in_dim.71), calls=%async_computation.7 | async-start | bytes 524288 | tf_op jit(solution)/shard_map/all_to_all | solution.py:16
  193.1 18.4 %all-to-all-start.8 = ((f32[8,2,16,128]{3,2,1,0:T(8,128)}), f32[8,2,16,128]{3,2,1,0:T(8,128)S(1)}, u32[]{:S(2)}, u32[]{:S(2)}) async-start(f32[8,2,16,128]{3,2,1,0:T(8,128)} %shard_map.29), calls=%async_computation.8 | async-start | bytes 262144 | tf_op jit(solution)/shard_map/all_to_all | solution.py:16
Sparse Core Ops, SparseCore 0:
  9.5 37.9 all-gather.6
  49.7 40.4 all-gather.8
  92.3 63.6 all-gather.10

commit v9 on v6

--- a/solution.py
+++ b/solution.py
@@ -41,24 +41,26 @@
     return (c + b) + a
 
 
-TILE, SLOTS = 1024, 6
+TILES = ((1024, 6), (512, 8))
 
 
 def stream(plan, early_ref, late_ref, held, sems, cases_of):
+    slots, tile = held.shape[0], held.shape[3]
+
     def copy(n):
         index, place = plan[n]
-        ref = (late_ref if index else early_ref).at[:, :, place : place + TILE]
-        return pltpu.make_async_copy(ref, held.at[n % SLOTS], sems.at[n % SLOTS])
+        ref = (late_ref if index else early_ref).at[:, :, place : place + tile]
+        return pltpu.make_async_copy(ref, held.at[n % slots], sems.at[n % slots])
 
-    for n in range(min(SLOTS, len(plan))):
+    for n in range(min(slots, len(plan))):
         copy(n).start()
     total = [None, None]
     for n, (index, place) in enumerate(plan):
         copy(n).wait()
-        part = times(cases_of(place), held[n % SLOTS].reshape(-1, TILE))
+        part = times(cases_of(place), held[n % slots].reshape(-1, tile))
         total[index] = part if total[index] is None else total[index] + part
-        if n + SLOTS < len(plan):
-            copy(n + SLOTS).start()
+        if n + slots < len(plan):
+            copy(n + slots).start()
     return total
 
 
@@ -68,7 +70,7 @@
 
     def cases_of(place):
         start = place % block
-        return whole[place // block][:, start : start + TILE]
+        return whole[place // block][:, start : start + held.shape[3]]
 
     total = stream(plan, early_ref, late_ref, held, sems, cases_of)
     for index in range(2):
@@ -81,7 +83,7 @@
 
     def cases_of(place):
         chip = (place - plan[0][1]) // pair
-        return jnp.concatenate([got[chip + n] for n in range(TILE // pair)], 1)
+        return jnp.concatenate([got[chip + n] for n in range(held.shape[3] // pair)], 1)
 
     total = stream(plan, early_ref, late_ref, held, sems, cases_of)
     owner = owner_ref[0] == 0
@@ -95,9 +97,11 @@
                 out[x * (out.shape[0] // xs) + core, index] = value
 
 
-def streaming(kernel, plan, early, out_shape, spaces):
+def streaming(kernel, span, tiles, early, out_shape, spaces):
     lines, share, _ = early.shape
-    count = len(plan) * lines * share * TILE
+    tile, slots = tiles
+    plan = [(index, place) for place in range(*span, tile) for index in range(2)]
+    count = len(plan) * lines * share * tile
     few = out_shape[-2]
     return pl.pallas_call(
         functools.partial(kernel, plan),
@@ -105,10 +109,10 @@
         in_specs=[pl.BlockSpec(memory_space=space) for space in spaces],
         out_specs=pl.BlockSpec(memory_space=pltpu.VMEM),
         scratch_shapes=[
-            pltpu.VMEM((SLOTS, lines, share, TILE), jnp.bfloat16),
-            pltpu.SemaphoreType.DMA((SLOTS,)),
+            pltpu.VMEM((slots, lines, share, tile), jnp.bfloat16),
+            pltpu.SemaphoreType.DMA((slots,)),
         ],
-        compiler_params=pltpu.CompilerParams(vmem_limit_bytes=60 * 2**20),
+        compiler_params=pltpu.CompilerParams(vmem_limit_bytes=52 * 2**20),
         cost_estimate=pl.CostEstimate(
             flops=2 * few * count, bytes_accessed=2 * count, transcendentals=0
         ),
@@ -132,10 +136,10 @@
         part = early[:, :, column * block : (column + 1) * block]
         return part.reshape(xs, pair, block)[row:].reshape(-1, block)
 
-    def to_all(part):
+    def to_all(part, own_plane=True):
         planes = ("yl",) + CHIPS
         got = exchange(repeat(part, lax.axis_size(planes)), planes)
-        return got[: lax.axis_size(CHIPS)]
+        return got[: lax.axis_size(CHIPS)] if own_plane else got
 
     together = lax.all_gather(given[0], "c", axis=0, tiled=True).T
     mine = lax.dynamic_index_in_dim(
@@ -159,21 +163,20 @@
         solved.append(times_exact(gather_chips(state[0]), panel(step, step)[:pair]))
         state = state[1:]
 
-    got = to_all(solved[-1].astype(jnp.bfloat16))
-    plan = [
-        [(index, place) for place in range(*span, TILE) for index in range(2)]
-        for span in ((0, width - block), (width - block, width))
-    ]
+    got = to_all(solved[-1].astype(jnp.bfloat16), False)
+    last = width - block
     sofar = streaming(
         first_kernel,
-        plan[0],
+        (0, last),
+        TILES[0],
         early,
         (2, few, xs * pair),
         [pltpu.VMEM] * len(known) + [pl.ANY] * 2,
     )(*known, early, late)
     both = streaming(
         last_kernel,
-        plan[1],
+        (last, width),
+        TILES[1],
         early,
         (xs * cores, 2, few, pair),
         [pltpu.SMEM] + [pltpu.VMEM] * 3 + [pl.ANY] * 2,

time: 216 us -> 214 us (level)
  waiting for transfers between devices: 53 us -> 57 us
  Pallas kernels: 11.7 us -> 8.85 us
  local copies, waits for them, and re-layouts: 16.3 us -> 13.8 us
    all_to_all x6, waiting for transfers between devices: 52.3 us -> 56.2 us  [exchange(): return lax.all_to_all(parts, axis, 0, 0, tiled=True)]
    pallas_call x2, Pallas kernels: 11.7 us -> 8.85 us  [the longest x1 5.45 us: body(): streaming(first_kernel, (0, last), TILES[0], early, (2, few, xs * pair),...]
  transfers between devices with their start and end apart: 8 -> 8, of which waited for: 6 -> 6; matrix products, arithmetic and copies ran while one was open for 7% -> 6% of each run, Pallas kernels for 3% -> 3%
where the time goes in v9:
time: 214 us; the launch traced here: 213 us
  blocking collectives  75.8 us (35%)
  waiting for transfers between devices  57 us (27%)
  starting transfers between devices  41.2 us (19%)
  local copies, waits for them, and re-layouts  13.8 us (6%)
  between operations  13.8 us (6%)
  Pallas kernels  8.85 us (4%)
  matrix products  2.36 us (1%)
    all_to_all x4, blocking collectives, exchange(): return lax.all_to_all(parts, axis, 0, 0, tiled=True)  64.6 us
    all_to_all x6, waiting for transfers between devices, exchange(): return lax.all_to_all(parts, axis, 0, 0, tiled=True)  56.2 us
    all_to_all x6, starting transfers between devices, exchange(): return lax.all_to_all(parts, axis, 0, 0, tiled=True)  41.2 us
    all_gather x1, blocking collectives, body(): together = lax.all_gather(given[0], 'c', axis=0, tiled=True).T  8.37 us
    pallas_call x1, Pallas kernels, body(): streaming(first_kernel, (0, last), TILES[0], early, (2, few, xs * pair),...  5.45 us
  transfers between devices with their start and end apart: 8, of which 6 were waited for; matrix products, arithmetic and copies ran while one was open for 6% of the time, Pallas kernels for 3%

profile of v9, /device:TPU:1, one launch (start us, length us, event | category | flops | bytes accessed | tf_op | source)
XLA Modules:
  0.0 213.1 jit_solution(5743989270953431543)
XLA Ops:
  6.5 3.1 %fusion.45 = (bf16[1,1,64,8192]{3,2,1,0:T(8,128)(2,1)}, bf16[1,1,64,8192]{3,2,1,0:T(8,128)(2,1)}) fusion(bf16[2,1,64,8192]{3,2,1,0:T(8,128)(2,1)} %param.2), kind=kLoop, calls=%fused_computation.89 | loop fusion | bytes 4194304 | tf_op jit(solution)/shard_map/slice | solution.py:133
  9.6 0.0 all-gather.9.cloned.1.call-start
  9.7 0.7 all-gather.9.cloned.1.call-update
  10.4 0.1 copy-done.1
  10.5 8.4 %all-gather = f32[1,1,128,128]{3,1,0,2:T(1,128)S(1)} all-gather(f32[1,1,64,128]{3,1,0,2:T(1,128)S(1)} %bitcast.154), channel_id=2, replica_groups=mesh['yl'=4,'x'=4,'z'=8,'yh'=2,'c'=2] {'c'}, dimensions={2}, use_global_device_ids=true | all-gather | bytes 98304 | tf_op jit(solution)/shard_map/all_gather | solution.py:144
  18.8 0.1 copy.14
  18.9 0.9 broadcast_in_dim.62
  19.8 10.0 %all-to-all-start = ((f32[16,64,128]{2,1,0:T(8,128)}), f32[16,64,128]{2,1,0:T(8,128)S(1)}, u32[]{:S(2)}, u32[]{:S(2)}) async-start(f32[16,64,128]{2,1,0:T(8,128)} %broadcast_in_dim.62), calls=%async_computation | async-start | bytes 1048576 | tf_op jit(solution)/shard_map/all_to_all | solution.py:16
  29.8 1.0 slice.130
  30.8 2.8 %all-gather.1 = bf16[1,128,2048]{2,1,0:T(8,128)(2,1)S(1)} all-gather(bf16[1,64,2048]{2,1,0:T(8,128)(2,1)S(1)} %slice.130), channel_id=3, replica_groups=mesh['yl'=4,'x'=4,'z'=8,'yh'=2,'c'=2] {'c'}, dimensions={1}, use_global_device_ids=true | all-gather | bytes 786432 | tf_op jit(solution)/shard_map/all_gather | solution.py:149
  33.7 11.1 %all-to-all-done = f32[16,64,128]{2,1,0:T(8,128)S(1)} async-done(((f32[16,64,128]{2,1,0:T(8,128)}), f32[16,64,128]{2,1,0:T(8,128)S(1)}, u32[]{:S(2)}, u32[]{:S(2)}) %all-to-all-start) | async-done | bytes 524320 | tf_op jit(solution)/shard_map/all_to_all | solution.py:16
  44.8 0.1 reduce-precision_convert_fusion.1
  44.9 0.4 fusion.4
  45.3 8.5 %all_to_all.50 = f32[4,16,128]{2,1,0:T(8,128)S(1)} all-to-all(f32[4,16,128]{2,1,0:T(8,128)S(1)} %bitcast.156), channel_id=1, replica_groups=mesh['yl'=4,'x'=4,'z'=8,'yh'=2,'c'=2] {'x'}, dimensions={0} | all-to-all | bytes 65536 | tf_op jit(solution)/shard_map/all_to_all | solution.py:16
  53.9 23.9 %all_to_all.51 = bf16[64,16,128]{2,1,0:T(8,128)(2,1)S(1)} all-to-all(bf16[64,16,128]{2,1,0:T(8,128)(2,1)S(1)} %broadcast_in_dim.64), channel_id=1, replica_groups=mesh['yl'=4,'x'=4,'z'=8,'yh'=2,'c'=2] {'yl','z','yh'}, dimensions={0} | all-to-all | bytes 524288 | tf_op jit(solution)/shard_map/all_to_all | solution.py:16
  77.8 0.0 all-gather.7.cloned.1.call-done
  77.9 1.5 slice.134
  79.4 0.5 fusion
  79.9 0.7 broadcast_in_dim.66
  80.6 5.3 %all-to-all-start.3 = ((f32[16,16,128]{2,1,0:T(8,128)}), f32[16,16,128]{2,1,0:T(8,128)S(1)}, u32[]{:S(2)}, u32[]{:S(2)}) async-start(f32[16,16,128]{2,1,0:T(8,128)} %broadcast_in_dim.66), calls=%async_computation.3 | async-start | bytes 262144 | tf_op jit(solution)/shard_map/all_to_all | solution.py:16
  85.9 1.8 fusion.44
  87.7 10.1 %all-to-all-done.3 = f32[16,16,128]{2,1,0:T(8,128)S(1)} async-done(((f32[16,16,128]{2,1,0:T(8,128)}), f32[16,16,128]{2,1,0:T(8,128)S(1)}, u32[]{:S(2)}, u32[]{:S(2)}) %all-to-all-start.3) | async-done | bytes 131104 | tf_op jit(solution)/shard_map/all_to_all | solution.py:16
  97.8 0.3 fusion.12
  98.1 0.7 broadcast_in_dim.67
  98.8 4.6 %all-to-all-start.4 = ((bf16[64,16,128]{2,1,0:T(8,128)(2,1)}), bf16[64,16,128]{2,1,0:T(8,128)(2,1)S(1)}, u32[]{:S(2)}, u32[]{:S(2)}) async-start(bf16[64,16,128]{2,1,0:T(8,128)(2,1)} %broadcast_in_dim.67), calls=%async_computation.4 | async-start | bytes 524288 | tf_op jit(solution)/shard_map/all_to_all | solution.py:16
  103.4 1.3 slice.139
  104.7 11.3 %all-to-all-done.4 = bf16[64,16,128]{2,1,0:T(8,128)(2,1)S(1)} async-done(((bf16[64,16,128]{2,1,0:T(8,128)(2,1)}), bf16[64,16,128]{2,1,0:T(8,128)(2,1)S(1)}, u32[]{:S(2)}, u32[]{:S(2)}) %all-to-all-start.4) | async-done | bytes 262176 | tf_op jit(solution)/shard_map/all_to_all | solution.py:16
  116.2 0.4 fusion.1
  116.6 14.6 %all_to_all.52 = f32[16,16,128]{2,1,0:T(8,128)S(1)} all-to-all(f32[16,16,128]{2,1,0:T(8,128)S(1)} %broadcast_in_dim.69), channel_id=1, replica_groups=mesh['yl'=4,'x'=4,'z'=8,'yh'=2,'c'=2] {'z','yh'}, dimensions={0} | all-to-all | bytes 262144 | tf_op jit(solution)/shard_map/all_to_all | solution.py:16
  131.2 0.3 fusion.18
  131.5 17.7 %all_to_all.53 = bf16[64,16,128]{2,1,0:T(8,128)(2,1)S(1)} all-to-all(bf16[64,16,128]{2,1,0:T(8,128)(2,1)S(1)} %broadcast_in_dim.70), channel_id=1, replica_groups=mesh['yl'=4,'x'=4,'z'=8,'yh'=2,'c'=2] {'yl','z','yh'}, dimensions={0} | all-to-all | bytes 524288 | tf_op jit(solution)/shard_map/all_to_all | solution.py:16
  149.2 0.2 fusion.3
  149.5 0.7 broadcast_in_dim.72
  150.2 3.5 %all-to-all-start.7 = ((f32[16,16,128]{2,1,0:T(8,128)}), f32[16,16,128]{2,1,0:T(8,128)S(1)}, u32[]{:S(2)}, u32[]{:S(2)}) async-start(f32[16,16,128]{2,1,0:T(8,128)} %broadcast_in_dim.72), calls=%async_computation.7 | async-start | bytes 262144 | tf_op jit(solution)/shard_map/all_to_all | solution.py:16
  153.7 11.7 %all-to-all-done.7 = f32[16,16,128]{2,1,0:T(8,128)S(1)} async-done(((f32[16,16,128]{2,1,0:T(8,128)}), f32[16,16,128]{2,1,0:T(8,128)S(1)}, u32[]{:S(2)}, u32[]{:S(2)}) %all-to-all-start.7) | async-done | bytes 131104 | tf_op jit(solution)/shard_map/all_to_all | solution.py:16
  165.5 0.3 fusion.24
  165.8 0.7 broadcast_in_dim.73
  166.5 4.6 %all-to-all-start.8 = ((bf16[64,16,128]{2,1,0:T(8,128)(2,1)}), bf16[64,16,128]{2,1,0:T(8,128)(2,1)S(1)}, u32[]{:S(2)}, u32[]{:S(2)}) async-start(bf16[64,16,128]{2,1,0:T(8,128)(2,1)} %broadcast_in_dim.73), calls=%async_computation.8 | async-start | bytes 524288 | tf_op jit(solution)/shard_map/all_to_all | solution.py:16
  171.2 0.0 all-gather.9.cloned.1.call-done
  171.2 5.5 %shard_map.28.sofar = f32[2,16,512]{2,1,0:T(8,128)S(1)} custom-call(bf16[16,2048]{1,0:T(8,128)(2,1)S(1)} %bitcast.135, bf16[16,2048]{1,0:T(8,128)(2,1)S(1)} %bitcast.136, bf16[16,2048]{1,0:T(8,128)(2,1)S(1)} %copy_bitcast_fusion.2.refs_2_, bf16[8,64,8192]{2,1,0:T(8,128)(2,1)} %bitcast.140, bf16[8,64,8192]{2,1,0:T(8,128)(2,1)} %bitcast.142), custom_call_target="tpu_custom_call" | custom-call | flops 201326592 | bytes 12582912 | tf_op jit(solution)/shard_map/pallas_call | solution.py:168
  176.7 6.8 %all-to-all-done.8.got = bf16[64,16,128]{2,1,0:T(8,128)(2,1)S(1)} async-done(((bf16[64,16,128]{2,1,0:T(8,128)(2,1)}), bf16[64,16,128]{2,1,0:T(8,128)(2,1)S(1)}, u32[]{:S(2)}, u32[]{:S(2)}) %all-to-all-start.8) | async-done | bytes 262176 | tf_op jit(solution)/shard_map/all_to_all | solution.py:16
  183.5 3.4 %shard_map.29 = f32[8,2,16,128]{3,2,1,0:T(8,128)} custom-call(s32[1]{0:T(128)} %bitcast.owner_ref, bf16[64,16,128]{2,1,0:T(8,128)(2,1)S(1)} %all-to-all-done.8.got, f32[2,16,512]{2,1,0:T(8,128)S(1)} %shard_map.28.sofar, f32[4,16,128]{2,1,0:T(8,128)S(1)} %pad_maximum_fusion.solved, bf16[8,64,8192]{2,1,0:T(8,128)(2,1)} %bitcast.141, bf16[8,64,8192]{2,1,0:T(8,128)(2,1)} %bitcast.143), custom_call_target="tpu_custom_call" | custom-call | flops 67108864 | bytes 4194304 | tf_op jit(solution)/shard_map/pallas_call | solution.py:176
  186.9 13.1 %all-to-all-start.9 = ((f32[8,2,16,128]{3,2,1,0:T(8,128)}), f32[8,2,16,128]{3,2,1,0:T(8,128)S(1)}, u32[]{:S(2)}, u32[]{:S(2)}) async-start(f32[8,2,16,128]{3,2,1,0:T(8,128)} %shard_map.29), calls=%async_computation.9 | async-start | bytes 262144 | tf_op jit(solution)/shard_map/all_to_all | solution.py:16
  200.0 0.1 copy.25
  200.1 0.1 copy.26
  200.2 5.1 %all-to-all-done.9 = f32[8,2,16,128]{3,2,1,0:T(8,128)S(1)} async-done(((f32[8,2,16,128]{3,2,1,0:T(8,128)}), f32[8,2,16,128]{3,2,1,0:T(8,128)S(1)}, u32[]{:S(2)}, u32[]{:S(2)}) %all-to-all-start.9) | async-done | bytes 131104 | tf_op jit(solution)/shard_map/all_to_all | solution.py:16
  205.4 0.1 dynamic-slice_bitcast_fusion
  205.5 0.7 copy.24
  (35 shorter events, 0.5 us)
Async XLA Ops:
  6.5 71.3 %all-gather.7.cloned.1.call-start = ((), (), s32[]{:S(2)}) async-start(), calls=%async_computation.10 | async-start | bytes 9437184 | tf_op jit(solution)/shard_map/all_gather | solution.py:132
  9.6 0.8 copy-start.1
  9.6 161.5 %all-gather.9.cloned.1.call-start = ((), (), s32[]{:S(2)}) async-start(), calls=%async_computation.11 | async-start | bytes 9437184 | tf_op jit(solution)/shard_map/all_gather | solution.py:133
  19.8 25.0 %all-to-all-start = ((f32[16,64,128]{2,1,0:T(8,128)}), f32[16,64,128]{2,1,0:T(8,128)S(1)}, u32[]{:S(2)}, u32[]{:S(2)}) async-start(f32[16,64,128]{2,1,0:T(8,128)} %broadcast_in_dim.62), calls=%async_computation | async-start | bytes 1048576 | tf_op jit(solution)/shard_map/all_to_all | solution.py:16
  53.8 99.9 %copy-start = (f32[4,16,128]{2,1,0:T(8,128)}, f32[4,16,128]{2,1,0:T(8,128)S(1)}, u32[]{:S(2)}) copy-start(f32[4,16,128]{2,1,0:T(8,128)S(1)} %all_to_all.50) | copy-start | bytes 98308
  80.6 17.2 %all-to-all-start.3 = ((f32[16,16,128]{2,1,0:T(8,128)}), f32[16,16,128]{2,1,0:T(8,128)S(1)}, u32[]{:S(2)}, u32[]{:S(2)}) async-start(f32[16,16,128]{2,1,0:T(8,128)} %broadcast_in_dim.66), calls=%async_computation.3 | async-start | bytes 262144 | tf_op jit(solution)/shard_map/all_to_all | solution.py:16
  98.8 17.3 %all-to-all-start.4 = ((bf16[64,16,128]{2,1,0:T(8,128)(2,1)}), bf16[64,16,128]{2,1,0:T(8,128)(2,1)S(1)}, u32[]{:S(2)}, u32[]{:S(2)}) async-start(bf16[64,16,128]{2,1,0:T(8,128)(2,1)} %broadcast_in_dim.67), calls=%async_computation.4 | async-start | bytes 524288 | tf_op jit(solution)/shard_map/all_to_all | solution.py:16
  150.2 15.3 %all-to-all-start.7 = ((f32[16,16,128]{2,1,0:T(8,128)}), f32[16,16,128]{2,1,0:T(8,128)S(1)}, u32[]{:S(2)}, u32[]{:S(2)}) async-start(f32[16,16,128]{2,1,0:T(8,128)} %broadcast_in_dim.72), calls=%async_computation.7 | async-start | bytes 262144 | tf_op jit(solution)/shard_map/all_to_all | solution.py:16
  166.5 17.0 %all-to-all-start.8 = ((bf16[64,16,128]{2,1,0:T(8,128)(2,1)}), bf16[64,16,128]{2,1,0:T(8,128)(2,1)S(1)}, u32[]{:S(2)}, u32[]{:S(2)}) async-start(bf16[64,16,128]{2,1,0:T(8,128)(2,1)} %broadcast_in_dim.73), calls=%async_computation.8 | async-start | bytes 524288 | tf_op jit(solution)/shard_map/all_to_all | solution.py:16
  171.2 5.5 %slice-start = ((f32[4,16,128]{2,1,0:T(8,128)}), f32[1,16,128]{2,1,0:T(8,128)S(1)}, s32[]{:S(2)}) async-start(f32[4,16,128]{2,1,0:T(8,128)} %copy-done), calls=%async_computation.12 | async-start | bytes 16384 | tf_op jit(solution)/shard_map/slice | solution.py:155
  186.9 18.4 %all-to-all-start.9 = ((f32[8,2,16,128]{3,2,1,0:T(8,128)}), f32[8,2,16,128]{3,2,1,0:T(8,128)S(1)}, u32[]{:S(2)}, u32[]{:S(2)}) async-start(f32[8,2,16,128]{3,2,1,0:T(8,128)} %shard_map.29), calls=%async_computation.9 | async-start | bytes 262144 | tf_op jit(solution)/shard_map/all_to_all | solution.py:16
Sparse Core Ops, SparseCore 0:
  9.8 61.2 all-gather.6
  73.2 55.2 all-gather.8

commit v10 on v9

--- a/solution.py
+++ b/solution.py
@@ -44,12 +44,14 @@
 TILES = ((1024, 6), (512, 8))
 
 
-def stream(plan, early_ref, late_ref, held, sems, cases_of):
+def stream(plan, early_ref, all_ref, held, sems, cases_of):
     slots, tile = held.shape[0], held.shape[3]
 
     def copy(n):
         index, place = plan[n]
-        ref = (late_ref if index else early_ref).at[:, :, place : place + tile]
+        early = index == 0 and place < early_ref.shape[2]
+        ref = early_ref if early else all_ref.at[:, index]
+        ref = ref.at[:, :, place : place + tile]
         return pltpu.make_async_copy(ref, held.at[n % slots], sems.at[n % slots])
 
     for n in range(min(slots, len(plan))):
@@ -65,19 +67,19 @@
 
 
 def first_kernel(plan, *refs):
-    *whole, early_ref, late_ref, out_ref, held, sems = refs
-    block = whole[0].shape[1]
+    *got, early_ref, all_ref, out_ref, held, sems = refs
 
     def cases_of(place):
-        start = place % block
-        return whole[place // block][:, start : start + held.shape[3]]
-
-    total = stream(plan, early_ref, late_ref, held, sems, cases_of)
+        chips, _, pair = got[0].shape
+        part, chip = got[place // (chips * pair)], place // pair % chips
+        return jnp.concatenate([part[chip + n] for n in range(held.shape[3] // pair)], 1)
+
+    total = stream(plan, early_ref, all_ref, held, sems, cases_of)
     for index in range(2):
         out_ref[index] = total[index]
 
 
-def last_kernel(plan, owner_ref, got, sofar, solved, early_ref, late_ref, out, held, sems):
+def last_kernel(plan, owner_ref, got, sofar, solved, early_ref, all_ref, out, held, sems):
     pair = got.shape[2]
     xs = solved.shape[0]
 
@@ -85,7 +87,7 @@
         chip = (place - plan[0][1]) // pair
         return jnp.concatenate([got[chip + n] for n in range(held.shape[3] // pair)], 1)
 
-    total = stream(plan, early_ref, late_ref, held, sems, cases_of)
+    total = stream(plan, early_ref, all_ref, held, sems, cases_of)
     owner = owner_ref[0] == 0
     for x in range(xs):
         for index in range(2):
@@ -129,11 +131,13 @@
     few = cases // (xs * cores)
     pair = cores * share
 
-    early = lax.all_gather(stored[0], ("x", "c"), axis=0)
-    late = lax.all_gather(stored[1], ("x", "c"), axis=0)
+    last = width - block
+    early = lax.all_gather(stored[0, :, :last], ("x", "c"), axis=0)
+    everything = lax.all_gather(stored, ("x", "c"), axis=0)
 
     def panel(row, column):
-        part = early[:, :, column * block : (column + 1) * block]
+        span = slice(column * block, (column + 1) * block)
+        part = early[:, :, span] if span.start < last else everything[:, 0, :, span]
         return part.reshape(xs, pair, block)[row:].reshape(-1, block)
 
     def to_all(part, own_plane=True):
@@ -156,15 +160,15 @@
     state = state[1:]
     for step in range(1, steps):
         got = to_all(solved[-1].astype(jnp.bfloat16))
-        known.append(jnp.swapaxes(got, 0, 1).reshape(few, block))
-        update = times(known[-1], panel(step, step - 1))
+        known.append(got)
+        whole = jnp.swapaxes(got, 0, 1).reshape(few, block)
+        update = times(whole, panel(step, step - 1))
         update = update.reshape(few, steps - step, pair)
         state = state - jnp.swapaxes(update, 0, 1)
         solved.append(times_exact(gather_chips(state[0]), panel(step, step)[:pair]))
         state = state[1:]
 
     got = to_all(solved[-1].astype(jnp.bfloat16), False)
-    last = width - block
     sofar = streaming(
         first_kernel,
         (0, last),
@@ -172,7 +176,7 @@
         early,
         (2, few, xs * pair),
         [pltpu.VMEM] * len(known) + [pl.ANY] * 2,
-    )(*known, early, late)
+    )(*known, early, everything)
     both = streaming(
         last_kernel,
         (last, width),
@@ -180,7 +184,7 @@
         early,
         (xs * cores, 2, few, pair),
         [pltpu.SMEM] + [pltpu.VMEM] * 3 + [pl.ANY] * 2,
-    )(lax.axis_index("yl")[None], got, sofar, jnp.stack(solved), early, late)
+    )(lax.axis_index("yl")[None], got, sofar, jnp.stack(solved), early, everything)
     back = exchange(both, ("x", "c"))
     owner = lax.axis_index("yl") == 0
     back = jnp.swapaxes(back, 0, 1).reshape(2, cases, pair).transpose(0, 2, 1)

time: 214 us -> 214 us (level)
  blocking collectives: 75.8 us -> 90.1 us
  waiting for transfers between devices: 57 us -> 45.3 us
  starting transfers between devices: 41.2 us -> 38.8 us
    all_to_all x4 -> x5, blocking collectives: 64.6 us -> 79 us  [exchange(): return lax.all_to_all(parts, axis, 0, 0, tiled=True)]
    all_to_all x6 -> x5, waiting for transfers between devices: 56.2 us -> 44.6 us  [exchange(): return lax.all_to_all(parts, axis, 0, 0, tiled=True)]
    all_to_all x6 -> x5, starting transfers between devices: 41.2 us -> 38.8 us  [exchange(): return lax.all_to_all(parts, axis, 0, 0, tiled=True)]
  transfers between devices with their start and end apart: 8 -> 7, of which waited for: 6 -> 5; matrix products, arithmetic and copies ran while one was open for 6% -> 5% of each run, Pallas kernels for 3% -> 3%
where the time goes in v10:
time: 214 us; the launch traced here: 213 us
  blocking collectives  90.1 us (42%)
  waiting for transfers between devices  45.3 us (21%)
  starting transfers between devices  38.8 us (18%)
  between operations  13.7 us (6%)
  local copies, waits for them, and re-layouts  13.2 us (6%)
  Pallas kernels  8.88 us (4%)
  matrix products  2.36 us (1%)
    all_to_all x5, blocking collectives, exchange(): return lax.all_to_all(parts, axis, 0, 0, tiled=True)  79 us
    all_to_all x5, waiting for transfers between devices, exchange(): return lax.all_to_all(parts, axis, 0, 0, tiled=True)  44.6 us
    all_to_all x5, starting transfers between devices, exchange(): return lax.all_to_all(parts, axis, 0, 0, tiled=True)  38.8 us
    all_gather x1, blocking collectives, body(): together = lax.all_gather(given[0], 'c', axis=0, tiled=True).T  8.37 us
    pallas_call x1, Pallas kernels, body(): streaming(first_kernel, (0, last), TILES[0], early, (2, few, xs * pair),...  5.46 us
  transfers between devices with their start and end apart: 7, of which 5 were waited for; matrix products, arithmetic and copies ran while one was open for 5% of the time, Pallas kernels for 3%

profile of v10, /device:TPU:1, one launch (start us, length us, event | category | flops | bytes accessed | tf_op | source)
XLA Modules:
  0.0 212.8 jit_solution(1365073806479731166)
XLA Ops:
  6.5 2.1 slice.122
  8.6 0.0 all-gather.6.cloned.1.call-update
  8.6 0.0 all-gather.8.cloned.1.call-start
  8.7 0.7 all-gather.8.cloned.1.call-update
  9.4 0.1 copy-done.1
  9.5 8.4 %all-gather = f32[1,1,128,128]{3,1,0,2:T(1,128)S(1)} all-gather(f32[1,1,64,128]{3,1,0,2:T(1,128)S(1)} %bitcast.135), channel_id=2, replica_groups=mesh['yl'=4,'x'=4,'z'=8,'yh'=2,'c'=2] {'c'}, dimensions={2}, use_global_device_ids=true | all-gather | bytes 98304 | tf_op jit(solution)/shard_map/all_gather | solution.py:148
  17.8 0.1 copy.13
  17.9 0.9 broadcast_in_dim.62
  18.8 10.0 %all-to-all-start = ((f32[16,64,128]{2,1,0:T(8,128)}), f32[16,64,128]{2,1,0:T(8,128)S(1)}, u32[]{:S(2)}, u32[]{:S(2)}) async-start(f32[16,64,128]{2,1,0:T(8,128)} %broadcast_in_dim.62), calls=%async_computation | async-start | bytes 1048576 | tf_op jit(solution)/shard_map/all_to_all | solution.py:16
  28.8 1.0 slice.118
  29.8 2.8 %all-gather.1 = bf16[1,128,2048]{2,1,0:T(8,128)(2,1)S(1)} all-gather(bf16[1,64,2048]{2,1,0:T(8,128)(2,1)S(1)} %slice.118), channel_id=3, replica_groups=mesh['yl'=4,'x'=4,'z'=8,'yh'=2,'c'=2] {'c'}, dimensions={1}, use_global_device_ids=true | all-gather | bytes 786432 | tf_op jit(solution)/shard_map/all_gather | solution.py:153
  32.6 11.2 %all-to-all-done = f32[16,64,128]{2,1,0:T(8,128)S(1)} async-done(((f32[16,64,128]{2,1,0:T(8,128)}), f32[16,64,128]{2,1,0:T(8,128)S(1)}, u32[]{:S(2)}, u32[]{:S(2)}) %all-to-all-start) | async-done | bytes 524320 | tf_op jit(solution)/shard_map/all_to_all | solution.py:16
  43.8 0.1 reduce-precision_convert_fusion.1
  43.9 0.4 fusion.4
  44.3 8.5 %all_to_all.50 = f32[4,16,128]{2,1,0:T(8,128)S(1)} all-to-all(f32[4,16,128]{2,1,0:T(8,128)S(1)} %bitcast.137), channel_id=1, replica_groups=mesh['yl'=4,'x'=4,'z'=8,'yh'=2,'c'=2] {'x'}, dimensions={0} | all-to-all | bytes 65536 | tf_op jit(solution)/shard_map/all_to_all | solution.py:16
  52.8 23.9 %all_to_all.51 = bf16[64,16,128]{2,1,0:T(8,128)(2,1)S(1)} all-to-all(bf16[64,16,128]{2,1,0:T(8,128)(2,1)S(1)} %broadcast_in_dim.64), channel_id=1, replica_groups=mesh['yl'=4,'x'=4,'z'=8,'yh'=2,'c'=2] {'yl','z','yh'}, dimensions={0} | all-to-all | bytes 524288 | tf_op jit(solution)/shard_map/all_to_all | solution.py:16
  76.8 0.0 all-gather.6.cloned.1.call-done.refs_3_.early_ref
  76.9 1.6 slice.123
  78.5 0.5 fusion
  79.0 0.7 broadcast_in_dim.66
  79.7 3.5 %all-to-all-start.3 = ((f32[16,16,128]{2,1,0:T(8,128)}), f32[16,16,128]{2,1,0:T(8,128)S(1)}, u32[]{:S(2)}, u32[]{:S(2)}) async-start(f32[16,16,128]{2,1,0:T(8,128)} %broadcast_in_dim.66), calls=%async_computation.3 | async-start | bytes 262144 | tf_op jit(solution)/shard_map/all_to_all | solution.py:16
  83.2 1.6 fusion.46
  84.8 10.3 %all-to-all-done.3 = f32[16,16,128]{2,1,0:T(8,128)S(1)} async-done(((f32[16,16,128]{2,1,0:T(8,128)}), f32[16,16,128]{2,1,0:T(8,128)S(1)}, u32[]{:S(2)}, u32[]{:S(2)}) %all-to-all-start.3) | async-done | bytes 131104 | tf_op jit(solution)/shard_map/all_to_all | solution.py:16
  95.1 0.3 fusion.12
  95.4 0.8 broadcast_in_dim.67
  96.2 4.6 %all-to-all-start.4 = ((bf16[64,16,128]{2,1,0:T(8,128)(2,1)}), bf16[64,16,128]{2,1,0:T(8,128)(2,1)S(1)}, u32[]{:S(2)}, u32[]{:S(2)}) async-start(bf16[64,16,128]{2,1,0:T(8,128)(2,1)} %broadcast_in_dim.67), calls=%async_computation.4 | async-start | bytes 524288 | tf_op jit(solution)/shard_map/all_to_all | solution.py:16
  100.8 1.3 slice.128
  102.1 11.1 %all-to-all-done.4 = bf16[64,16,128]{2,1,0:T(8,128)(2,1)S(1)} async-done(((bf16[64,16,128]{2,1,0:T(8,128)(2,1)}), bf16[64,16,128]{2,1,0:T(8,128)(2,1)S(1)}, u32[]{:S(2)}, u32[]{:S(2)}) %all-to-all-start.4) | async-done | bytes 262176 | tf_op jit(solution)/shard_map/all_to_all | solution.py:16
  113.3 0.4 fusion.1
  113.7 14.8 %all_to_all.52 = f32[16,16,128]{2,1,0:T(8,128)S(1)} all-to-all(f32[16,16,128]{2,1,0:T(8,128)S(1)} %broadcast_in_dim.69), channel_id=1, replica_groups=mesh['yl'=4,'x'=4,'z'=8,'yh'=2,'c'=2] {'z','yh'}, dimensions={0} | all-to-all | bytes 262144 | tf_op jit(solution)/shard_map/all_to_all | solution.py:16
  128.5 0.3 fusion.18
  128.9 17.1 %all_to_all.53 = bf16[64,16,128]{2,1,0:T(8,128)(2,1)S(1)} all-to-all(bf16[64,16,128]{2,1,0:T(8,128)(2,1)S(1)} %broadcast_in_dim.70), channel_id=1, replica_groups=mesh['yl'=4,'x'=4,'z'=8,'yh'=2,'c'=2] {'yl','z','yh'}, dimensions={0} | all-to-all | bytes 524288 | tf_op jit(solution)/shard_map/all_to_all | solution.py:16
  146.0 0.2 fusion.3
  146.3 14.7 %all_to_all.54 = f32[16,16,128]{2,1,0:T(8,128)S(1)} all-to-all(f32[16,16,128]{2,1,0:T(8,128)S(1)} %broadcast_in_dim.72), channel_id=1, replica_groups=mesh['yl'=4,'x'=4,'z'=8,'yh'=2,'c'=2] {'z','yh'}, dimensions={0} | all-to-all | bytes 262144 | tf_op jit(solution)/shard_map/all_to_all | solution.py:16
  161.1 0.0 all-gather.8.cloned.1.call-done
  161.1 1.1 slice.134
  162.2 0.3 fusion.24
  162.5 0.8 broadcast_in_dim.73
  163.2 6.5 %all-to-all-start.8 = ((bf16[64,16,128]{2,1,0:T(8,128)(2,1)}), bf16[64,16,128]{2,1,0:T(8,128)(2,1)S(1)}, u32[]{:S(2)}, u32[]{:S(2)}) async-start(bf16[64,16,128]{2,1,0:T(8,128)(2,1)} %broadcast_in_dim.73), calls=%async_computation.8 | async-start | bytes 524288 | tf_op jit(solution)/shard_map/all_to_all | solution.py:16
  169.8 5.5 %shard_map.28.sofar = f32[2,16,512]{2,1,0:T(8,128)S(1)} custom-call(bf16[16,16,128]{2,1,0:T(8,128)(2,1)S(1)} %get-tuple-element.15.refs_0_, bf16[16,16,128]{2,1,0:T(8,128)(2,1)S(1)} %get-tuple-element.13.refs_1_, bf16[16,16,128]{2,1,0:T(8,128)(2,1)S(1)} %get-tuple-element.11.refs_2_, bf16[8,64,6144]{2,1,0:T(8,128)(2,1)} %all-gather.6.cloned.1.call-done.refs_3_.early_ref, ...), custom_call_target="tpu_custom_call" | custom-call | flops 201326592 | bytes 12582912 | tf_op jit(solution)/shard_map/pallas_call | solution.py:172
  175.3 6.9 %all-to-all-done.8.got = bf16[64,16,128]{2,1,0:T(8,128)(2,1)S(1)} async-done(((bf16[64,16,128]{2,1,0:T(8,128)(2,1)}), bf16[64,16,128]{2,1,0:T(8,128)(2,1)S(1)}, u32[]{:S(2)}, u32[]{:S(2)}) %all-to-all-start.8) | async-done | bytes 262176 | tf_op jit(solution)/shard_map/all_to_all | solution.py:16
  182.2 3.4 %shard_map.29 = f32[8,2,16,128]{3,2,1,0:T(8,128)} custom-call(s32[1]{0:T(128)} %bitcast.owner_ref, bf16[64,16,128]{2,1,0:T(8,128)(2,1)S(1)} %all-to-all-done.8.got, f32[2,16,512]{2,1,0:T(8,128)S(1)} %shard_map.28.sofar, f32[4,16,128]{2,1,0:T(8,128)S(1)} %pad_maximum_fusion.solved, bf16[8,64,6144]{2,1,0:T(8,128)(2,1)} %all-gather.6.cloned.1.call-done.refs_3_.early_ref, ...), custom_call_target="tpu_custom_call" | custom-call | flops 67108864 | bytes 4194304 | tf_op jit(solution)/shard_map/pallas_call | solution.py:180
  185.7 14.1 %all-to-all-start.9 = ((f32[8,2,16,128]{3,2,1,0:T(8,128)}), f32[8,2,16,128]{3,2,1,0:T(8,128)S(1)}, u32[]{:S(2)}, u32[]{:S(2)}) async-start(f32[8,2,16,128]{3,2,1,0:T(8,128)} %shard_map.29), calls=%async_computation.9 | async-start | bytes 262144 | tf_op jit(solution)/shard_map/all_to_all | solution.py:16
  199.8 0.1 copy.24
  199.9 0.1 copy.25
  200.0 5.1 %all-to-all-done.9 = f32[8,2,16,128]{3,2,1,0:T(8,128)S(1)} async-done(((f32[8,2,16,128]{3,2,1,0:T(8,128)}), f32[8,2,16,128]{3,2,1,0:T(8,128)S(1)}, u32[]{:S(2)}, u32[]{:S(2)}) %all-to-all-start.9) | async-done | bytes 131104 | tf_op jit(solution)/shard_map/all_to_all | solution.py:16
  205.1 0.1 dynamic-slice_bitcast_fusion
  205.2 0.7 copy.23
  (33 shorter events, 0.5 us)
Async XLA Ops:
  6.5 70.3 %all-gather.6.cloned.1.call-start = ((), (), s32[]{:S(2)}) async-start(), calls=%async_computation.10 | async-start | bytes 7077888 | tf_op jit(solution)/shard_map/all_gather | solution.py:135
  8.6 0.8 copy-start.1
  8.6 152.4 %all-gather.8.cloned.1.call-start = ((), (), s32[]{:S(2)}) async-start(), calls=%async_computation.11 | async-start | bytes 18874368 | tf_op jit(solution)/shard_map/all_gather | solution.py:136
  18.8 25.0 %all-to-all-start = ((f32[16,64,128]{2,1,0:T(8,128)}), f32[16,64,128]{2,1,0:T(8,128)S(1)}, u32[]{:S(2)}, u32[]{:S(2)}) async-start(f32[16,64,128]{2,1,0:T(8,128)} %broadcast_in_dim.62), calls=%async_computation | async-start | bytes 1048576 | tf_op jit(solution)/shard_map/all_to_all | solution.py:16
  52.8 117.0 %copy-start = (f32[4,16,128]{2,1,0:T(8,128)}, f32[4,16,128]{2,1,0:T(8,128)S(1)}, u32[]{:S(2)}) copy-start(f32[4,16,128]{2,1,0:T(8,128)S(1)} %all_to_all.50) | copy-start | bytes 98308
  79.7 15.4 %all-to-all-start.3 = ((f32[16,16,128]{2,1,0:T(8,128)}), f32[16,16,128]{2,1,0:T(8,128)S(1)}, u32[]{:S(2)}, u32[]{:S(2)}) async-start(f32[16,16,128]{2,1,0:T(8,128)} %broadcast_in_dim.66), calls=%async_computation.3 | async-start | bytes 262144 | tf_op jit(solution)/shard_map/all_to_all | solution.py:16
  96.2 17.0 %all-to-all-start.4 = ((bf16[64,16,128]{2,1,0:T(8,128)(2,1)}), bf16[64,16,128]{2,1,0:T(8,128)(2,1)S(1)}, u32[]{:S(2)}, u32[]{:S(2)}) async-start(bf16[64,16,128]{2,1,0:T(8,128)(2,1)} %broadcast_in_dim.67), calls=%async_computation.4 | async-start | bytes 524288 | tf_op jit(solution)/shard_map/all_to_all | solution.py:16
  163.2 19.0 %all-to-all-start.8 = ((bf16[64,16,128]{2,1,0:T(8,128)(2,1)}), bf16[64,16,128]{2,1,0:T(8,128)(2,1)S(1)}, u32[]{:S(2)}, u32[]{:S(2)}) async-start(bf16[64,16,128]{2,1,0:T(8,128)(2,1)} %broadcast_in_dim.73), calls=%async_computation.8 | async-start | bytes 524288 | tf_op jit(solution)/shard_map/all_to_all | solution.py:16
  169.8 5.5 %slice-start = ((f32[4,16,128]{2,1,0:T(8,128)}), f32[1,16,128]{2,1,0:T(8,128)S(1)}, s32[]{:S(2)}) async-start(f32[4,16,128]{2,1,0:T(8,128)} %copy-done), calls=%async_computation.12 | async-start | bytes 16384 | tf_op jit(solution)/shard_map/slice | solution.py:159
  185.7 19.4 %all-to-all-start.9 = ((f32[8,2,16,128]{3,2,1,0:T(8,128)}), f32[8,2,16,128]{3,2,1,0:T(8,128)S(1)}, u32[]{:S(2)}, u32[]{:S(2)}) async-start(f32[8,2,16,128]{3,2,1,0:T(8,128)} %shard_map.29), calls=%async_computation.9 | async-start | bytes 262144 | tf_op jit(solution)/shard_map/all_to_all | solution.py:16
Sparse Core Ops, SparseCore 0:
  9.5 52.4 all-gather.5
  64.2 90.4 all-gather.7

commit v11 on v9

--- a/solution.py
+++ b/solution.py
@@ -65,12 +65,12 @@
 
 
 def first_kernel(plan, *refs):
-    *whole, early_ref, late_ref, out_ref, held, sems = refs
-    block = whole[0].shape[1]
+    got, early_ref, late_ref, out_ref, held, sems = refs
 
     def cases_of(place):
-        start = place % block
-        return whole[place // block][:, start : start + held.shape[3]]
+        _, chips, _, pair = got.shape
+        part, chip = got.at[place // (chips * pair)], place // pair % chips
+        return jnp.concatenate([part[chip + n] for n in range(held.shape[3] // pair)], 1)
 
     total = stream(plan, early_ref, late_ref, held, sems, cases_of)
     for index in range(2):
@@ -129,6 +129,7 @@
     few = cases // (xs * cores)
     pair = cores * share
 
+    last = width - block
     early = lax.all_gather(stored[0], ("x", "c"), axis=0)
     late = lax.all_gather(stored[1], ("x", "c"), axis=0)
 
@@ -136,10 +137,7 @@
         part = early[:, :, column * block : (column + 1) * block]
         return part.reshape(xs, pair, block)[row:].reshape(-1, block)
 
-    def to_all(part, own_plane=True):
-        planes = ("yl",) + CHIPS
-        got = exchange(repeat(part, lax.axis_size(planes)), planes)
-        return got[: lax.axis_size(CHIPS)] if own_plane else got
+    chips = lax.axis_size(CHIPS)
 
     together = lax.all_gather(given[0], "c", axis=0, tiled=True).T
     mine = lax.dynamic_index_in_dim(
@@ -155,24 +153,28 @@
     solved, known = [state[0]], []
     state = state[1:]
     for step in range(1, steps):
-        got = to_all(solved[-1].astype(jnp.bfloat16))
-        known.append(jnp.swapaxes(got, 0, 1).reshape(few, block))
-        update = times(known[-1], panel(step, step - 1))
+        got = exchange(repeat(solved[-1].astype(jnp.bfloat16), chips), CHIPS)
+        known.append(got)
+        whole = jnp.swapaxes(got, 0, 1).reshape(few, block)
+        update = times(whole, panel(step, step - 1))
         update = update.reshape(few, steps - step, pair)
         state = state - jnp.swapaxes(update, 0, 1)
         solved.append(times_exact(gather_chips(state[0]), panel(step, step)[:pair]))
         state = state[1:]
 
-    got = to_all(solved[-1].astype(jnp.bfloat16), False)
-    last = width - block
+    known = lax.all_gather(jnp.stack(known), "yl", axis=0)[0]
+    none = jnp.minimum(jnp.abs(known[0, 0, :1].astype(jnp.float32)), 0.0)
+    planes = ("yl",) + CHIPS
+    got = (solved[-1] + none).astype(jnp.bfloat16)
+    got = exchange(repeat(got, lax.axis_size(planes)), planes)
     sofar = streaming(
         first_kernel,
         (0, last),
         TILES[0],
         early,
         (2, few, xs * pair),
-        [pltpu.VMEM] * len(known) + [pl.ANY] * 2,
-    )(*known, early, late)
+        [pltpu.VMEM] + [pl.ANY] * 2,
+    )(known, early, late)
     both = streaming(
         last_kernel,
         (last, width),

time: 214 us -> 218 us (1.019)
  waiting for transfers between devices: 57 us -> 44.5 us
  blocking collectives: 75.8 us -> 85.3 us
  starting transfers between devices: 41.2 us -> 48.1 us
    all_gather x0 -> x1, blocking collectives: none -> 16.4 us  [body(): known = lax.all_gather(jnp.stack(known), 'yl', axis=0)[0]]
    all_to_all x6, waiting for transfers between devices: 56.2 us -> 43.7 us  [exchange(): return lax.all_to_all(parts, axis, 0, 0, tiled=True)]
    all_to_all x6, starting transfers between devices: 41.2 us -> 48 us  [exchange(): return lax.all_to_all(parts, axis, 0, 0, tiled=True)]
    all_to_all x4, blocking collectives: 64.6 us -> 57.8 us  [exchange(): return lax.all_to_all(parts, axis, 0, 0, tiled=True)]
    slice x2 -> x3, local copies, waits for them, and re-layouts: 2.81 us -> 4.56 us  [panel(): return part.reshape(xs, pair, block)[row:].reshape(-1, block)]
  transfers between devices with their start and end apart: 8 -> 8, of which waited for: 6 -> 5; matrix products, arithmetic and copies ran while one was open for 6% -> 6% of each run, Pallas kernels for 3% -> 3%
where the time goes in v11:
time: 218 us; the launch traced here: 217 us
  blocking collectives  85.3 us (39%)
  starting transfers between devices  48.1 us (22%)
  waiting for transfers between devices  44.5 us (20%)
  between operations  13.7 us (6%)
  local copies, waits for them, and re-layouts  13.6 us (6%)
  Pallas kernels  8.87 us (4%)
  matrix products  2.37 us (1%)
    all_to_all x4, blocking collectives, exchange(): return lax.all_to_all(parts, axis, 0, 0, tiled=True)  57.8 us
    all_to_all x6, starting transfers between devices, exchange(): return lax.all_to_all(parts, axis, 0, 0, tiled=True)  48 us
    all_to_all x6, waiting for transfers between devices, exchange(): return lax.all_to_all(parts, axis, 0, 0, tiled=True)  43.7 us
    all_gather x1, blocking collectives, body(): known = lax.all_gather(jnp.stack(known), 'yl', axis=0)[0]  16.4 us
    all_gather x1, blocking collectives, body(): together = lax.all_gather(given[0], 'c', axis=0, tiled=True).T  8.37 us
    pallas_call x1, Pallas kernels, body(): streaming(first_kernel, (0, last), TILES[0], early, (2, few, xs * pair),...  5.45 us
    slice x3, local copies, waits for them, and re-layouts, panel(): return part.reshape(xs, pair, block)[row:].reshape(-1, block)  4.56 us
  transfers between devices with their start and end apart: 8, of which 5 were waited for; matrix products, arithmetic and copies ran while one was open for 6% of the time, Pallas kernels for 3%

profile of v11, /device:TPU:1, one launch (start us, length us, event | category | flops | bytes accessed | tf_op | source)
XLA Modules:
  0.0 216.8 jit_solution(5935516365957579780)
XLA Ops:
  6.5 3.1 %fusion.49 = (bf16[1,1,64,8192]{3,2,1,0:T(8,128)(2,1)}, bf16[1,1,64,8192]{3,2,1,0:T(8,128)(2,1)}) fusion(bf16[2,1,64,8192]{3,2,1,0:T(8,128)(2,1)} %param.2), kind=kLoop, calls=%fused_computation.88 | loop fusion | bytes 4194304 | tf_op jit(solution)/shard_map/slice | solution.py:134
  9.6 0.0 all-gather.10.cloned.1.call-start
  9.7 0.7 all-gather.10.cloned.1.call-update
  10.4 0.1 copy-done.1
  10.5 8.4 %all-gather = f32[1,1,128,128]{3,1,0,2:T(1,128)S(1)} all-gather(f32[1,1,64,128]{3,1,0,2:T(1,128)S(1)} %bitcast.149), channel_id=2, replica_groups=mesh['yl'=4,'x'=4,'z'=8,'yh'=2,'c'=2] {'c'}, dimensions={2}, use_global_device_ids=true | all-gather | bytes 98304 | tf_op jit(solution)/shard_map/all_gather | solution.py:142
  18.8 0.1 copy.17
  19.0 0.9 broadcast_in_dim.62
  19.8 10.0 %all-to-all-start = ((f32[16,64,128]{2,1,0:T(8,128)}), f32[16,64,128]{2,1,0:T(8,128)S(1)}, u32[]{:S(2)}, u32[]{:S(2)}) async-start(f32[16,64,128]{2,1,0:T(8,128)} %broadcast_in_dim.62), calls=%async_computation | async-start | bytes 1048576 | tf_op jit(solution)/shard_map/all_to_all | solution.py:16
  29.9 1.0 slice.128
  30.9 2.8 %all-gather.1 = bf16[1,128,2048]{2,1,0:T(8,128)(2,1)S(1)} all-gather(bf16[1,64,2048]{2,1,0:T(8,128)(2,1)S(1)} %slice.128), channel_id=3, replica_groups=mesh['yl'=4,'x'=4,'z'=8,'yh'=2,'c'=2] {'c'}, dimensions={1}, use_global_device_ids=true | all-gather | bytes 786432 | tf_op jit(solution)/shard_map/all_gather | solution.py:147
  33.7 11.1 %all-to-all-done = f32[16,64,128]{2,1,0:T(8,128)S(1)} async-done(((f32[16,64,128]{2,1,0:T(8,128)}), f32[16,64,128]{2,1,0:T(8,128)S(1)}, u32[]{:S(2)}, u32[]{:S(2)}) %all-to-all-start) | async-done | bytes 524320 | tf_op jit(solution)/shard_map/all_to_all | solution.py:16
  44.8 0.1 reduce-precision_convert_fusion.1
  44.9 0.4 fusion.4
  45.3 8.5 %all_to_all.50 = f32[4,16,128]{2,1,0:T(8,128)S(1)} all-to-all(f32[4,16,128]{2,1,0:T(8,128)S(1)} %bitcast.151), channel_id=1, replica_groups=mesh['yl'=4,'x'=4,'z'=8,'yh'=2,'c'=2] {'x'}, dimensions={0} | all-to-all | bytes 65536 | tf_op jit(solution)/shard_map/all_to_all | solution.py:16
  53.8 20.7 %all_to_all.51 = bf16[16,16,128]{2,1,0:T(8,128)(2,1)S(1)} all-to-all(bf16[16,16,128]{2,1,0:T(8,128)(2,1)S(1)} %broadcast_in_dim.64), channel_id=1, replica_groups=mesh['yl'=4,'x'=4,'z'=8,'yh'=2,'c'=2] {'z','yh'}, dimensions={0} | all-to-all | bytes 131072 | tf_op jit(solution)/shard_map/all_to_all | solution.py:16
  74.6 0.0 all-gather.8.cloned.1.call-done
  74.6 1.5 slice.131
  76.2 0.5 fusion
  76.7 0.7 broadcast_in_dim.66
  77.3 8.6 %all-to-all-start.3 = ((f32[16,16,128]{2,1,0:T(8,128)}), f32[16,16,128]{2,1,0:T(8,128)S(1)}, u32[]{:S(2)}, u32[]{:S(2)}) async-start(f32[16,16,128]{2,1,0:T(8,128)} %broadcast_in_dim.66), calls=%async_computation.3 | async-start | bytes 262144 | tf_op jit(solution)/shard_map/all_to_all | solution.py:16
  85.9 1.8 fusion.48
  87.7 10.2 %all-to-all-done.3 = f32[16,16,128]{2,1,0:T(8,128)S(1)} async-done(((f32[16,16,128]{2,1,0:T(8,128)}), f32[16,16,128]{2,1,0:T(8,128)S(1)}, u32[]{:S(2)}, u32[]{:S(2)}) %all-to-all-start.3) | async-done | bytes 131104 | tf_op jit(solution)/shard_map/all_to_all | solution.py:16
  97.9 0.3 fusion.12
  98.2 0.6 broadcast_in_dim.67
  98.9 3.9 %all-to-all-start.4 = ((bf16[16,16,128]{2,1,0:T(8,128)(2,1)}), bf16[16,16,128]{2,1,0:T(8,128)(2,1)S(1)}, u32[]{:S(2)}, u32[]{:S(2)}) async-start(bf16[16,16,128]{2,1,0:T(8,128)(2,1)} %broadcast_in_dim.67), calls=%async_computation.4 | async-start | bytes 131072 | tf_op jit(solution)/shard_map/all_to_all | solution.py:16
  102.8 1.3 slice.135
  104.1 10.3 %all-to-all-done.4 = bf16[16,16,128]{2,1,0:T(8,128)(2,1)S(1)} async-done(((bf16[16,16,128]{2,1,0:T(8,128)(2,1)}), bf16[16,16,128]{2,1,0:T(8,128)(2,1)S(1)}, u32[]{:S(2)}, u32[]{:S(2)}) %all-to-all-start.4) | async-done | bytes 65568 | tf_op jit(solution)/shard_map/all_to_all | solution.py:16
  114.5 0.4 fusion.1
  114.9 14.4 %all_to_all.52 = f32[16,16,128]{2,1,0:T(8,128)S(1)} all-to-all(f32[16,16,128]{2,1,0:T(8,128)S(1)} %broadcast_in_dim.69), channel_id=1, replica_groups=mesh['yl'=4,'x'=4,'z'=8,'yh'=2,'c'=2] {'z','yh'}, dimensions={0} | all-to-all | bytes 262144 | tf_op jit(solution)/shard_map/all_to_all | solution.py:16
  129.3 0.3 fusion.18
  129.6 14.2 %all_to_all.53 = bf16[16,16,128]{2,1,0:T(8,128)(2,1)S(1)} all-to-all(bf16[16,16,128]{2,1,0:T(8,128)(2,1)S(1)} %broadcast_in_dim.70), channel_id=1, replica_groups=mesh['yl'=4,'x'=4,'z'=8,'yh'=2,'c'=2] {'z','yh'}, dimensions={0} | all-to-all | bytes 131072 | tf_op jit(solution)/shard_map/all_to_all | solution.py:16
  143.9 0.2 fusion.3
  144.1 0.7 broadcast_in_dim.72
  144.8 3.5 %all-to-all-start.7 = ((f32[16,16,128]{2,1,0:T(8,128)}), f32[16,16,128]{2,1,0:T(8,128)S(1)}, u32[]{:S(2)}, u32[]{:S(2)}) async-start(f32[16,16,128]{2,1,0:T(8,128)} %broadcast_in_dim.72), calls=%async_computation.7 | async-start | bytes 262144 | tf_op jit(solution)/shard_map/all_to_all | solution.py:16
  148.3 16.4 %all-gather.3 = bf16[12,16,16,128]{3,2,1,0:T(8,128)(2,1)S(1)} all-gather(bf16[3,16,16,128]{3,2,1,0:T(8,128)(2,1)S(1)} %pad_maximum_fusion), channel_id=5, replica_groups=mesh['yl'=4,'x'=4,'z'=8,'yh'=2,'c'=2] {'yl'}, dimensions={0}, use_global_device_ids=true | all-gather | bytes 983040 | tf_op jit(solution)/shard_map/all_gather | solution.py:165
  164.7 0.3 fusion.24
  165.0 0.7 broadcast_in_dim.73
  165.8 11.0 %all-to-all-start.8 = ((bf16[64,16,128]{2,1,0:T(8,128)(2,1)}), bf16[64,16,128]{2,1,0:T(8,128)(2,1)S(1)}, u32[]{:S(2)}, u32[]{:S(2)}) async-start(bf16[64,16,128]{2,1,0:T(8,128)(2,1)} %broadcast_in_dim.73), calls=%async_computation.8 | async-start | bytes 524288 | tf_op jit(solution)/shard_map/all_to_all | solution.py:16
  176.8 0.0 all-gather.10.cloned.1.call-done
  176.9 5.5 %shard_map.28.sofar = f32[2,16,512]{2,1,0:T(8,128)S(1)} custom-call(bf16[3,16,16,128]{3,2,1,0:T(8,128)(2,1)S(1)} %slice.142.refs_0_, bf16[8,64,8192]{2,1,0:T(8,128)(2,1)} %bitcast.130, bf16[8,64,8192]{2,1,0:T(8,128)(2,1)} %bitcast.132), custom_call_target="tpu_custom_call" | custom-call | flops 201326592 | bytes 12582912 | tf_op jit(solution)/shard_map/pallas_call | solution.py:170
  182.3 6.9 %all-to-all-done.8.got = bf16[64,16,128]{2,1,0:T(8,128)(2,1)S(1)} async-done(((bf16[64,16,128]{2,1,0:T(8,128)(2,1)}), bf16[64,16,128]{2,1,0:T(8,128)(2,1)S(1)}, u32[]{:S(2)}, u32[]{:S(2)}) %all-to-all-start.8) | async-done | bytes 262176 | tf_op jit(solution)/shard_map/all_to_all | solution.py:16
  189.3 3.4 %shard_map.29 = f32[8,2,16,128]{3,2,1,0:T(8,128)} custom-call(s32[1]{0:T(128)} %bitcast.owner_ref, bf16[64,16,128]{2,1,0:T(8,128)(2,1)S(1)} %all-to-all-done.8.got, f32[2,16,512]{2,1,0:T(8,128)S(1)} %shard_map.28.sofar, f32[4,16,128]{2,1,0:T(8,128)S(1)} %pad_maximum_fusion.1.solved, bf16[8,64,8192]{2,1,0:T(8,128)(2,1)} %bitcast.131, ...), custom_call_target="tpu_custom_call" | custom-call | flops 67108864 | bytes 4194304 | tf_op jit(solution)/shard_map/pallas_call | solution.py:178
  192.7 11.1 %all-to-all-start.9 = ((f32[8,2,16,128]{3,2,1,0:T(8,128)}), f32[8,2,16,128]{3,2,1,0:T(8,128)S(1)}, u32[]{:S(2)}, u32[]{:S(2)}) async-start(f32[8,2,16,128]{3,2,1,0:T(8,128)} %shard_map.29), calls=%async_computation.9 | async-start | bytes 262144 | tf_op jit(solution)/shard_map/all_to_all | solution.py:16
  203.7 0.1 copy.28
  203.8 0.1 copy.29
  203.9 5.1 %all-to-all-done.9 = f32[8,2,16,128]{3,2,1,0:T(8,128)S(1)} async-done(((f32[8,2,16,128]{3,2,1,0:T(8,128)}), f32[8,2,16,128]{3,2,1,0:T(8,128)S(1)}, u32[]{:S(2)}, u32[]{:S(2)}) %all-to-all-start.9) | async-done | bytes 131104 | tf_op jit(solution)/shard_map/all_to_all | solution.py:16
  209.1 0.1 dynamic-slice_bitcast_fusion
  209.2 0.7 copy.27
  (34 shorter events, 0.4 us)
Async XLA Ops:
  6.5 68.1 %all-gather.8.cloned.1.call-start = ((), (), s32[]{:S(2)}) async-start(), calls=%async_computation.10 | async-start | bytes 9437184 | tf_op jit(solution)/shard_map/all_gather | solution.py:133
  9.6 0.8 copy-start.1
  9.6 167.2 %all-gather.10.cloned.1.call-start = ((), (), s32[]{:S(2)}) async-start(), calls=%async_computation.11 | async-start | bytes 9437184 | tf_op jit(solution)/shard_map/all_gather | solution.py:134
  19.8 25.0 %all-to-all-start = ((f32[16,64,128]{2,1,0:T(8,128)}), f32[16,64,128]{2,1,0:T(8,128)S(1)}, u32[]{:S(2)}, u32[]{:S(2)}) async-start(f32[16,64,128]{2,1,0:T(8,128)} %broadcast_in_dim.62), calls=%async_computation | async-start | bytes 1048576 | tf_op jit(solution)/shard_map/all_to_all | solution.py:16
  53.8 123.0 %copy-start = (f32[4,16,128]{2,1,0:T(8,128)}, f32[4,16,128]{2,1,0:T(8,128)S(1)}, u32[]{:S(2)}) copy-start(f32[4,16,128]{2,1,0:T(8,128)S(1)} %all_to_all.50) | copy-start | bytes 98308
  77.3 20.6 %all-to-all-start.3 = ((f32[16,16,128]{2,1,0:T(8,128)}), f32[16,16,128]{2,1,0:T(8,128)S(1)}, u32[]{:S(2)}, u32[]{:S(2)}) async-start(f32[16,16,128]{2,1,0:T(8,128)} %broadcast_in_dim.66), calls=%async_computation.3 | async-start | bytes 262144 | tf_op jit(solution)/shard_map/all_to_all | solution.py:16
  98.9 15.5 %all-to-all-start.4 = ((bf16[16,16,128]{2,1,0:T(8,128)(2,1)}), bf16[16,16,128]{2,1,0:T(8,128)(2,1)S(1)}, u32[]{:S(2)}, u32[]{:S(2)}) async-start(bf16[16,16,128]{2,1,0:T(8,128)(2,1)} %broadcast_in_dim.67), calls=%async_computation.4 | async-start | bytes 131072 | tf_op jit(solution)/shard_map/all_to_all | solution.py:16
  144.8 19.9 %all-to-all-start.7 = ((f32[16,16,128]{2,1,0:T(8,128)}), f32[16,16,128]{2,1,0:T(8,128)S(1)}, u32[]{:S(2)}, u32[]{:S(2)}) async-start(f32[16,16,128]{2,1,0:T(8,128)} %broadcast_in_dim.72), calls=%async_computation.7 | async-start | bytes 262144 | tf_op jit(solution)/shard_map/all_to_all | solution.py:16
  165.8 23.5 %all-to-all-start.8 = ((bf16[64,16,128]{2,1,0:T(8,128)(2,1)}), bf16[64,16,128]{2,1,0:T(8,128)(2,1)S(1)}, u32[]{:S(2)}, u32[]{:S(2)}) async-start(bf16[64,16,128]{2,1,0:T(8,128)(2,1)} %broadcast_in_dim.73), calls=%async_computation.8 | async-start | bytes 524288 | tf_op jit(solution)/shard_map/all_to_all | solution.py:16
  176.9 5.5 %slice-start = ((f32[4,16,128]{2,1,0:T(8,128)}), f32[1,16,128]{2,1,0:T(8,128)S(1)}, s32[]{:S(2)}) async-start(f32[4,16,128]{2,1,0:T(8,128)} %copy-done), calls=%async_computation.12 | async-start | bytes 16384 | tf_op jit(solution)/shard_map/slice | solution.py:153
  192.7 16.3 %all-to-all-start.9 = ((f32[8,2,16,128]{3,2,1,0:T(8,128)}), f32[8,2,16,128]{3,2,1,0:T(8,128)S(1)}, u32[]{:S(2)}, u32[]{:S(2)}) async-start(f32[8,2,16,128]{3,2,1,0:T(8,128)} %shard_map.29), calls=%async_computation.9 | async-start | bytes 262144 | tf_op jit(solution)/shard_map/all_to_all | solution.py:16
Sparse Core Ops, SparseCore 0:
  9.8 61.2 all-gather.7
  73.3 55.2 all-gather.9

commit v12 on v11

--- a/solution.py
+++ b/solution.py
@@ -65,11 +65,12 @@
 
 
 def first_kernel(plan, *refs):
-    got, early_ref, late_ref, out_ref, held, sems = refs
+    *got, early_ref, late_ref, out_ref, held, sems = refs
 
     def cases_of(place):
-        _, chips, _, pair = got.shape
-        part, chip = got.at[place // (chips * pair)], place // pair % chips
+        _, chips, _, pair = got[0].shape
+        parts = [ref.at[n] for ref in got for n in range(ref.shape[0])]
+        part, chip = parts[place // (chips * pair)], place // pair % chips
         return jnp.concatenate([part[chip + n] for n in range(held.shape[3] // pair)], 1)
 
     total = stream(plan, early_ref, late_ref, held, sems, cases_of)
@@ -150,10 +151,19 @@
     first = jnp.where(lax.axis_index("x") == 0, first, mine)
     state = exchange(first.reshape(xs, few, pair), "x")
 
-    solved, known = [state[0]], []
+    def to_planes(parts):
+        got = lax.all_gather(jnp.stack(parts), "yl", axis=0)[0]
+        return got, jnp.minimum(jnp.abs(got[0, 0, :1].astype(jnp.float32)), 0.0)
+
+    solved, known, spread = [state[0]], [], []
     state = state[1:]
     for step in range(1, steps):
-        got = exchange(repeat(solved[-1].astype(jnp.bfloat16), chips), CHIPS)
+        part = solved[-1]
+        if step + 1 == steps:
+            got, none = to_planes(known)
+            part, spread = part + none, [got]
+            known = []
+        got = exchange(repeat(part.astype(jnp.bfloat16), chips), CHIPS)
         known.append(got)
         whole = jnp.swapaxes(got, 0, 1).reshape(few, block)
         update = times(whole, panel(step, step - 1))
@@ -162,8 +172,8 @@
         solved.append(times_exact(gather_chips(state[0]), panel(step, step)[:pair]))
         state = state[1:]
 
-    known = lax.all_gather(jnp.stack(known), "yl", axis=0)[0]
-    none = jnp.minimum(jnp.abs(known[0, 0, :1].astype(jnp.float32)), 0.0)
+    got, none = to_planes(known)
+    spread.append(got)
     planes = ("yl",) + CHIPS
     got = (solved[-1] + none).astype(jnp.bfloat16)
     got = exchange(repeat(got, lax.axis_size(planes)), planes)
@@ -173,8 +183,8 @@
         TILES[0],
         early,
         (2, few, xs * pair),
-        [pltpu.VMEM] + [pl.ANY] * 2,
-    )(known, early, late)
+        [pltpu.VMEM] * len(spread) + [pl.ANY] * 2,
+    )(*spread, early, late)
     both = streaming(
         last_kernel,
         (last, width),

time: 218 us -> 229 us (1.050)
  starting transfers between devices: 48.1 us -> 54.1 us
  blocking collectives: 85.3 us -> 89.9 us
    all_gather x1 -> x2, blocking collectives: 16.4 us -> 27.2 us  [to_planes(): got = lax.all_gather(jnp.stack(parts), 'yl', axis=0)[0]]
    all_to_all x4 -> x3, blocking collectives: 57.8 us -> 51.5 us  [exchange(): return lax.all_to_all(parts, axis, 0, 0, tiled=True)]
    all_to_all x6 -> x7, starting transfers between devices: 48 us -> 54 us  [exchange(): return lax.all_to_all(parts, axis, 0, 0, tiled=True)]
    all_to_all x6 -> x7, waiting for transfers between devices: 43.7 us -> 43.7 us  [exchange(): return lax.all_to_all(parts, axis, 0, 0, tiled=True)]
  transfers between devices with their start and end apart: 8 -> 9, of which waited for: 5 -> 5; matrix products, arithmetic and copies ran while one was open for 6% -> 6% of each run, Pallas kernels for 3% -> 2%
where the time goes in v12:
time: 229 us; the launch traced here: 228 us
  blocking collectives  89.9 us (39%)
  starting transfers between devices  54.1 us (24%)
  waiting for transfers between devices  44.4 us (19%)
  local copies, waits for them, and re-layouts  14.2 us (6%)
  between operations  13.8 us (6%)
  Pallas kernels  8.86 us (4%)
  matrix products  2.36 us (1%)
    all_to_all x7, starting transfers between devices, exchange(): return lax.all_to_all(parts, axis, 0, 0, tiled=True)  54 us
    all_to_all x3, blocking collectives, exchange(): return lax.all_to_all(parts, axis, 0, 0, tiled=True)  51.5 us
    all_to_all x7, waiting for transfers between devices, exchange(): return lax.all_to_all(parts, axis, 0, 0, tiled=True)  43.7 us
    all_gather x2, blocking collectives, to_planes(): got = lax.all_gather(jnp.stack(parts), 'yl', axis=0)[0]  27.2 us
    all_gather x1, blocking collectives, body(): together = lax.all_gather(given[0], 'c', axis=0, tiled=True).T  8.37 us
    pallas_call x1, Pallas kernels, body(): streaming(first_kernel, (0, last), TILES[0], early, (2, few, xs * pair),...  5.45 us
  transfers between devices with their start and end apart: 9, of which 5 were waited for; matrix products, arithmetic and copies ran while one was open for 6% of the time, Pallas kernels for 2%

profile of v12, /device:TPU:1, one launch (start us, length us, event | category | flops | bytes accessed | tf_op | source)
XLA Modules:
  0.0 227.9 jit_solution(2406929498114702415)
XLA Ops:
  6.5 3.1 %fusion.51 = (bf16[1,1,64,8192]{3,2,1,0:T(8,128)(2,1)}, bf16[1,1,64,8192]{3,2,1,0:T(8,128)(2,1)}) fusion(bf16[2,1,64,8192]{3,2,1,0:T(8,128)(2,1)} %param.2), kind=kLoop, calls=%fused_computation.93 | loop fusion | bytes 4194304 | tf_op jit(solution)/shard_map/slice | solution.py:135
  9.6 0.0 all-gather.11.cloned.1.call-start
  9.7 0.7 all-gather.11.cloned.1.call-update
  10.4 0.1 copy-done.1
  10.5 8.4 %all-gather = f32[1,1,128,128]{3,1,0,2:T(1,128)S(1)} all-gather(f32[1,1,64,128]{3,1,0,2:T(1,128)S(1)} %bitcast.151), channel_id=2, replica_groups=mesh['yl'=4,'x'=4,'z'=8,'yh'=2,'c'=2] {'c'}, dimensions={2}, use_global_device_ids=true | all-gather | bytes 98304 | tf_op jit(solution)/shard_map/all_gather | solution.py:143
  18.8 0.1 copy.17
  18.9 0.9 broadcast_in_dim.62
  19.8 10.0 %all-to-all-start = ((f32[16,64,128]{2,1,0:T(8,128)}), f32[16,64,128]{2,1,0:T(8,128)S(1)}, u32[]{:S(2)}, u32[]{:S(2)}) async-start(f32[16,64,128]{2,1,0:T(8,128)} %broadcast_in_dim.62), calls=%async_computation | async-start | bytes 1048576 | tf_op jit(solution)/shard_map/all_to_all | solution.py:16
  29.8 1.0 slice.137
  30.8 2.8 %all-gather.1 = bf16[1,128,2048]{2,1,0:T(8,128)(2,1)S(1)} all-gather(bf16[1,64,2048]{2,1,0:T(8,128)(2,1)S(1)} %slice.137), channel_id=3, replica_groups=mesh['yl'=4,'x'=4,'z'=8,'yh'=2,'c'=2] {'c'}, dimensions={1}, use_global_device_ids=true | all-gather | bytes 786432 | tf_op jit(solution)/shard_map/all_gather | solution.py:148
  33.7 11.1 %all-to-all-done = f32[16,64,128]{2,1,0:T(8,128)S(1)} async-done(((f32[16,64,128]{2,1,0:T(8,128)}), f32[16,64,128]{2,1,0:T(8,128)S(1)}, u32[]{:S(2)}, u32[]{:S(2)}) %all-to-all-start) | async-done | bytes 524320 | tf_op jit(solution)/shard_map/all_to_all | solution.py:16
  44.8 0.1 reduce-precision_convert_fusion.1
  44.9 0.4 fusion.4
  45.3 8.5 %all_to_all.50 = f32[4,16,128]{2,1,0:T(8,128)S(1)} all-to-all(f32[4,16,128]{2,1,0:T(8,128)S(1)} %bitcast.153), channel_id=1, replica_groups=mesh['yl'=4,'x'=4,'z'=8,'yh'=2,'c'=2] {'x'}, dimensions={0} | all-to-all | bytes 65536 | tf_op jit(solution)/shard_map/all_to_all | solution.py:16
  53.8 20.7 %all_to_all.51 = bf16[16,16,128]{2,1,0:T(8,128)(2,1)S(1)} all-to-all(bf16[16,16,128]{2,1,0:T(8,128)(2,1)S(1)} %broadcast_in_dim.64), channel_id=1, replica_groups=mesh['yl'=4,'x'=4,'z'=8,'yh'=2,'c'=2] {'z','yh'}, dimensions={0} | all-to-all | bytes 131072 | tf_op jit(solution)/shard_map/all_to_all | solution.py:16
  74.6 1.5 slice.140
  76.1 0.5 fusion
  76.7 0.7 broadcast_in_dim.66
  77.3 8.6 %all-to-all-start.3 = ((f32[16,16,128]{2,1,0:T(8,128)}), f32[16,16,128]{2,1,0:T(8,128)S(1)}, u32[]{:S(2)}, u32[]{:S(2)}) async-start(f32[16,16,128]{2,1,0:T(8,128)} %broadcast_in_dim.66), calls=%async_computation.3 | async-start | bytes 262144 | tf_op jit(solution)/shard_map/all_to_all | solution.py:16
  85.9 1.8 fusion.50
  87.7 10.2 %all-to-all-done.3 = f32[16,16,128]{2,1,0:T(8,128)S(1)} async-done(((f32[16,16,128]{2,1,0:T(8,128)}), f32[16,16,128]{2,1,0:T(8,128)S(1)}, u32[]{:S(2)}, u32[]{:S(2)}) %all-to-all-start.3) | async-done | bytes 131104 | tf_op jit(solution)/shard_map/all_to_all | solution.py:16
  97.9 0.3 fusion.12
  98.2 0.6 broadcast_in_dim.67
  98.9 3.9 %all-to-all-start.4 = ((bf16[16,16,128]{2,1,0:T(8,128)(2,1)}), bf16[16,16,128]{2,1,0:T(8,128)(2,1)S(1)}, u32[]{:S(2)}, u32[]{:S(2)}) async-start(bf16[16,16,128]{2,1,0:T(8,128)(2,1)} %broadcast_in_dim.67), calls=%async_computation.4 | async-start | bytes 131072 | tf_op jit(solution)/shard_map/all_to_all | solution.py:16
  102.8 1.3 slice.144
  104.1 10.3 %all-to-all-done.4 = bf16[16,16,128]{2,1,0:T(8,128)(2,1)S(1)} async-done(((bf16[16,16,128]{2,1,0:T(8,128)(2,1)}), bf16[16,16,128]{2,1,0:T(8,128)(2,1)S(1)}, u32[]{:S(2)}, u32[]{:S(2)}) %all-to-all-start.4) | async-done | bytes 65568 | tf_op jit(solution)/shard_map/all_to_all | solution.py:16
  114.4 0.4 fusion.1
  114.8 0.7 broadcast_in_dim.69
  115.5 3.5 %all-to-all-start.5 = ((f32[16,16,128]{2,1,0:T(8,128)}), f32[16,16,128]{2,1,0:T(8,128)S(1)}, u32[]{:S(2)}, u32[]{:S(2)}) async-start(f32[16,16,128]{2,1,0:T(8,128)} %broadcast_in_dim.69), calls=%async_computation.5 | async-start | bytes 262144 | tf_op jit(solution)/shard_map/all_to_all | solution.py:16
  119.0 14.3 %all-gather.3 = bf16[8,16,16,128]{3,2,1,0:T(8,128)(2,1)S(1)} all-gather(bf16[2,16,16,128]{3,2,1,0:T(8,128)(2,1)S(1)} %pad_maximum_fusion), channel_id=5, replica_groups=mesh['yl'=4,'x'=4,'z'=8,'yh'=2,'c'=2] {'yl'}, dimensions={0}, use_global_device_ids=true | all-gather | bytes 655360 | tf_op jit(solution)/shard_map/all_gather | solution.py:155
  133.4 0.3 fusion.18
  133.8 22.4 %all_to_all.52 = bf16[16,16,128]{2,1,0:T(8,128)(2,1)S(1)} all-to-all(bf16[16,16,128]{2,1,0:T(8,128)(2,1)S(1)} %broadcast_in_dim.70), channel_id=1, replica_groups=mesh['yl'=4,'x'=4,'z'=8,'yh'=2,'c'=2] {'z','yh'}, dimensions={0} | all-to-all | bytes 131072 | tf_op jit(solution)/shard_map/all_to_all | solution.py:16
  156.1 0.2 fusion.3
  156.4 0.7 broadcast_in_dim.72
  157.0 3.5 %all-to-all-start.7 = ((f32[16,16,128]{2,1,0:T(8,128)}), f32[16,16,128]{2,1,0:T(8,128)S(1)}, u32[]{:S(2)}, u32[]{:S(2)}) async-start(f32[16,16,128]{2,1,0:T(8,128)} %broadcast_in_dim.72), calls=%async_computation.7 | async-start | bytes 262144 | tf_op jit(solution)/shard_map/all_to_all | solution.py:16
  160.6 12.8 %all-gather.4 = bf16[64,16,128]{2,1,0:T(8,128)(2,1)S(1)} all-gather(bf16[16,16,128]{2,1,0:T(8,128)(2,1)S(1)} %all_to_all.52), channel_id=6, replica_groups=mesh['yl'=4,'x'=4,'z'=8,'yh'=2,'c'=2] {'yl'}, dimensions={0}, use_global_device_ids=true | all-gather | bytes 327680 | tf_op jit(solution)/shard_map/all_gather | solution.py:155
  173.4 0.3 fusion.24
  173.8 0.7 broadcast_in_dim.73
  174.5 12.2 %all-to-all-start.8 = ((bf16[64,16,128]{2,1,0:T(8,128)(2,1)}), bf16[64,16,128]{2,1,0:T(8,128)(2,1)S(1)}, u32[]{:S(2)}, u32[]{:S(2)}) async-start(bf16[64,16,128]{2,1,0:T(8,128)(2,1)} %broadcast_in_dim.73), calls=%async_computation.8 | async-start | bytes 524288 | tf_op jit(solution)/shard_map/all_to_all | solution.py:16
  186.7 5.5 %shard_map.28.sofar = f32[2,16,512]{2,1,0:T(8,128)S(1)} custom-call(bf16[2,16,16,128]{3,2,1,0:T(8,128)(2,1)S(1)} %slice.153.refs_0_, bf16[1,16,16,128]{3,2,1,0:T(8,128)(2,1)S(1)} %slice_bitcast_fusion.refs_1_, bf16[8,64,8192]{2,1,0:T(8,128)(2,1)} %bitcast.133, bf16[8,64,8192]{2,1,0:T(8,128)(2,1)} %bitcast.135), custom_call_target="tpu_custom_call" | custom-call | flops 201326592 | bytes 12582912 | tf_op jit(solution)/shard_map/pallas_call | solution.py:180
  192.2 6.9 %all-to-all-done.8.got = bf16[64,16,128]{2,1,0:T(8,128)(2,1)S(1)} async-done(((bf16[64,16,128]{2,1,0:T(8,128)(2,1)}), bf16[64,16,128]{2,1,0:T(8,128)(2,1)S(1)}, u32[]{:S(2)}, u32[]{:S(2)}) %all-to-all-start.8) | async-done | bytes 262176 | tf_op jit(solution)/shard_map/all_to_all | solution.py:16
  199.1 3.4 %shard_map.29 = f32[8,2,16,128]{3,2,1,0:T(8,128)} custom-call(s32[1]{0:T(128)} %bitcast.owner_ref, bf16[64,16,128]{2,1,0:T(8,128)(2,1)S(1)} %all-to-all-done.8.got, f32[2,16,512]{2,1,0:T(8,128)S(1)} %shard_map.28.sofar, f32[4,16,128]{2,1,0:T(8,128)S(1)} %pad_maximum_fusion.1.solved, bf16[8,64,8192]{2,1,0:T(8,128)(2,1)} %bitcast.134, ...), custom_call_target="tpu_custom_call" | custom-call | flops 67108864 | bytes 4194304 | tf_op jit(solution)/shard_map/pallas_call | solution.py:188
  202.5 12.4 %all-to-all-start.9 = ((f32[8,2,16,128]{3,2,1,0:T(8,128)}), f32[8,2,16,128]{3,2,1,0:T(8,128)S(1)}, u32[]{:S(2)}, u32[]{:S(2)}) async-start(f32[8,2,16,128]{3,2,1,0:T(8,128)} %shard_map.29), calls=%async_computation.9 | async-start | bytes 262144 | tf_op jit(solution)/shard_map/all_to_all | solution.py:16
  214.9 0.1 copy.28
  215.0 0.1 copy.29
  215.1 5.1 %all-to-all-done.9 = f32[8,2,16,128]{3,2,1,0:T(8,128)S(1)} async-done(((f32[8,2,16,128]{3,2,1,0:T(8,128)}), f32[8,2,16,128]{3,2,1,0:T(8,128)S(1)}, u32[]{:S(2)}, u32[]{:S(2)}) %all-to-all-start.9) | async-done | bytes 131104 | tf_op jit(solution)/shard_map/all_to_all | solution.py:16
  220.2 0.1 dynamic-slice_bitcast_fusion
  220.4 0.7 copy.27
  (38 shorter events, 0.4 us)
Async XLA Ops:
  6.5 68.1 %all-gather.9.cloned.1.call-start = ((), (), s32[]{:S(2)}) async-start(), calls=%async_computation.10 | async-start | bytes 9437184 | tf_op jit(solution)/shard_map/all_gather | solution.py:134
  9.6 0.8 copy-start.1
  9.6 177.1 %all-gather.11.cloned.1.call-start = ((), (), s32[]{:S(2)}) async-start(), calls=%async_computation.11 | async-start | bytes 9437184 | tf_op jit(solution)/shard_map/all_gather | solution.py:135
  19.8 25.0 %all-to-all-start = ((f32[16,64,128]{2,1,0:T(8,128)}), f32[16,64,128]{2,1,0:T(8,128)S(1)}, u32[]{:S(2)}, u32[]{:S(2)}) async-start(f32[16,64,128]{2,1,0:T(8,128)} %broadcast_in_dim.62), calls=%async_computation | async-start | bytes 1048576 | tf_op jit(solution)/shard_map/all_to_all | solution.py:16
  53.8 132.8 %copy-start = (f32[4,16,128]{2,1,0:T(8,128)}, f32[4,16,128]{2,1,0:T(8,128)S(1)}, u32[]{:S(2)}) copy-start(f32[4,16,128]{2,1,0:T(8,128)S(1)} %all_to_all.50) | copy-start | bytes 98308
  77.3 20.6 %all-to-all-start.3 = ((f32[16,16,128]{2,1,0:T(8,128)}), f32[16,16,128]{2,1,0:T(8,128)S(1)}, u32[]{:S(2)}, u32[]{:S(2)}) async-start(f32[16,16,128]{2,1,0:T(8,128)} %broadcast_in_dim.66), calls=%async_computation.3 | async-start | bytes 262144 | tf_op jit(solution)/shard_map/all_to_all | solution.py:16
  98.9 15.5 %all-to-all-start.4 = ((bf16[16,16,128]{2,1,0:T(8,128)(2,1)}), bf16[16,16,128]{2,1,0:T(8,128)(2,1)S(1)}, u32[]{:S(2)}, u32[]{:S(2)}) async-start(bf16[16,16,128]{2,1,0:T(8,128)(2,1)} %broadcast_in_dim.67), calls=%async_computation.4 | async-start | bytes 131072 | tf_op jit(solution)/shard_map/all_to_all | solution.py:16
  115.5 17.9 %all-to-all-start.5 = ((f32[16,16,128]{2,1,0:T(8,128)}), f32[16,16,128]{2,1,0:T(8,128)S(1)}, u32[]{:S(2)}, u32[]{:S(2)}) async-start(f32[16,16,128]{2,1,0:T(8,128)} %broadcast_in_dim.69), calls=%async_computation.5 | async-start | bytes 262144 | tf_op jit(solution)/shard_map/all_to_all | solution.py:16
  157.0 16.4 %all-to-all-start.7 = ((f32[16,16,128]{2,1,0:T(8,128)}), f32[16,16,128]{2,1,0:T(8,128)S(1)}, u32[]{:S(2)}, u32[]{:S(2)}) async-start(f32[16,16,128]{2,1,0:T(8,128)} %broadcast_in_dim.72), calls=%async_computation.7 | async-start | bytes 262144 | tf_op jit(solution)/shard_map/all_to_all | solution.py:16
  174.5 24.6 %all-to-all-start.8 = ((bf16[64,16,128]{2,1,0:T(8,128)(2,1)}), bf16[64,16,128]{2,1,0:T(8,128)(2,1)S(1)}, u32[]{:S(2)}, u32[]{:S(2)}) async-start(bf16[64,16,128]{2,1,0:T(8,128)(2,1)} %broadcast_in_dim.73), calls=%async_computation.8 | async-start | bytes 524288 | tf_op jit(solution)/shard_map/all_to_all | solution.py:16
  186.7 5.5 %slice-start = ((f32[4,16,128]{2,1,0:T(8,128)}), f32[1,16,128]{2,1,0:T(8,128)S(1)}, s32[]{:S(2)}) async-start(f32[4,16,128]{2,1,0:T(8,128)} %copy-done), calls=%async_computation.12 | async-start | bytes 16384 | tf_op jit(solution)/shard_map/slice | solution.py:158
  202.5 17.7 %all-to-all-start.9 = ((f32[8,2,16,128]{3,2,1,0:T(8,128)}), f32[8,2,16,128]{3,2,1,0:T(8,128)S(1)}, u32[]{:S(2)}, u32[]{:S(2)}) async-start(f32[8,2,16,128]{3,2,1,0:T(8,128)} %shard_map.29), calls=%async_computation.9 | async-start | bytes 262144 | tf_op jit(solution)/shard_map/all_to_all | solution.py:16
Sparse Core Ops, SparseCore 0:
  9.8 61.2 all-gather.8
  73.2 55.2 all-gather.10

commit v13 on v9

--- a/solution.py
+++ b/solution.py
@@ -65,12 +65,12 @@
 
 
 def first_kernel(plan, *refs):
-    *whole, early_ref, late_ref, out_ref, held, sems = refs
-    block = whole[0].shape[1]
+    *got, early_ref, late_ref, out_ref, held, sems = refs
 
     def cases_of(place):
-        start = place % block
-        return whole[place // block][:, start : start + held.shape[3]]
+        chips, _, pair = got[0].shape
+        part, chip = got[place // (chips * pair)], place // pair % chips
+        return jnp.concatenate([part[chip + n] for n in range(held.shape[3] // pair)], 1)
 
     total = stream(plan, early_ref, late_ref, held, sems, cases_of)
     for index in range(2):
@@ -129,6 +129,7 @@
     few = cases // (xs * cores)
     pair = cores * share
 
+    last = width - block
     early = lax.all_gather(stored[0], ("x", "c"), axis=0)
     late = lax.all_gather(stored[1], ("x", "c"), axis=0)
 
@@ -156,15 +157,20 @@
     state = state[1:]
     for step in range(1, steps):
         got = to_all(solved[-1].astype(jnp.bfloat16))
-        known.append(jnp.swapaxes(got, 0, 1).reshape(few, block))
-        update = times(known[-1], panel(step, step - 1))
-        update = update.reshape(few, steps - step, pair)
-        state = state - jnp.swapaxes(update, 0, 1)
-        solved.append(times_exact(gather_chips(state[0]), panel(step, step)[:pair]))
-        state = state[1:]
+        known.append(got)
+        whole = jnp.swapaxes(got, 0, 1).reshape(few, block)
+        if step == 1:
+            first = state[0] - times(whole, panel(step, step - 1)[:pair])
+            rest = times(whole, panel(step + 1, step - 1))
+        else:
+            rest = times(whole, panel(step, step - 1))
+            first = state[0] - rest[:, :pair]
+            rest = rest[:, pair:]
+        solved.append(times_exact(gather_chips(first), panel(step, step)[:pair]))
+        rest = rest.reshape(few, steps - step - 1, pair)
+        state = state[1:] - jnp.swapaxes(rest, 0, 1)
 
     got = to_all(solved[-1].astype(jnp.bfloat16), False)
-    last = width - block
     sofar = streaming(
         first_kernel,
         (0, last),

time: 214 us -> 213 us (level)
  blocking collectives: 75.8 us -> 90.2 us
  waiting for transfers between devices: 57 us -> 46.4 us
  starting transfers between devices: 41.2 us -> 38.5 us
    all_to_all x4 -> x5, blocking collectives: 64.6 us -> 79.1 us  [exchange(): return lax.all_to_all(parts, axis, 0, 0, tiled=True)]
    all_to_all x6 -> x5, waiting for transfers between devices: 56.2 us -> 45.6 us  [exchange(): return lax.all_to_all(parts, axis, 0, 0, tiled=True)]
    all_to_all x6 -> x5, starting transfers between devices: 41.2 us -> 38.4 us  [exchange(): return lax.all_to_all(parts, axis, 0, 0, tiled=True)]
  transfers between devices with their start and end apart: 8 -> 7, of which waited for: 6 -> 5; matrix products, arithmetic and copies ran while one was open for 6% -> 5% of each run, Pallas kernels for 3% -> 3%
where the time goes in v13:
time: 213 us; the launch traced here: 212 us
  blocking collectives  90.2 us (42%)
  waiting for transfers between devices  46.4 us (22%)
  starting transfers between devices  38.5 us (18%)
  between operations  13.7 us (6%)
  local copies, waits for them, and re-layouts  12 us (6%)
  Pallas kernels  8.86 us (4%)
  matrix products  2.46 us (1%)
    all_to_all x5, blocking collectives, exchange(): return lax.all_to_all(parts, axis, 0, 0, tiled=True)  79.1 us
    all_to_all x5, waiting for transfers between devices, exchange(): return lax.all_to_all(parts, axis, 0, 0, tiled=True)  45.6 us
    all_to_all x5, starting transfers between devices, exchange(): return lax.all_to_all(parts, axis, 0, 0, tiled=True)  38.4 us
    all_gather x1, blocking collectives, body(): together = lax.all_gather(given[0], 'c', axis=0, tiled=True).T  8.37 us
    pallas_call x1, Pallas kernels, body(): streaming(first_kernel, (0, last), TILES[0], early, (2, few, xs * pair),...  5.45 us
  transfers between devices with their start and end apart: 7, of which 5 were waited for; matrix products, arithmetic and copies ran while one was open for 5% of the time, Pallas kernels for 3%

profile of v13, /device:TPU:1, one launch (start us, length us, event | category | flops | bytes accessed | tf_op | source)
XLA Modules:
  0.0 212.4 jit_solution(3190256599093103564)
XLA Ops:
  6.5 3.1 %fusion.52 = (bf16[1,1,64,8192]{3,2,1,0:T(8,128)(2,1)}, bf16[1,1,64,8192]{3,2,1,0:T(8,128)(2,1)}) fusion(bf16[2,1,64,8192]{3,2,1,0:T(8,128)(2,1)} %param.2), kind=kLoop, calls=%fused_computation.94 | loop fusion | bytes 4194304 | tf_op jit(solution)/shard_map/slice | solution.py:134
  9.6 0.0 all-gather.7.cloned.1.call-update
  9.6 0.0 all-gather.9.cloned.1.call-start
  9.7 0.7 all-gather.9.cloned.1.call-update
  10.4 0.1 copy-done.1
  10.5 8.4 %all-gather = f32[1,1,128,128]{3,1,0,2:T(1,128)S(1)} all-gather(f32[1,1,64,128]{3,1,0,2:T(1,128)S(1)} %bitcast.153), channel_id=2, replica_groups=mesh['yl'=4,'x'=4,'z'=8,'yh'=2,'c'=2] {'c'}, dimensions={2}, use_global_device_ids=true | all-gather | bytes 98304 | tf_op jit(solution)/shard_map/all_gather | solution.py:145
  18.8 0.1 copy.17
  18.9 0.9 broadcast_in_dim.26
  19.8 10.0 %all-to-all-start = ((f32[16,64,128]{2,1,0:T(8,128)}), f32[16,64,128]{2,1,0:T(8,128)S(1)}, u32[]{:S(2)}, u32[]{:S(2)}) async-start(f32[16,64,128]{2,1,0:T(8,128)} %broadcast_in_dim.26), calls=%async_computation | async-start | bytes 1048576 | tf_op jit(solution)/shard_map/all_to_all | solution.py:16
  29.8 1.0 slice.150
  30.8 2.8 %all-gather.1 = bf16[1,128,2048]{2,1,0:T(8,128)(2,1)S(1)} all-gather(bf16[1,64,2048]{2,1,0:T(8,128)(2,1)S(1)} %slice.150), channel_id=3, replica_groups=mesh['yl'=4,'x'=4,'z'=8,'yh'=2,'c'=2] {'c'}, dimensions={1}, use_global_device_ids=true | all-gather | bytes 786432 | tf_op jit(solution)/shard_map/all_gather | solution.py:150
  33.7 11.1 %all-to-all-done = f32[16,64,128]{2,1,0:T(8,128)S(1)} async-done(((f32[16,64,128]{2,1,0:T(8,128)}), f32[16,64,128]{2,1,0:T(8,128)S(1)}, u32[]{:S(2)}, u32[]{:S(2)}) %all-to-all-start) | async-done | bytes 524320 | tf_op jit(solution)/shard_map/all_to_all | solution.py:16
  44.8 0.1 reduce-precision_convert_fusion.1
  44.9 0.4 fusion.1
  45.3 8.5 %all_to_all.50 = f32[4,16,128]{2,1,0:T(8,128)S(1)} all-to-all(f32[4,16,128]{2,1,0:T(8,128)S(1)} %bitcast.155), channel_id=1, replica_groups=mesh['yl'=4,'x'=4,'z'=8,'yh'=2,'c'=2] {'x'}, dimensions={0} | all-to-all | bytes 65536 | tf_op jit(solution)/shard_map/all_to_all | solution.py:16
  53.9 23.9 %all_to_all.51 = bf16[64,16,128]{2,1,0:T(8,128)(2,1)S(1)} all-to-all(bf16[64,16,128]{2,1,0:T(8,128)(2,1)S(1)} %broadcast_in_dim.28), channel_id=1, replica_groups=mesh['yl'=4,'x'=4,'z'=8,'yh'=2,'c'=2] {'yl','z','yh'}, dimensions={0} | all-to-all | bytes 524288 | tf_op jit(solution)/shard_map/all_to_all | solution.py:16
  77.8 0.0 all-gather.7.cloned.1.call-done
  77.8 1.9 fusion.51
  79.7 0.2 convolution_subtract_fusion.1
  79.9 0.7 broadcast_in_dim.29
  80.6 5.4 %all-to-all-start.3 = ((f32[16,16,128]{2,1,0:T(8,128)}), f32[16,16,128]{2,1,0:T(8,128)S(1)}, u32[]{:S(2)}, u32[]{:S(2)}) async-start(f32[16,16,128]{2,1,0:T(8,128)} %broadcast_in_dim.29), calls=%async_computation.3 | async-start | bytes 262144 | tf_op jit(solution)/shard_map/all_to_all | solution.py:16
  86.1 11.8 %all-to-all-done.3 = f32[16,16,128]{2,1,0:T(8,128)S(1)} async-done(((f32[16,16,128]{2,1,0:T(8,128)}), f32[16,16,128]{2,1,0:T(8,128)S(1)}, u32[]{:S(2)}, u32[]{:S(2)}) %all-to-all-start.3) | async-done | bytes 131104 | tf_op jit(solution)/shard_map/all_to_all | solution.py:16
  97.9 0.3 fusion.9
  98.2 0.7 broadcast_in_dim.30
  98.9 4.6 %all-to-all-start.4 = ((bf16[64,16,128]{2,1,0:T(8,128)(2,1)}), bf16[64,16,128]{2,1,0:T(8,128)(2,1)S(1)}, u32[]{:S(2)}, u32[]{:S(2)}) async-start(bf16[64,16,128]{2,1,0:T(8,128)(2,1)} %broadcast_in_dim.30), calls=%async_computation.4 | async-start | bytes 524288 | tf_op jit(solution)/shard_map/all_to_all | solution.py:16
  103.5 1.7 fusion.50
  105.2 0.4 fusion
  105.6 10.7 %all-to-all-done.4 = bf16[64,16,128]{2,1,0:T(8,128)(2,1)S(1)} async-done(((bf16[64,16,128]{2,1,0:T(8,128)(2,1)}), bf16[64,16,128]{2,1,0:T(8,128)(2,1)S(1)}, u32[]{:S(2)}, u32[]{:S(2)}) %all-to-all-start.4) | async-done | bytes 262176 | tf_op jit(solution)/shard_map/all_to_all | solution.py:16
  116.3 0.4 fusion.32
  116.7 14.6 %all_to_all.52 = f32[16,16,128]{2,1,0:T(8,128)S(1)} all-to-all(f32[16,16,128]{2,1,0:T(8,128)S(1)} %broadcast_in_dim.31), channel_id=1, replica_groups=mesh['yl'=4,'x'=4,'z'=8,'yh'=2,'c'=2] {'z','yh'}, dimensions={0} | all-to-all | bytes 262144 | tf_op jit(solution)/shard_map/all_to_all | solution.py:16
  131.3 0.3 fusion.15
  131.6 17.5 %all_to_all.53 = bf16[64,16,128]{2,1,0:T(8,128)(2,1)S(1)} all-to-all(bf16[64,16,128]{2,1,0:T(8,128)(2,1)S(1)} %broadcast_in_dim.32), channel_id=1, replica_groups=mesh['yl'=4,'x'=4,'z'=8,'yh'=2,'c'=2] {'yl','z','yh'}, dimensions={0} | all-to-all | bytes 524288 | tf_op jit(solution)/shard_map/all_to_all | solution.py:16
  149.2 0.2 convolution_subtract_fusion
  149.5 14.6 %all_to_all.54 = f32[16,16,128]{2,1,0:T(8,128)S(1)} all-to-all(f32[16,16,128]{2,1,0:T(8,128)S(1)} %broadcast_in_dim.66), channel_id=1, replica_groups=mesh['yl'=4,'x'=4,'z'=8,'yh'=2,'c'=2] {'z','yh'}, dimensions={0} | all-to-all | bytes 262144 | tf_op jit(solution)/shard_map/all_to_all | solution.py:16
  164.1 0.3 fusion.21
  164.4 0.7 broadcast_in_dim.67
  165.1 5.2 %all-to-all-start.8 = ((bf16[64,16,128]{2,1,0:T(8,128)(2,1)}), bf16[64,16,128]{2,1,0:T(8,128)(2,1)S(1)}, u32[]{:S(2)}, u32[]{:S(2)}) async-start(bf16[64,16,128]{2,1,0:T(8,128)(2,1)} %broadcast_in_dim.67), calls=%async_computation.8 | async-start | bytes 524288 | tf_op jit(solution)/shard_map/all_to_all | solution.py:16
  170.3 0.0 all-gather.9.cloned.1.call-done
  170.4 0.0 slice-start
  170.4 5.5 %shard_map.28.sofar = f32[2,16,512]{2,1,0:T(8,128)S(1)} custom-call(bf16[16,16,128]{2,1,0:T(8,128)(2,1)S(1)} %get-tuple-element.21.refs_0_, bf16[16,16,128]{2,1,0:T(8,128)(2,1)S(1)} %get-tuple-element.19.refs_1_, bf16[16,16,128]{2,1,0:T(8,128)(2,1)S(1)} %get-tuple-element.17.refs_2_, bf16[8,64,8192]{2,1,0:T(8,128)(2,1)} %bitcast.138, ...), custom_call_target="tpu_custom_call" | custom-call | flops 201326592 | bytes 12582912 | tf_op jit(solution)/shard_map/pallas_call | solution.py:174
  175.9 6.9 %all-to-all-done.8.got = bf16[64,16,128]{2,1,0:T(8,128)(2,1)S(1)} async-done(((bf16[64,16,128]{2,1,0:T(8,128)(2,1)}), bf16[64,16,128]{2,1,0:T(8,128)(2,1)S(1)}, u32[]{:S(2)}, u32[]{:S(2)}) %all-to-all-start.8) | async-done | bytes 262176 | tf_op jit(solution)/shard_map/all_to_all | solution.py:16
  182.8 3.4 %shard_map.29 = f32[8,2,16,128]{3,2,1,0:T(8,128)} custom-call(s32[1]{0:T(128)} %bitcast.owner_ref, bf16[64,16,128]{2,1,0:T(8,128)(2,1)S(1)} %all-to-all-done.8.got, f32[2,16,512]{2,1,0:T(8,128)S(1)} %shard_map.28.sofar, f32[4,16,128]{2,1,0:T(8,128)S(1)} %pad_maximum_fusion.solved, bf16[8,64,8192]{2,1,0:T(8,128)(2,1)} %bitcast.139, bf16[8,64,8192]{2,1,0:T(8,128)(2,1)} %bitcast.141), custom_call_target="tpu_custom_call" | custom-call | flops 67108864 | bytes 4194304 | tf_op jit(solution)/shard_map/pallas_call | solution.py:182
  186.2 13.2 %all-to-all-start.9 = ((f32[8,2,16,128]{3,2,1,0:T(8,128)}), f32[8,2,16,128]{3,2,1,0:T(8,128)S(1)}, u32[]{:S(2)}, u32[]{:S(2)}) async-start(f32[8,2,16,128]{3,2,1,0:T(8,128)} %shard_map.29), calls=%async_computation.9 | async-start | bytes 262144 | tf_op jit(solution)/shard_map/all_to_all | solution.py:16
  199.4 0.1 copy.28
  199.5 0.1 copy.29
  199.6 5.1 %all-to-all-done.9 = f32[8,2,16,128]{3,2,1,0:T(8,128)S(1)} async-done(((f32[8,2,16,128]{3,2,1,0:T(8,128)}), f32[8,2,16,128]{3,2,1,0:T(8,128)S(1)}, u32[]{:S(2)}, u32[]{:S(2)}) %all-to-all-start.9) | async-done | bytes 131104 | tf_op jit(solution)/shard_map/all_to_all | solution.py:16
  204.7 0.1 dynamic-slice_bitcast_fusion
  204.9 0.7 copy.27
  (29 shorter events, 0.4 us)
Async XLA Ops:
  6.5 71.3 %all-gather.7.cloned.1.call-start = ((), (), s32[]{:S(2)}) async-start(), calls=%async_computation.10 | async-start | bytes 9437184 | tf_op jit(solution)/shard_map/all_gather | solution.py:133
  9.6 0.8 copy-start.1
  9.6 160.7 %all-gather.9.cloned.1.call-start = ((), (), s32[]{:S(2)}) async-start(), calls=%async_computation.11 | async-start | bytes 9437184 | tf_op jit(solution)/shard_map/all_gather | solution.py:134
  19.8 25.0 %all-to-all-start = ((f32[16,64,128]{2,1,0:T(8,128)}), f32[16,64,128]{2,1,0:T(8,128)S(1)}, u32[]{:S(2)}, u32[]{:S(2)}) async-start(f32[16,64,128]{2,1,0:T(8,128)} %broadcast_in_dim.26), calls=%async_computation | async-start | bytes 1048576 | tf_op jit(solution)/shard_map/all_to_all | solution.py:16
  53.8 116.5 %copy-start = (f32[4,16,128]{2,1,0:T(8,128)}, f32[4,16,128]{2,1,0:T(8,128)S(1)}, u32[]{:S(2)}) copy-start(f32[4,16,128]{2,1,0:T(8,128)S(1)} %all_to_all.50) | copy-start | bytes 98308
  80.6 17.2 %all-to-all-start.3 = ((f32[16,16,128]{2,1,0:T(8,128)}), f32[16,16,128]{2,1,0:T(8,128)S(1)}, u32[]{:S(2)}, u32[]{:S(2)}) async-start(f32[16,16,128]{2,1,0:T(8,128)} %broadcast_in_dim.29), calls=%async_computation.3 | async-start | bytes 262144 | tf_op jit(solution)/shard_map/all_to_all | solution.py:16
  98.9 17.4 %all-to-all-start.4 = ((bf16[64,16,128]{2,1,0:T(8,128)(2,1)}), bf16[64,16,128]{2,1,0:T(8,128)(2,1)S(1)}, u32[]{:S(2)}, u32[]{:S(2)}) async-start(bf16[64,16,128]{2,1,0:T(8,128)(2,1)} %broadcast_in_dim.30), calls=%async_computation.4 | async-start | bytes 524288 | tf_op jit(solution)/shard_map/all_to_all | solution.py:16
  165.1 17.6 %all-to-all-start.8 = ((bf16[64,16,128]{2,1,0:T(8,128)(2,1)}), bf16[64,16,128]{2,1,0:T(8,128)(2,1)S(1)}, u32[]{:S(2)}, u32[]{:S(2)}) async-start(bf16[64,16,128]{2,1,0:T(8,128)(2,1)} %broadcast_in_dim.67), calls=%async_computation.8 | async-start | bytes 524288 | tf_op jit(solution)/shard_map/all_to_all | solution.py:16
  170.4 5.5 %slice-start = ((f32[4,16,128]{2,1,0:T(8,128)}), f32[1,16,128]{2,1,0:T(8,128)S(1)}, s32[]{:S(2)}) async-start(f32[4,16,128]{2,1,0:T(8,128)} %copy-done), calls=%async_computation.12 | async-start | bytes 16384 | tf_op jit(solution)/shard_map/slice | solution.py:156
  186.2 18.5 %all-to-all-start.9 = ((f32[8,2,16,128]{3,2,1,0:T(8,128)}), f32[8,2,16,128]{3,2,1,0:T(8,128)S(1)}, u32[]{:S(2)}, u32[]{:S(2)}) async-start(f32[8,2,16,128]{3,2,1,0:T(8,128)} %shard_map.29), calls=%async_computation.9 | async-start | bytes 262144 | tf_op jit(solution)/shard_map/all_to_all | solution.py:16
Sparse Core Ops, SparseCore 0:
  9.8 61.2 all-gather.6
  73.2 55.2 all-gather.8

commit v14 on v13

--- a/solution.py
+++ b/solution.py
@@ -95,6 +95,17 @@
                 value = jnp.where(owner, solved[x], value)
             for core in range(out.shape[0] // xs):
                 out[x * (out.shape[0] // xs) + core, index] = value
+
+
+def output_kernel(owner_ref, core_ref, back, given, out):
+    lines, rounds, few, pair = back.shape
+    share = out.shape[1]
+    owner, first = owner_ref[0] == 0, core_ref[0] == 0
+    for index in range(rounds):
+        rows = back[:, index].reshape(lines * few, pair).T
+        rows = jnp.where(first, rows[:share], rows[share:])
+        value = given[index] - rows
+        out[index] = jnp.where(owner, rows, value) if index == 0 else value
 
 
 def streaming(kernel, span, tiles, early, out_shape, spaces):
@@ -188,11 +199,14 @@
         [pltpu.SMEM] + [pltpu.VMEM] * 3 + [pl.ANY] * 2,
     )(lax.axis_index("yl")[None], got, sofar, jnp.stack(solved), early, late)
     back = exchange(both, ("x", "c"))
-    owner = lax.axis_index("yl") == 0
-    back = jnp.swapaxes(back, 0, 1).reshape(2, cases, pair).transpose(0, 2, 1)
-    back = lax.dynamic_slice_in_dim(back, lax.axis_index("c") * share, share, 1)
-    top = jnp.where(owner, back[0], given[0] - back[0])
-    return jnp.stack([top, given[1] - back[1]])[:, None]
+    result = pl.pallas_call(
+        output_kernel,
+        out_shape=jax.ShapeDtypeStruct(given.shape, jnp.float32),
+        in_specs=[pl.BlockSpec(memory_space=pltpu.SMEM)] * 2
+        + [pl.BlockSpec(memory_space=pltpu.VMEM)] * 2,
+        out_specs=pl.BlockSpec(memory_space=pltpu.VMEM),
+    )(lax.axis_index("yl")[None], lax.axis_index("c")[None], back, given)
+    return result[:, None]
 
 
 def solution(mesh):

time: 213 us -> 213 us (level)
  blocking collectives: 90.2 us -> 108 us
  starting transfers between devices: 38.5 us -> 25.3 us
  waiting for transfers between devices: 46.4 us -> 41.3 us
    all_to_all x5 -> x6, blocking collectives: 79.1 us -> 97.3 us  [exchange(): return lax.all_to_all(parts, axis, 0, 0, tiled=True)]
    all_to_all x5 -> x4, starting transfers between devices: 38.4 us -> 25.2 us  [exchange(): return lax.all_to_all(parts, axis, 0, 0, tiled=True)]
    all_to_all x5 -> x4, waiting for transfers between devices: 45.6 us -> 40.5 us  [exchange(): return lax.all_to_all(parts, axis, 0, 0, tiled=True)]
  transfers between devices with their start and end apart: 7 -> 6, of which waited for: 5 -> 4; matrix products, arithmetic and copies ran while one was open for 5% -> 5% of each run, Pallas kernels for 3% -> 3%
where the time goes in v14:
time: 213 us; the launch traced here: 212 us
  blocking collectives  108 us (51%)
  waiting for transfers between devices  41.3 us (19%)
  starting transfers between devices  25.3 us (12%)
  between operations  13.7 us (6%)
  local copies, waits for them, and re-layouts  11 us (5%)
  Pallas kernels  9.85 us (5%)
  matrix products  2.47 us (1%)
    all_to_all x6, blocking collectives, exchange(): return lax.all_to_all(parts, axis, 0, 0, tiled=True)  97.3 us
    all_to_all x4, waiting for transfers between devices, exchange(): return lax.all_to_all(parts, axis, 0, 0, tiled=True)  40.5 us
    all_to_all x4, starting transfers between devices, exchange(): return lax.all_to_all(parts, axis, 0, 0, tiled=True)  25.2 us
    all_gather x1, blocking collectives, body(): together = lax.all_gather(given[0], 'c', axis=0, tiled=True).T  8.38 us
    pallas_call x1, Pallas kernels, body(): streaming(first_kernel, (0, last), TILES[0], early, (2, few, xs * pair),...  5.45 us
  transfers between devices with their start and end apart: 6, of which 4 were waited for; matrix products, arithmetic and copies ran while one was open for 5% of the time, Pallas kernels for 3%

profile of v14, /device:TPU:1, one launch (start us, length us, event | category | flops | bytes accessed | tf_op | source)
XLA Modules:
  0.0 212.3 jit_solution(15600501932460107603)
XLA Ops:
  6.5 0.0 all-gather.7.cloned.1.call-start
  6.5 3.1 %fusion.52 = (bf16[1,1,64,8192]{3,2,1,0:T(8,128)(2,1)}, bf16[1,1,64,8192]{3,2,1,0:T(8,128)(2,1)}) fusion(bf16[2,1,64,8192]{3,2,1,0:T(8,128)(2,1)} %param.2), kind=kLoop, calls=%fused_computation.90 | loop fusion | bytes 4194304 | tf_op jit(solution)/shard_map/slice | solution.py:145
  9.6 0.0 all-gather.7.cloned.1.call-update
  9.6 0.0 all-gather.9.cloned.1.call-start
  9.7 0.7 all-gather.9.cloned.1.call-update
  10.4 0.0 slice-done.1
  10.4 8.4 %all-gather = f32[1,1,128,128]{3,1,0,2:T(1,128)S(1)} all-gather(f32[1,1,64,128]{3,1,0,2:T(1,128)S(1)} %bitcast.148), channel_id=2, replica_groups=mesh['yl'=4,'x'=4,'z'=8,'yh'=2,'c'=2] {'c'}, dimensions={2}, use_global_device_ids=true | all-gather | bytes 98304 | tf_op jit(solution)/shard_map/all_gather | solution.py:156
  18.8 0.1 copy.15
  18.9 0.9 broadcast_in_dim.29
  19.8 10.0 %all-to-all-start = ((f32[16,64,128]{2,1,0:T(8,128)}), f32[16,64,128]{2,1,0:T(8,128)S(1)}, u32[]{:S(2)}, u32[]{:S(2)}) async-start(f32[16,64,128]{2,1,0:T(8,128)} %broadcast_in_dim.29), calls=%async_computation | async-start | bytes 1048576 | tf_op jit(solution)/shard_map/all_to_all | solution.py:16
  29.8 1.0 slice.135
  30.8 2.8 %all-gather.1 = bf16[1,128,2048]{2,1,0:T(8,128)(2,1)S(1)} all-gather(bf16[1,64,2048]{2,1,0:T(8,128)(2,1)S(1)} %slice.135), channel_id=3, replica_groups=mesh['yl'=4,'x'=4,'z'=8,'yh'=2,'c'=2] {'c'}, dimensions={1}, use_global_device_ids=true | all-gather | bytes 786432 | tf_op jit(solution)/shard_map/all_gather | solution.py:161
  33.6 11.1 %all-to-all-done = f32[16,64,128]{2,1,0:T(8,128)S(1)} async-done(((f32[16,64,128]{2,1,0:T(8,128)}), f32[16,64,128]{2,1,0:T(8,128)S(1)}, u32[]{:S(2)}, u32[]{:S(2)}) %all-to-all-start) | async-done | bytes 524320 | tf_op jit(solution)/shard_map/all_to_all | solution.py:16
  44.8 0.1 reduce-precision_convert_fusion.1
  44.9 0.4 fusion.1
  45.3 8.5 %all_to_all.50 = f32[4,16,128]{2,1,0:T(8,128)S(1)} all-to-all(f32[4,16,128]{2,1,0:T(8,128)S(1)} %bitcast.149), channel_id=1, replica_groups=mesh['yl'=4,'x'=4,'z'=8,'yh'=2,'c'=2] {'x'}, dimensions={0} | all-to-all | bytes 65536 | tf_op jit(solution)/shard_map/all_to_all | solution.py:16
  53.8 0.0 copy-start
  53.8 23.9 %all_to_all.51 = bf16[64,16,128]{2,1,0:T(8,128)(2,1)S(1)} all-to-all(bf16[64,16,128]{2,1,0:T(8,128)(2,1)S(1)} %broadcast_in_dim.31), channel_id=1, replica_groups=mesh['yl'=4,'x'=4,'z'=8,'yh'=2,'c'=2] {'yl','z','yh'}, dimensions={0} | all-to-all | bytes 524288 | tf_op jit(solution)/shard_map/all_to_all | solution.py:16
  77.8 0.0 all-gather.7.cloned.1.call-done
  77.8 1.9 fusion.51
  79.7 0.2 convolution_subtract_fusion.1
  79.9 0.7 broadcast_in_dim.32
  80.6 5.4 %all-to-all-start.3 = ((f32[16,16,128]{2,1,0:T(8,128)}), f32[16,16,128]{2,1,0:T(8,128)S(1)}, u32[]{:S(2)}, u32[]{:S(2)}) async-start(f32[16,16,128]{2,1,0:T(8,128)} %broadcast_in_dim.32), calls=%async_computation.3 | async-start | bytes 262144 | tf_op jit(solution)/shard_map/all_to_all | solution.py:16
  86.0 11.8 %all-to-all-done.3 = f32[16,16,128]{2,1,0:T(8,128)S(1)} async-done(((f32[16,16,128]{2,1,0:T(8,128)}), f32[16,16,128]{2,1,0:T(8,128)S(1)}, u32[]{:S(2)}, u32[]{:S(2)}) %all-to-all-start.3) | async-done | bytes 131104 | tf_op jit(solution)/shard_map/all_to_all | solution.py:16
  97.9 0.3 fusion.9
  98.2 0.7 broadcast_in_dim.33
  98.9 4.6 %all-to-all-start.4 = ((bf16[64,16,128]{2,1,0:T(8,128)(2,1)}), bf16[64,16,128]{2,1,0:T(8,128)(2,1)S(1)}, u32[]{:S(2)}, u32[]{:S(2)}) async-start(bf16[64,16,128]{2,1,0:T(8,128)(2,1)} %broadcast_in_dim.33), calls=%async_computation.4 | async-start | bytes 524288 | tf_op jit(solution)/shard_map/all_to_all | solution.py:16
  103.5 1.7 fusion.50
  105.2 0.4 fusion
  105.6 10.7 %all-to-all-done.4 = bf16[64,16,128]{2,1,0:T(8,128)(2,1)S(1)} async-done(((bf16[64,16,128]{2,1,0:T(8,128)(2,1)}), bf16[64,16,128]{2,1,0:T(8,128)(2,1)S(1)}, u32[]{:S(2)}, u32[]{:S(2)}) %all-to-all-start.4) | async-done | bytes 262176 | tf_op jit(solution)/shard_map/all_to_all | solution.py:16
  116.3 0.4 fusion.32
  116.7 14.6 %all_to_all.52 = f32[16,16,128]{2,1,0:T(8,128)S(1)} all-to-all(f32[16,16,128]{2,1,0:T(8,128)S(1)} %broadcast_in_dim.34), channel_id=1, replica_groups=mesh['yl'=4,'x'=4,'z'=8,'yh'=2,'c'=2] {'z','yh'}, dimensions={0} | all-to-all | bytes 262144 | tf_op jit(solution)/shard_map/all_to_all | solution.py:16
  131.3 0.3 fusion.15
  131.7 17.4 %all_to_all.53 = bf16[64,16,128]{2,1,0:T(8,128)(2,1)S(1)} all-to-all(bf16[64,16,128]{2,1,0:T(8,128)(2,1)S(1)} %broadcast_in_dim.70), channel_id=1, replica_groups=mesh['yl'=4,'x'=4,'z'=8,'yh'=2,'c'=2] {'yl','z','yh'}, dimensions={0} | all-to-all | bytes 524288 | tf_op jit(solution)/shard_map/all_to_all | solution.py:16
  149.1 0.2 convolution_subtract_fusion
  149.4 14.6 %all_to_all.54 = f32[16,16,128]{2,1,0:T(8,128)S(1)} all-to-all(f32[16,16,128]{2,1,0:T(8,128)S(1)} %broadcast_in_dim.71), channel_id=1, replica_groups=mesh['yl'=4,'x'=4,'z'=8,'yh'=2,'c'=2] {'z','yh'}, dimensions={0} | all-to-all | bytes 262144 | tf_op jit(solution)/shard_map/all_to_all | solution.py:16
  164.1 0.3 fusion.21
  164.4 0.7 broadcast_in_dim.72
  165.1 5.2 %all-to-all-start.8 = ((bf16[64,16,128]{2,1,0:T(8,128)(2,1)}), bf16[64,16,128]{2,1,0:T(8,128)(2,1)S(1)}, u32[]{:S(2)}, u32[]{:S(2)}) async-start(bf16[64,16,128]{2,1,0:T(8,128)(2,1)} %broadcast_in_dim.72), calls=%async_computation.8 | async-start | bytes 524288 | tf_op jit(solution)/shard_map/all_to_all | solution.py:16
  170.3 0.0 copy-done
  170.4 0.0 all-gather.9.cloned.1.call-done
  170.4 0.0 slice-start
  170.4 5.5 %shard_map.28.sofar = f32[2,16,512]{2,1,0:T(8,128)S(1)} custom-call(bf16[16,16,128]{2,1,0:T(8,128)(2,1)S(1)} %get-tuple-element.21.refs_0_, bf16[16,16,128]{2,1,0:T(8,128)(2,1)S(1)} %get-tuple-element.19.refs_1_, bf16[16,16,128]{2,1,0:T(8,128)(2,1)S(1)} %get-tuple-element.17.refs_2_, bf16[8,64,8192]{2,1,0:T(8,128)(2,1)} %bitcast.133, ...), custom_call_target="tpu_custom_call" | custom-call | flops 201326592 | bytes 12582912 | tf_op jit(solution)/shard_map/pallas_call | solution.py:185
  175.9 0.0 slice-done
  175.9 6.9 %all-to-all-done.8.got = bf16[64,16,128]{2,1,0:T(8,128)(2,1)S(1)} async-done(((bf16[64,16,128]{2,1,0:T(8,128)(2,1)}), bf16[64,16,128]{2,1,0:T(8,128)(2,1)S(1)}, u32[]{:S(2)}, u32[]{:S(2)}) %all-to-all-start.8) | async-done | bytes 262176 | tf_op jit(solution)/shard_map/all_to_all | solution.py:16
  182.8 2.8 %shard_map.29 = f32[8,2,16,128]{3,2,1,0:T(8,128)S(1)} custom-call(s32[1]{0:T(128)} %bitcast.owner_ref, bf16[64,16,128]{2,1,0:T(8,128)(2,1)S(1)} %all-to-all-done.8.got, f32[2,16,512]{2,1,0:T(8,128)S(1)} %shard_map.28.sofar, f32[4,16,128]{2,1,0:T(8,128)S(1)} %pad_maximum_fusion.solved, bf16[8,64,8192]{2,1,0:T(8,128)(2,1)} %bitcast.134, ...), custom_call_target="tpu_custom_call" | custom-call | flops 67108864 | bytes 4194304 | tf_op jit(solution)/shard_map/pallas_call | solution.py:193
  185.6 18.3 %all_to_all.55.back = f32[8,2,16,128]{3,2,1,0:T(8,128)} all-to-all(f32[8,2,16,128]{3,2,1,0:T(8,128)S(1)} %shard_map.29), channel_id=1, replica_groups=mesh['yl'=4,'x'=4,'z'=8,'yh'=2,'c'=2] {'x','c'}, dimensions={0} | all-to-all | bytes 262144 | tf_op jit(solution)/shard_map/all_to_all | solution.py:16
  203.8 1.6 shard_map.30
  (21 shorter events, 0.4 us)
Async XLA Ops:
  6.5 71.2 %all-gather.7.cloned.1.call-start = ((), (), s32[]{:S(2)}) async-start(), calls=%async_computation.10 | async-start | bytes 9437184 | tf_op jit(solution)/shard_map/all_gather | solution.py:144
  9.6 0.8 slice-start.1
  9.6 160.7 %all-gather.9.cloned.1.call-start = ((), (), s32[]{:S(2)}) async-start(), calls=%async_computation.11 | async-start | bytes 9437184 | tf_op jit(solution)/shard_map/all_gather | solution.py:145
  19.8 25.0 %all-to-all-start = ((f32[16,64,128]{2,1,0:T(8,128)}), f32[16,64,128]{2,1,0:T(8,128)S(1)}, u32[]{:S(2)}, u32[]{:S(2)}) async-start(f32[16,64,128]{2,1,0:T(8,128)} %broadcast_in_dim.29), calls=%async_computation | async-start | bytes 1048576 | tf_op jit(solution)/shard_map/all_to_all | solution.py:16
  53.8 116.6 %copy-start = (f32[4,16,128]{2,1,0:T(8,128)}, f32[4,16,128]{2,1,0:T(8,128)S(1)}, u32[]{:S(2)}) copy-start(f32[4,16,128]{2,1,0:T(8,128)S(1)} %all_to_all.50) | copy-start | bytes 98308
  80.6 17.3 %all-to-all-start.3 = ((f32[16,16,128]{2,1,0:T(8,128)}), f32[16,16,128]{2,1,0:T(8,128)S(1)}, u32[]{:S(2)}, u32[]{:S(2)}) async-start(f32[16,16,128]{2,1,0:T(8,128)} %broadcast_in_dim.32), calls=%async_computation.3 | async-start | bytes 262144 | tf_op jit(solution)/shard_map/all_to_all | solution.py:16
  98.9 17.4 %all-to-all-start.4 = ((bf16[64,16,128]{2,1,0:T(8,128)(2,1)}), bf16[64,16,128]{2,1,0:T(8,128)(2,1)S(1)}, u32[]{:S(2)}, u32[]{:S(2)}) async-start(bf16[64,16,128]{2,1,0:T(8,128)(2,1)} %broadcast_in_dim.33), calls=%async_computation.4 | async-start | bytes 524288 | tf_op jit(solution)/shard_map/all_to_all | solution.py:16
  165.1 17.7 %all-to-all-start.8 = ((bf16[64,16,128]{2,1,0:T(8,128)(2,1)}), bf16[64,16,128]{2,1,0:T(8,128)(2,1)S(1)}, u32[]{:S(2)}, u32[]{:S(2)}) async-start(bf16[64,16,128]{2,1,0:T(8,128)(2,1)} %broadcast_in_dim.72), calls=%async_computation.8 | async-start | bytes 524288 | tf_op jit(solution)/shard_map/all_to_all | solution.py:16
  170.4 5.5 %slice-start = ((f32[4,16,128]{2,1,0:T(8,128)}), f32[1,16,128]{2,1,0:T(8,128)S(1)}, s32[]{:S(2)}) async-start(f32[4,16,128]{2,1,0:T(8,128)} %copy-done), calls=%async_computation.12 | async-start | bytes 16384 | tf_op jit(solution)/shard_map/slice | solution.py:167
Sparse Core Ops, SparseCore 0:
  9.8 61.2 all-gather.6
  73.2 55.2 all-gather.8

commit v15 on v14

--- a/solution.py
+++ b/solution.py
@@ -172,6 +172,7 @@
         whole = jnp.swapaxes(got, 0, 1).reshape(few, block)
         if step == 1:
             first = state[0] - times(whole, panel(step, step - 1)[:pair])
+            early, first = lax.optimization_barrier((early, first))
             rest = times(whole, panel(step + 1, step - 1))
         else:
             rest = times(whole, panel(step, step - 1))

time: 213 us -> 212 us (level)
  no operation moved by 1% of the time
where the time goes in v15:
time: 212 us
  blocking collectives  109 us (51%)
  waiting for transfers between devices  39.7 us (19%)
  starting transfers between devices  25.2 us (12%)
  between operations  13.7 us (6%)
  local copies, waits for them, and re-layouts  11.9 us (6%)
  Pallas kernels  9.85 us (5%)
  matrix products  2.47 us (1%)
    all_to_all x6, blocking collectives, exchange(): return lax.all_to_all(parts, axis, 0, 0, tiled=True)  97.3 us
    all_to_all x4, waiting for transfers between devices, exchange(): return lax.all_to_all(parts, axis, 0, 0, tiled=True)  38.9 us
    all_to_all x4, starting transfers between devices, exchange(): return lax.all_to_all(parts, axis, 0, 0, tiled=True)  25.2 us
    all_gather x1, blocking collectives, body(): together = lax.all_gather(given[0], 'c', axis=0, tiled=True).T  8.38 us
    pallas_call x1, Pallas kernels, body(): streaming(first_kernel, (0, last), TILES[0], early, (2, few, xs * pair),...  5.45 us
  transfers between devices with their start and end apart: 6, of which 4 were waited for; matrix products, arithmetic and copies ran while one was open for 5% of the time, Pallas kernels for 3%

profile of v15, /device:TPU:1, one launch (start us, length us, event | category | flops | bytes accessed | tf_op | source)
XLA Modules:
  0.0 211.6 jit_solution(12888651489780859677)
XLA Ops:
  6.5 0.0 all-gather.7.cloned.1.call-start
  6.5 3.1 %fusion.52 = (bf16[1,1,64,8192]{3,2,1,0:T(8,128)(2,1)}, bf16[1,1,64,8192]{3,2,1,0:T(8,128)(2,1)}) fusion(bf16[2,1,64,8192]{3,2,1,0:T(8,128)(2,1)} %param.2), kind=kLoop, calls=%fused_computation.90 | loop fusion | bytes 4194304 | tf_op jit(solution)/shard_map/slice | solution.py:145
  9.6 0.0 all-gather.7.cloned.1.call-update
  9.6 0.0 all-gather.9.cloned.1.call-start
  9.7 0.7 all-gather.9.cloned.1.call-update
  10.4 0.0 slice-done.1
  10.4 8.4 %all-gather = f32[1,1,128,128]{3,1,0,2:T(1,128)S(1)} all-gather(f32[1,1,64,128]{3,1,0,2:T(1,128)S(1)} %bitcast.149), channel_id=2, replica_groups=mesh['yl'=4,'x'=4,'z'=8,'yh'=2,'c'=2] {'c'}, dimensions={2}, use_global_device_ids=true | all-gather | bytes 98304 | tf_op jit(solution)/shard_map/all_gather | solution.py:156
  18.8 0.1 copy.15
  18.9 0.9 broadcast_in_dim.29
  19.8 10.0 %all-to-all-start = ((f32[16,64,128]{2,1,0:T(8,128)}), f32[16,64,128]{2,1,0:T(8,128)S(1)}, u32[]{:S(2)}, u32[]{:S(2)}) async-start(f32[16,64,128]{2,1,0:T(8,128)} %broadcast_in_dim.29), calls=%async_computation | async-start | bytes 1048576 | tf_op jit(solution)/shard_map/all_to_all | solution.py:16
  29.8 1.0 slice.135
  30.8 2.8 %all-gather.1 = bf16[1,128,2048]{2,1,0:T(8,128)(2,1)S(1)} all-gather(bf16[1,64,2048]{2,1,0:T(8,128)(2,1)S(1)} %slice.135), channel_id=3, replica_groups=mesh['yl'=4,'x'=4,'z'=8,'yh'=2,'c'=2] {'c'}, dimensions={1}, use_global_device_ids=true | all-gather | bytes 786432 | tf_op jit(solution)/shard_map/all_gather | solution.py:161
  33.6 11.1 %all-to-all-done = f32[16,64,128]{2,1,0:T(8,128)S(1)} async-done(((f32[16,64,128]{2,1,0:T(8,128)}), f32[16,64,128]{2,1,0:T(8,128)S(1)}, u32[]{:S(2)}, u32[]{:S(2)}) %all-to-all-start) | async-done | bytes 524320 | tf_op jit(solution)/shard_map/all_to_all | solution.py:16
  44.8 0.1 reduce-precision_convert_fusion.1
  44.9 0.4 fusion.1
  45.3 8.5 %all_to_all.50 = f32[4,16,128]{2,1,0:T(8,128)S(1)} all-to-all(f32[4,16,128]{2,1,0:T(8,128)S(1)} %bitcast.150), channel_id=1, replica_groups=mesh['yl'=4,'x'=4,'z'=8,'yh'=2,'c'=2] {'x'}, dimensions={0} | all-to-all | bytes 65536 | tf_op jit(solution)/shard_map/all_to_all | solution.py:16
  53.8 23.9 %all_to_all.51 = bf16[64,16,128]{2,1,0:T(8,128)(2,1)S(1)} all-to-all(bf16[64,16,128]{2,1,0:T(8,128)(2,1)S(1)} %broadcast_in_dim.31), channel_id=1, replica_groups=mesh['yl'=4,'x'=4,'z'=8,'yh'=2,'c'=2] {'yl','z','yh'}, dimensions={0} | all-to-all | bytes 524288 | tf_op jit(solution)/shard_map/all_to_all | solution.py:16
  77.8 0.0 all-gather.7.cloned.1.call-done
  77.9 1.1 slice.140
  78.9 0.2 convolution_subtract_fusion.1
  79.2 0.7 broadcast_in_dim.32
  79.8 5.3 %all-to-all-start.3 = ((f32[16,16,128]{2,1,0:T(8,128)}), f32[16,16,128]{2,1,0:T(8,128)S(1)}, u32[]{:S(2)}, u32[]{:S(2)}) async-start(f32[16,16,128]{2,1,0:T(8,128)} %broadcast_in_dim.32), calls=%async_computation.3 | async-start | bytes 262144 | tf_op jit(solution)/shard_map/all_to_all | solution.py:16
  85.2 1.7 fusion.51
  86.9 10.2 %all-to-all-done.3 = f32[16,16,128]{2,1,0:T(8,128)S(1)} async-done(((f32[16,16,128]{2,1,0:T(8,128)}), f32[16,16,128]{2,1,0:T(8,128)S(1)}, u32[]{:S(2)}, u32[]{:S(2)}) %all-to-all-start.3) | async-done | bytes 131104 | tf_op jit(solution)/shard_map/all_to_all | solution.py:16
  97.1 0.3 fusion.9
  97.4 0.7 broadcast_in_dim.33
  98.1 4.6 %all-to-all-start.4 = ((bf16[64,16,128]{2,1,0:T(8,128)(2,1)}), bf16[64,16,128]{2,1,0:T(8,128)(2,1)S(1)}, u32[]{:S(2)}, u32[]{:S(2)}) async-start(bf16[64,16,128]{2,1,0:T(8,128)(2,1)} %broadcast_in_dim.33), calls=%async_computation.4 | async-start | bytes 524288 | tf_op jit(solution)/shard_map/all_to_all | solution.py:16
  102.8 1.7 fusion.50
  104.4 0.4 fusion
  104.8 10.7 %all-to-all-done.4 = bf16[64,16,128]{2,1,0:T(8,128)(2,1)S(1)} async-done(((bf16[64,16,128]{2,1,0:T(8,128)(2,1)}), bf16[64,16,128]{2,1,0:T(8,128)(2,1)S(1)}, u32[]{:S(2)}, u32[]{:S(2)}) %all-to-all-start.4) | async-done | bytes 262176 | tf_op jit(solution)/shard_map/all_to_all | solution.py:16
  115.5 0.4 fusion.32
  115.9 14.5 %all_to_all.52 = f32[16,16,128]{2,1,0:T(8,128)S(1)} all-to-all(f32[16,16,128]{2,1,0:T(8,128)S(1)} %broadcast_in_dim.34), channel_id=1, replica_groups=mesh['yl'=4,'x'=4,'z'=8,'yh'=2,'c'=2] {'z','yh'}, dimensions={0} | all-to-all | bytes 262144 | tf_op jit(solution)/shard_map/all_to_all | solution.py:16
  130.5 0.3 fusion.15
  130.9 17.5 %all_to_all.53 = bf16[64,16,128]{2,1,0:T(8,128)(2,1)S(1)} all-to-all(bf16[64,16,128]{2,1,0:T(8,128)(2,1)S(1)} %broadcast_in_dim.70), channel_id=1, replica_groups=mesh['yl'=4,'x'=4,'z'=8,'yh'=2,'c'=2] {'yl','z','yh'}, dimensions={0} | all-to-all | bytes 524288 | tf_op jit(solution)/shard_map/all_to_all | solution.py:16
  148.4 0.2 convolution_subtract_fusion
  148.7 14.6 %all_to_all.54 = f32[16,16,128]{2,1,0:T(8,128)S(1)} all-to-all(f32[16,16,128]{2,1,0:T(8,128)S(1)} %broadcast_in_dim.71), channel_id=1, replica_groups=mesh['yl'=4,'x'=4,'z'=8,'yh'=2,'c'=2] {'z','yh'}, dimensions={0} | all-to-all | bytes 262144 | tf_op jit(solution)/shard_map/all_to_all | solution.py:16
  163.3 0.3 fusion.21
  163.6 0.7 broadcast_in_dim.72
  164.4 5.2 %all-to-all-start.8 = ((bf16[64,16,128]{2,1,0:T(8,128)(2,1)}), bf16[64,16,128]{2,1,0:T(8,128)(2,1)S(1)}, u32[]{:S(2)}, u32[]{:S(2)}) async-start(bf16[64,16,128]{2,1,0:T(8,128)(2,1)} %broadcast_in_dim.72), calls=%async_computation.8 | async-start | bytes 524288 | tf_op jit(solution)/shard_map/all_to_all | solution.py:16
  169.6 0.0 copy-done
  169.6 0.0 all-gather.9.cloned.1.call-done
  169.6 0.0 slice-start
  169.6 5.5 %shard_map.28.sofar = f32[2,16,512]{2,1,0:T(8,128)S(1)} custom-call(bf16[16,16,128]{2,1,0:T(8,128)(2,1)S(1)} %get-tuple-element.24.refs_0_, bf16[16,16,128]{2,1,0:T(8,128)(2,1)S(1)} %get-tuple-element.22.refs_1_, bf16[16,16,128]{2,1,0:T(8,128)(2,1)S(1)} %get-tuple-element.20.refs_2_, bf16[8,64,8192]{2,1,0:T(8,128)(2,1)} %bitcast.134, ...), custom_call_target="tpu_custom_call" | custom-call | flops 201326592 | bytes 12582912 | tf_op jit(solution)/shard_map/pallas_call | solution.py:186
  175.1 0.0 slice-done
  175.1 6.9 %all-to-all-done.8.got = bf16[64,16,128]{2,1,0:T(8,128)(2,1)S(1)} async-done(((bf16[64,16,128]{2,1,0:T(8,128)(2,1)}), bf16[64,16,128]{2,1,0:T(8,128)(2,1)S(1)}, u32[]{:S(2)}, u32[]{:S(2)}) %all-to-all-start.8) | async-done | bytes 262176 | tf_op jit(solution)/shard_map/all_to_all | solution.py:16
  182.0 2.8 %shard_map.29 = f32[8,2,16,128]{3,2,1,0:T(8,128)S(1)} custom-call(s32[1]{0:T(128)} %bitcast.owner_ref, bf16[64,16,128]{2,1,0:T(8,128)(2,1)S(1)} %all-to-all-done.8.got, f32[2,16,512]{2,1,0:T(8,128)S(1)} %shard_map.28.sofar, f32[4,16,128]{2,1,0:T(8,128)S(1)} %pad_maximum_fusion.solved, bf16[8,64,8192]{2,1,0:T(8,128)(2,1)} %bitcast.135, ...), custom_call_target="tpu_custom_call" | custom-call | flops 67108864 | bytes 4194304 | tf_op jit(solution)/shard_map/pallas_call | solution.py:194
  184.8 18.3 %all_to_all.55.back = f32[8,2,16,128]{3,2,1,0:T(8,128)} all-to-all(f32[8,2,16,128]{3,2,1,0:T(8,128)S(1)} %shard_map.29), channel_id=1, replica_groups=mesh['yl'=4,'x'=4,'z'=8,'yh'=2,'c'=2] {'x','c'}, dimensions={0} | all-to-all | bytes 262144 | tf_op jit(solution)/shard_map/all_to_all | solution.py:16
  203.1 1.6 shard_map.30
  (22 shorter events, 0.4 us)
Async XLA Ops:
  6.5 71.3 %all-gather.7.cloned.1.call-start = ((), (), s32[]{:S(2)}) async-start(), calls=%async_computation.10 | async-start | bytes 9437184 | tf_op jit(solution)/shard_map/all_gather | solution.py:144
  9.6 0.8 slice-start.1
  9.6 160.0 %all-gather.9.cloned.1.call-start = ((), (), s32[]{:S(2)}) async-start(), calls=%async_computation.11 | async-start | bytes 9437184 | tf_op jit(solution)/shard_map/all_gather | solution.py:145
  19.8 25.0 %all-to-all-start = ((f32[16,64,128]{2,1,0:T(8,128)}), f32[16,64,128]{2,1,0:T(8,128)S(1)}, u32[]{:S(2)}, u32[]{:S(2)}) async-start(f32[16,64,128]{2,1,0:T(8,128)} %broadcast_in_dim.29), calls=%async_computation | async-start | bytes 1048576 | tf_op jit(solution)/shard_map/all_to_all | solution.py:16
  53.8 115.8 %copy-start = (f32[4,16,128]{2,1,0:T(8,128)}, f32[4,16,128]{2,1,0:T(8,128)S(1)}, u32[]{:S(2)}) copy-start(f32[4,16,128]{2,1,0:T(8,128)S(1)} %all_to_all.50) | copy-start | bytes 98308
  79.8 17.2 %all-to-all-start.3 = ((f32[16,16,128]{2,1,0:T(8,128)}), f32[16,16,128]{2,1,0:T(8,128)S(1)}, u32[]{:S(2)}, u32[]{:S(2)}) async-start(f32[16,16,128]{2,1,0:T(8,128)} %broadcast_in_dim.32), calls=%async_computation.3 | async-start | bytes 262144 | tf_op jit(solution)/shard_map/all_to_all | solution.py:16
  98.1 17.4 %all-to-all-start.4 = ((bf16[64,16,128]{2,1,0:T(8,128)(2,1)}), bf16[64,16,128]{2,1,0:T(8,128)(2,1)S(1)}, u32[]{:S(2)}, u32[]{:S(2)}) async-start(bf16[64,16,128]{2,1,0:T(8,128)(2,1)} %broadcast_in_dim.33), calls=%async_computation.4 | async-start | bytes 524288 | tf_op jit(solution)/shard_map/all_to_all | solution.py:16
  164.4 17.7 %all-to-all-start.8 = ((bf16[64,16,128]{2,1,0:T(8,128)(2,1)}), bf16[64,16,128]{2,1,0:T(8,128)(2,1)S(1)}, u32[]{:S(2)}, u32[]{:S(2)}) async-start(bf16[64,16,128]{2,1,0:T(8,128)(2,1)} %broadcast_in_dim.72), calls=%async_computation.8 | async-start | bytes 524288 | tf_op jit(solution)/shard_map/all_to_all | solution.py:16
  169.6 5.5 %slice-start = ((f32[4,16,128]{2,1,0:T(8,128)}), f32[1,16,128]{2,1,0:T(8,128)S(1)}, s32[]{:S(2)}) async-start(f32[4,16,128]{2,1,0:T(8,128)} %copy-done), calls=%async_computation.12 | async-start | bytes 16384 | tf_op jit(solution)/shard_map/slice | solution.py:167
Sparse Core Ops, SparseCore 0:
  9.8 61.2 all-gather.6
  73.2 55.2 all-gather.8

commit v16 on v15

--- a/solution.py
+++ b/solution.py
@@ -41,7 +41,7 @@
     return (c + b) + a
 
 
-TILES = ((1024, 6), (512, 8))
+TILES = ((1024, 6), (256, 16))
 
 
 def stream(plan, early_ref, late_ref, held, sems, cases_of):

time: 212 us -> 212 us (level)
  no operation moved by 1% of the time
where the time goes in v16:
time: 212 us; the launch traced here: 211 us
  blocking collectives  109 us (51%)
  waiting for transfers between devices  39.7 us (19%)
  starting transfers between devices  25.2 us (12%)
  between operations  13.7 us (6%)
  local copies, waits for them, and re-layouts  11.9 us (6%)
  Pallas kernels  9.71 us (5%)
  matrix products  2.47 us (1%)
    all_to_all x6, blocking collectives, exchange(): return lax.all_to_all(parts, axis, 0, 0, tiled=True)  97.3 us
    all_to_all x4, waiting for transfers between devices, exchange(): return lax.all_to_all(parts, axis, 0, 0, tiled=True)  38.9 us
    all_to_all x4, starting transfers between devices, exchange(): return lax.all_to_all(parts, axis, 0, 0, tiled=True)  25.2 us
    all_gather x1, blocking collectives, body(): together = lax.all_gather(given[0], 'c', axis=0, tiled=True).T  8.38 us
    pallas_call x1, Pallas kernels, body(): streaming(first_kernel, (0, last), TILES[0], early, (2, few, xs * pair),...  5.45 us
  transfers between devices with their start and end apart: 6, of which 4 were waited for; matrix products, arithmetic and copies ran while one was open for 5% of the time, Pallas kernels for 3%

profile of v16, /device:TPU:1, one launch (start us, length us, event | category | flops | bytes accessed | tf_op | source)
XLA Modules:
  0.0 211.4 jit_solution(18223532433934349423)
XLA Ops:
  6.5 0.0 all-gather.7.cloned.1.call-start
  6.5 3.1 %fusion.52 = (bf16[1,1,64,8192]{3,2,1,0:T(8,128)(2,1)}, bf16[1,1,64,8192]{3,2,1,0:T(8,128)(2,1)}) fusion(bf16[2,1,64,8192]{3,2,1,0:T(8,128)(2,1)} %param.2), kind=kLoop, calls=%fused_computation.90 | loop fusion | bytes 4194304 | tf_op jit(solution)/shard_map/slice | solution.py:145
  9.6 0.0 all-gather.7.cloned.1.call-update
  9.6 0.0 all-gather.9.cloned.1.call-start
  9.7 0.7 all-gather.9.cloned.1.call-update
  10.4 0.0 slice-done.1
  10.4 8.4 %all-gather = f32[1,1,128,128]{3,1,0,2:T(1,128)S(1)} all-gather(f32[1,1,64,128]{3,1,0,2:T(1,128)S(1)} %bitcast.149), channel_id=2, replica_groups=mesh['yl'=4,'x'=4,'z'=8,'yh'=2,'c'=2] {'c'}, dimensions={2}, use_global_device_ids=true | all-gather | bytes 98304 | tf_op jit(solution)/shard_map/all_gather | solution.py:156
  18.8 0.1 copy.15
  18.9 0.9 broadcast_in_dim.29
  19.8 10.0 %all-to-all-start = ((f32[16,64,128]{2,1,0:T(8,128)}), f32[16,64,128]{2,1,0:T(8,128)S(1)}, u32[]{:S(2)}, u32[]{:S(2)}) async-start(f32[16,64,128]{2,1,0:T(8,128)} %broadcast_in_dim.29), calls=%async_computation | async-start | bytes 1048576 | tf_op jit(solution)/shard_map/all_to_all | solution.py:16
  29.8 1.0 slice.135
  30.8 2.8 %all-gather.1 = bf16[1,128,2048]{2,1,0:T(8,128)(2,1)S(1)} all-gather(bf16[1,64,2048]{2,1,0:T(8,128)(2,1)S(1)} %slice.135), channel_id=3, replica_groups=mesh['yl'=4,'x'=4,'z'=8,'yh'=2,'c'=2] {'c'}, dimensions={1}, use_global_device_ids=true | all-gather | bytes 786432 | tf_op jit(solution)/shard_map/all_gather | solution.py:161
  33.6 11.1 %all-to-all-done = f32[16,64,128]{2,1,0:T(8,128)S(1)} async-done(((f32[16,64,128]{2,1,0:T(8,128)}), f32[16,64,128]{2,1,0:T(8,128)S(1)}, u32[]{:S(2)}, u32[]{:S(2)}) %all-to-all-start) | async-done | bytes 524320 | tf_op jit(solution)/shard_map/all_to_all | solution.py:16
  44.8 0.1 reduce-precision_convert_fusion.1
  44.9 0.4 fusion.1
  45.3 8.5 %all_to_all.50 = f32[4,16,128]{2,1,0:T(8,128)S(1)} all-to-all(f32[4,16,128]{2,1,0:T(8,128)S(1)} %bitcast.150), channel_id=1, replica_groups=mesh['yl'=4,'x'=4,'z'=8,'yh'=2,'c'=2] {'x'}, dimensions={0} | all-to-all | bytes 65536 | tf_op jit(solution)/shard_map/all_to_all | solution.py:16
  53.8 23.9 %all_to_all.51 = bf16[64,16,128]{2,1,0:T(8,128)(2,1)S(1)} all-to-all(bf16[64,16,128]{2,1,0:T(8,128)(2,1)S(1)} %broadcast_in_dim.31), channel_id=1, replica_groups=mesh['yl'=4,'x'=4,'z'=8,'yh'=2,'c'=2] {'yl','z','yh'}, dimensions={0} | all-to-all | bytes 524288 | tf_op jit(solution)/shard_map/all_to_all | solution.py:16
  77.8 0.0 all-gather.7.cloned.1.call-done
  77.9 1.1 slice.140
  78.9 0.2 convolution_subtract_fusion.1
  79.2 0.7 broadcast_in_dim.32
  79.8 5.3 %all-to-all-start.3 = ((f32[16,16,128]{2,1,0:T(8,128)}), f32[16,16,128]{2,1,0:T(8,128)S(1)}, u32[]{:S(2)}, u32[]{:S(2)}) async-start(f32[16,16,128]{2,1,0:T(8,128)} %broadcast_in_dim.32), calls=%async_computation.3 | async-start | bytes 262144 | tf_op jit(solution)/shard_map/all_to_all | solution.py:16
  85.2 1.7 fusion.51
  86.9 10.2 %all-to-all-done.3 = f32[16,16,128]{2,1,0:T(8,128)S(1)} async-done(((f32[16,16,128]{2,1,0:T(8,128)}), f32[16,16,128]{2,1,0:T(8,128)S(1)}, u32[]{:S(2)}, u32[]{:S(2)}) %all-to-all-start.3) | async-done | bytes 131104 | tf_op jit(solution)/shard_map/all_to_all | solution.py:16
  97.1 0.3 fusion.9
  97.4 0.7 broadcast_in_dim.33
  98.1 4.6 %all-to-all-start.4 = ((bf16[64,16,128]{2,1,0:T(8,128)(2,1)}), bf16[64,16,128]{2,1,0:T(8,128)(2,1)S(1)}, u32[]{:S(2)}, u32[]{:S(2)}) async-start(bf16[64,16,128]{2,1,0:T(8,128)(2,1)} %broadcast_in_dim.33), calls=%async_computation.4 | async-start | bytes 524288 | tf_op jit(solution)/shard_map/all_to_all | solution.py:16
  102.8 1.7 fusion.50
  104.4 0.4 fusion
  104.8 10.7 %all-to-all-done.4 = bf16[64,16,128]{2,1,0:T(8,128)(2,1)S(1)} async-done(((bf16[64,16,128]{2,1,0:T(8,128)(2,1)}), bf16[64,16,128]{2,1,0:T(8,128)(2,1)S(1)}, u32[]{:S(2)}, u32[]{:S(2)}) %all-to-all-start.4) | async-done | bytes 262176 | tf_op jit(solution)/shard_map/all_to_all | solution.py:16
  115.5 0.4 fusion.32
  115.9 14.5 %all_to_all.52 = f32[16,16,128]{2,1,0:T(8,128)S(1)} all-to-all(f32[16,16,128]{2,1,0:T(8,128)S(1)} %broadcast_in_dim.34), channel_id=1, replica_groups=mesh['yl'=4,'x'=4,'z'=8,'yh'=2,'c'=2] {'z','yh'}, dimensions={0} | all-to-all | bytes 262144 | tf_op jit(solution)/shard_map/all_to_all | solution.py:16
  130.5 0.3 fusion.15
  130.9 17.5 %all_to_all.53 = bf16[64,16,128]{2,1,0:T(8,128)(2,1)S(1)} all-to-all(bf16[64,16,128]{2,1,0:T(8,128)(2,1)S(1)} %broadcast_in_dim.70), channel_id=1, replica_groups=mesh['yl'=4,'x'=4,'z'=8,'yh'=2,'c'=2] {'yl','z','yh'}, dimensions={0} | all-to-all | bytes 524288 | tf_op jit(solution)/shard_map/all_to_all | solution.py:16
  148.4 0.2 convolution_subtract_fusion
  148.7 14.6 %all_to_all.54 = f32[16,16,128]{2,1,0:T(8,128)S(1)} all-to-all(f32[16,16,128]{2,1,0:T(8,128)S(1)} %broadcast_in_dim.71), channel_id=1, replica_groups=mesh['yl'=4,'x'=4,'z'=8,'yh'=2,'c'=2] {'z','yh'}, dimensions={0} | all-to-all | bytes 262144 | tf_op jit(solution)/shard_map/all_to_all | solution.py:16
  163.3 0.3 fusion.21
  163.6 0.7 broadcast_in_dim.72
  164.4 5.2 %all-to-all-start.8 = ((bf16[64,16,128]{2,1,0:T(8,128)(2,1)}), bf16[64,16,128]{2,1,0:T(8,128)(2,1)S(1)}, u32[]{:S(2)}, u32[]{:S(2)}) async-start(bf16[64,16,128]{2,1,0:T(8,128)(2,1)} %broadcast_in_dim.72), calls=%async_computation.8 | async-start | bytes 524288 | tf_op jit(solution)/shard_map/all_to_all | solution.py:16
  169.6 0.0 copy-done
  169.6 0.0 all-gather.9.cloned.1.call-done
  169.6 0.0 slice-start
  169.6 5.5 %shard_map.28.sofar = f32[2,16,512]{2,1,0:T(8,128)S(1)} custom-call(bf16[16,16,128]{2,1,0:T(8,128)(2,1)S(1)} %get-tuple-element.24.refs_0_, bf16[16,16,128]{2,1,0:T(8,128)(2,1)S(1)} %get-tuple-element.22.refs_1_, bf16[16,16,128]{2,1,0:T(8,128)(2,1)S(1)} %get-tuple-element.20.refs_2_, bf16[8,64,8192]{2,1,0:T(8,128)(2,1)} %bitcast.134, ...), custom_call_target="tpu_custom_call" | custom-call | flops 201326592 | bytes 12582912 | tf_op jit(solution)/shard_map/pallas_call | solution.py:186
  175.1 0.0 slice-done
  175.1 6.9 %all-to-all-done.8.got = bf16[64,16,128]{2,1,0:T(8,128)(2,1)S(1)} async-done(((bf16[64,16,128]{2,1,0:T(8,128)(2,1)}), bf16[64,16,128]{2,1,0:T(8,128)(2,1)S(1)}, u32[]{:S(2)}, u32[]{:S(2)}) %all-to-all-start.8) | async-done | bytes 262176 | tf_op jit(solution)/shard_map/all_to_all | solution.py:16
  182.0 2.6 %shard_map.29 = f32[8,2,16,128]{3,2,1,0:T(8,128)S(1)} custom-call(s32[1]{0:T(128)} %bitcast.owner_ref, bf16[64,16,128]{2,1,0:T(8,128)(2,1)S(1)} %all-to-all-done.8.got, f32[2,16,512]{2,1,0:T(8,128)S(1)} %shard_map.28.sofar, f32[4,16,128]{2,1,0:T(8,128)S(1)} %pad_maximum_fusion.solved, bf16[8,64,8192]{2,1,0:T(8,128)(2,1)} %bitcast.135, ...), custom_call_target="tpu_custom_call" | custom-call | flops 67108864 | bytes 4194304 | tf_op jit(solution)/shard_map/pallas_call | solution.py:194
  184.7 18.3 %all_to_all.55.back = f32[8,2,16,128]{3,2,1,0:T(8,128)} all-to-all(f32[8,2,16,128]{3,2,1,0:T(8,128)S(1)} %shard_map.29), channel_id=1, replica_groups=mesh['yl'=4,'x'=4,'z'=8,'yh'=2,'c'=2] {'x','c'}, dimensions={0} | all-to-all | bytes 262144 | tf_op jit(solution)/shard_map/all_to_all | solution.py:16
  203.0 1.6 shard_map.30
  (22 shorter events, 0.4 us)
Async XLA Ops:
  6.5 71.3 %all-gather.7.cloned.1.call-start = ((), (), s32[]{:S(2)}) async-start(), calls=%async_computation.10 | async-start | bytes 9437184 | tf_op jit(solution)/shard_map/all_gather | solution.py:144
  9.6 0.8 slice-start.1
  9.6 160.0 %all-gather.9.cloned.1.call-start = ((), (), s32[]{:S(2)}) async-start(), calls=%async_computation.11 | async-start | bytes 9437184 | tf_op jit(solution)/shard_map/all_gather | solution.py:145
  19.8 25.0 %all-to-all-start = ((f32[16,64,128]{2,1,0:T(8,128)}), f32[16,64,128]{2,1,0:T(8,128)S(1)}, u32[]{:S(2)}, u32[]{:S(2)}) async-start(f32[16,64,128]{2,1,0:T(8,128)} %broadcast_in_dim.29), calls=%async_computation | async-start | bytes 1048576 | tf_op jit(solution)/shard_map/all_to_all | solution.py:16
  53.8 115.8 %copy-start = (f32[4,16,128]{2,1,0:T(8,128)}, f32[4,16,128]{2,1,0:T(8,128)S(1)}, u32[]{:S(2)}) copy-start(f32[4,16,128]{2,1,0:T(8,128)S(1)} %all_to_all.50) | copy-start | bytes 98308
  79.8 17.2 %all-to-all-start.3 = ((f32[16,16,128]{2,1,0:T(8,128)}), f32[16,16,128]{2,1,0:T(8,128)S(1)}, u32[]{:S(2)}, u32[]{:S(2)}) async-start(f32[16,16,128]{2,1,0:T(8,128)} %broadcast_in_dim.32), calls=%async_computation.3 | async-start | bytes 262144 | tf_op jit(solution)/shard_map/all_to_all | solution.py:16
  98.1 17.4 %all-to-all-start.4 = ((bf16[64,16,128]{2,1,0:T(8,128)(2,1)}), bf16[64,16,128]{2,1,0:T(8,128)(2,1)S(1)}, u32[]{:S(2)}, u32[]{:S(2)}) async-start(bf16[64,16,128]{2,1,0:T(8,128)(2,1)} %broadcast_in_dim.33), calls=%async_computation.4 | async-start | bytes 524288 | tf_op jit(solution)/shard_map/all_to_all | solution.py:16
  164.4 17.7 %all-to-all-start.8 = ((bf16[64,16,128]{2,1,0:T(8,128)(2,1)}), bf16[64,16,128]{2,1,0:T(8,128)(2,1)S(1)}, u32[]{:S(2)}, u32[]{:S(2)}) async-start(bf16[64,16,128]{2,1,0:T(8,128)(2,1)} %broadcast_in_dim.72), calls=%async_computation.8 | async-start | bytes 524288 | tf_op jit(solution)/shard_map/all_to_all | solution.py:16
  169.6 5.5 %slice-start = ((f32[4,16,128]{2,1,0:T(8,128)}), f32[1,16,128]{2,1,0:T(8,128)S(1)}, s32[]{:S(2)}) async-start(f32[4,16,128]{2,1,0:T(8,128)} %copy-done), calls=%async_computation.12 | async-start | bytes 16384 | tf_op jit(solution)/shard_map/slice | solution.py:167
Sparse Core Ops, SparseCore 0:
  9.8 61.2 all-gather.6
  73.2 55.2 all-gather.8
